TPU v7x, 32 devices: a whole 2x2x4 slice. The times are simulated.
32 devices in a mesh: dp: 16 (over z, x, core), head: 2 (over y).
Axes of the slice: x: 2, y: 2, z: 4, core: 2. Of those that a mesh axis runs over, the one named last changes fastest.
Arguments:
- tokens: bfloat16 [32768, 512], P(('dp', 'head')), may hold values from -6 to 6
- lengths: int32 [128], P('dp'), may hold values from 40 to 256, as said below
- ln1_gain: float32 [512], replicated, may hold values from 0.5 to 1.5
- ln1_bias: float32 [512], replicated, may hold values from -1 to 1
- w_query: bfloat16 [512, 512], P(None, 'head'), may hold values from -0.25 to 0.25
- w_key: bfloat16 [512, 512], P(None, 'head'), may hold values from -0.25 to 0.25
- w_value: bfloat16 [512, 512], P(None, 'head'), may hold values from -0.25 to 0.25
- w_out: bfloat16 [512, 512], P('head'), may hold values from -1 to 1
- sort_first: bfloat16 [512, 512], replicated, may hold values from -0.25 to 0.25
- sort_second: bfloat16 [512, 8], replicated, may hold values from -0.5 to 0.5
- ln2_gain: float32 [512], replicated, may hold values from 0.5 to 1.5
- ln2_bias: float32 [512], replicated, may hold values from -1 to 1
- w_up: bfloat16 [512, 2048], replicated, may hold values from -0.25 to 0.25
- w_down: bfloat16 [2048, 512], replicated, may hold values from -0.125 to 0.125
- cotangent: bfloat16 [32768, 512], P(('dp', 'head')), may hold values from -6 to 6
Outputs:
- output: bfloat16 [32768, 512], P(('dp', 'head'))
- input_grad: bfloat16 [32768, 512], P(('dp', 'head'))
- grad_ln1_gain: float32 [512], replicated
- grad_ln1_bias: float32 [512], replicated
- grad_query: float32 [512, 512], P(None, 'head')
- grad_key: float32 [512, 512], P(None, 'head')
- grad_value: float32 [512, 512], P(None, 'head')
- grad_out: float32 [512, 512], P('head')
- grad_sort_first: float32 [512, 512], replicated
- grad_sort_second: float32 [512, 8], replicated
- grad_ln2_gain: float32 [512], replicated
- grad_ln2_bias: float32 [512], replicated
- grad_up: float32 [512, 2048], replicated
- grad_down: float32 [2048, 512], replicated
Inputs may be any that keep to these rules, and one draw needn't show every extreme that they name: `lengths`: some sequence has exactly 256 valid tokens and some has exactly 40.
All inputs are finite; a program needn't handle non-finite values.
Results may differ from a plain program's by a relative error of at most 0.017.
Values may be sent and summed in bfloat16 or wider, within the bound.
No kernel may reach another device: no remote copies, remote signals or barrier semaphores. Data moves between devices by JAX's collectives and lax.ppermute only.
A program may use at most 192 MiB of HBM per device.

v0:
```python
import functools

import jax
import jax.numpy as jnp
from jax import lax
from jax.experimental import pallas as pl
from jax.experimental.pallas import tpu as pltpu
from jax.sharding import PartitionSpec as P

HD = 64
BL = 32
ITERS = 8
LMAX = 256
NB = LMAX // BL
SUMMARY_SCALE = BL**-0.5
F32 = jnp.float32
LOW = jnp.bfloat16
AXES = ("dp", "head")
VMEM_LIMIT = 56 * 1024 * 1024
TURNS = ["ffn", "last", "last", "ffn", "last", "ffn", "last", "last", "ffn", "last", "ffn", "last", "last", "ffn", "last", "ffn"]

ERF_P = 0.3875
ERF_C = (
    0.23607149955804155,
    0.07450957017858355,
    0.6926085194492264,
    -0.6975625302575207,
    0.9269567150083973,
    -0.23258376165572045,
)


def normal_parts(v):
    size = jnp.abs(v)
    bell = jnp.exp(v * v * -0.5)
    t = 1.0 / (1.0 + size * (ERF_P * 0.5**0.5))
    poly = ERF_C[5]
    for coef in ERF_C[4::-1]:
        poly = poly * t + coef
    tail = (0.5 * t) * poly * bell
    return jnp.where(v >= 0, 1.0 - tail, tail), bell * 0.3989422804014327


def dot_nn(a, b):
    return lax.dot_general(a, b, (((1,), (0,)), ((), ())), preferred_element_type=F32)


def dot_nt(a, b):
    return lax.dot_general(a, b, (((1,), (1,)), ((), ())), preferred_element_type=F32)


def dot_tn(a, b):
    return lax.dot_general(a, b, (((0,), (0,)), ((), ())), preferred_element_type=F32)


def split3(v):
    high = v.astype(LOW)
    left = v - high.astype(F32)
    mid = left.astype(LOW)
    return high, mid, (left - mid.astype(F32)).astype(LOW)


def split2(v):
    high = v.astype(LOW)
    return high, (v - high.astype(F32)).astype(LOW)


def exact_right(dot, v, w):
    a, b, c = split3(v)
    return dot(a, w) + dot(b, w) + dot(c, w)


def exact_both(dot, v, w):
    a, b, c = split3(v)
    d, e, f = split3(w)
    return dot(a, d) + (dot(a, e) + dot(b, d)) + (dot(b, e) + dot(a, f) + dot(c, d))


def row_norm(x):
    center = x - jnp.mean(x, axis=-1, keepdims=True)
    spread = jnp.mean(center * center, axis=-1, keepdims=True)
    scale = lax.rsqrt(spread + 1e-05)
    return center * scale, scale


def norm_pull(grad, unit, scale):
    return scale * (
        grad
        - jnp.mean(grad, axis=-1, keepdims=True)
        - unit * jnp.mean(grad * unit, axis=-1, keepdims=True)
    )


def iota(shape, axis):
    return lax.broadcasted_iota(jnp.int32, shape, axis)


def plan_allowed(count, spans):
    shape = (count, NB, NB)
    seq = iota(shape, 0)
    span = jnp.zeros(shape, jnp.int32)
    for s in range(count):
        span = jnp.where(seq == s, spans[s], span)
    row, col = iota(shape, 1), iota(shape, 2)
    row_ok, col_ok = row * BL < span, col * BL < span
    return (row_ok & col_ok) | ((row == col) & ~row_ok)


def head_mask(value):
    row, lane = iota((LMAX, 8 * HD), 0), iota((LMAX, 8 * HD), 1)
    return jnp.where(row // BL == lane // HD, value, 0.0).astype(LOW)


def spread_plan(plan, flip):
    pick = jnp.where(iota((LMAX, NB), 0) // BL == iota((LMAX, NB), 1), 1.0, 0.0).astype(LOW)
    same = (iota((LMAX, LMAX), 0) % BL) == (iota((LMAX, LMAX), 1) % BL)
    parts = []
    for part in split2(plan):
        tall = (dot_nt if flip else dot_nn)(pick, part).astype(LOW)
        parts.append(jnp.where(same, dot_nt(tall, pick), 0.0).astype(LOW))
    return parts


def pair_rows(left_t, right, m, lane_low):
    both = dot_nn(left_t[2 * BL * m : 2 * BL * (m + 1), :], right[:, 2 * HD * m : 2 * HD * (m + 1)])
    return jnp.where(lane_low, both[:BL], both[BL:])


PART = 256
PIECE = 64


def prepare_kernel(
    count, lens, ids, tokens, ln_gain, ln_bias, first, second, cotangent, down,
    normed, normed_t, summary, pre, steps, plan, cot_t, grad_hidden,
):
    spans = [lens[ids[2] * count + s] for s in range(count)]
    tokens.wait()
    ln_gain.wait()
    ln_bias.wait()
    gain, bias = ln_gain[...], ln_bias[...]
    token, block = iota((NB, LMAX), 1), iota((NB, LMAX), 0)

    def norm(s, carry):
        rows = pl.ds(pl.multiple_of(s * LMAX, LMAX), LMAX)
        unit, _ = row_norm(tokens[rows, :].astype(F32))
        low = (unit * gain + bias).astype(LOW)
        normed[rows, :] = low
        normed_t[:, rows] = low.T
        member = (token // BL == block) & (token < lens[ids[2] * count + s])
        picked = jnp.where(member, 1.0, 0.0).astype(LOW)
        blocks = pl.ds(pl.multiple_of(s * NB, NB), NB)
        summary[blocks, :] = dot_nn(picked, low) * SUMMARY_SCALE
        return carry

    lax.fori_loop(0, count, norm, 0)
    for out in (normed, normed_t, summary):
        out.send()
    for value in (first, second, cotangent, down):
        value.wait()
    before = exact_right(dot_nn, summary[...], first[...])
    pre[...] = before
    gate, _ = normal_parts(before)
    logits = exact_right(dot_nt, before * gate, second[...])
    logits = logits.reshape(count, NB, NB)
    x = jnp.where(plan_allowed(count, spans), logits, -1e30)
    for k in range(2 * ITERS):
        axis = 2 - k % 2
        top = jnp.max(x, axis=axis, keepdims=True)
        x = x - (top + jnp.log(jnp.sum(jnp.exp(x - top), axis=axis, keepdims=True)))
        steps[k] = x
    plan[...] = jnp.exp(x)
    for out in (pre, steps, plan):
        out.send()
    rows = cotangent[...]
    for s in range(count):
        seq = slice(s * LMAX, (s + 1) * LMAX)
        cot_t[:, seq] = cotangent[seq, :].T
    cot_t.send()

    def expand(c, carry):
        at = pl.ds(pl.multiple_of(c * PART, PART), PART)
        grad_hidden[:, at] = dot_nt(rows, down[at, :]).astype(LOW)
        return carry

    lax.fori_loop(0, down.shape[0] // PART, expand, 0)


def forward_kernel(
    count, lens, ids, w_q, w_k, w_v, w_o, near_w, far_w, normed, plan, tokens, ln_gain, ln_bias,
    up, grad_hidden, cot_t, down, cotangent,
    q_out, k_out, v_out, sk_out, sv_out, p_out, w_all, sent, kept, output, grad_middle, grad_att,
    grad_vecs,
    mask, mixed, mixed_t, middle, normed2, normed2_t, up0, up1, hid0, hid1, gup0, gup1, out_s, gn_s,
    grad_s, parts, part_sems,
):
    mask[...] = head_mask(HD**-0.5)
    for value in (w_q, w_k, w_v, w_o, near_w, far_w, normed, plan):
        value.wait()
    core, head = ids[0], ids[2]
    half, quarter = 4 * HD, 2 * HD
    own = pl.ds(pl.multiple_of(head * half, half), half)
    near = pl.ds(pl.multiple_of((1 - head) * half + core * quarter, quarter), quarter)
    far = pl.ds(pl.multiple_of((1 - head) * half + (1 - core) * quarter, quarter), quarter)
    for slot, w in enumerate((w_q, w_k, w_v)):
        w_all[slot, :, own] = w[...]
        w_all[slot, :, near] = near_w[512 * slot : 512 * (slot + 1), :]
        w_all[slot, :, far] = far_w[512 * slot : 512 * (slot + 1), :]
    w_all[3, own, :] = w_o[...]
    for m in range(4):
        lanes, rows = slice(128 * m, 128 * (m + 1)), slice(1536 + 128 * m, 1664 + 128 * m)
        w_all[3, near, lanes] = near_w[rows, :]
        w_all[3, far, lanes] = far_w[rows, :]
    w_all.send()
    keep_row = iota((LMAX, 8 * HD), 0)
    key_row = iota((2 * BL, 8 * BL), 0)
    query = iota((2 * BL, 8 * BL), 1) % BL
    lane_low = iota((BL, 2 * HD), 1) < HD

    def one(s, carry):
        span = lens[ids[2] * count + s]
        seq = pl.ds(pl.multiple_of(s * LMAX, LMAX), LMAX)
        n = normed[seq, :]
        keep = keep_row < span
        q_out[seq, :] = dot_nn(n, w_all[0]).astype(LOW)
        key = jnp.where(keep, dot_nn(n, w_all[1]), 0.0).astype(LOW)
        value = jnp.where(keep, dot_nn(n, w_all[2]), 0.0).astype(LOW)
        k_out[seq, :] = key
        v_out[seq, :] = value
        high, low = spread_plan(plan[s], False)
        sk_out[seq, :] = (dot_nn(high, key) + dot_nn(low, key)).astype(LOW)
        sv_out[seq, :] = (dot_nn(high, value) + dot_nn(low, value)).astype(LOW)
        rows = [pl.ds(pl.multiple_of(s * LMAX + i * BL, BL), BL) for i in range(NB)]
        scores = []
        for r in rows:
            keys = jnp.concatenate([k_out[r, :], sk_out[r, :]], 0)
            wide = jnp.concatenate([q_out[r, :]] * 8, 0) * mask[...]
            scores.append(dot_nt(keys, wide))
        weights = []
        for i, score in enumerate(scores):
            valid = jnp.where(key_row < BL, i * BL + key_row, i * BL) < span
            score = jnp.where(valid | (i * BL + query >= span), score, -1e30)
            grown = jnp.exp(score - jnp.max(score, axis=0, keepdims=True))
            weights.append(grown * (1.0 / jnp.sum(grown, axis=0, keepdims=True)))
        for i, weight in enumerate(weights):
            at = pl.multiple_of(s * 2 * LMAX + i * 2 * BL, 2 * BL)
            p_out[pl.ds(at, 2 * BL), :] = weight.astype(LOW)
        turned = [weight.T.astype(LOW) for weight in weights]
        for i, (r, weight_t) in enumerate(zip(rows, turned)):
            values = jnp.concatenate([v_out[r, :], sv_out[r, :]], 0)
            out = jnp.concatenate([pair_rows(weight_t, values, m, lane_low) for m in range(4)], 1)
            out = jnp.where(iota((BL, 8 * HD), 0) + i * BL < span, out, 0.0)
            mixed[i * BL : (i + 1) * BL, :] = out.astype(LOW)
        blended = mixed[...]
        mixed_t[:, seq] = blended.T

        @pl.when(s == 0)
        def _():
            tokens.wait()
            ln_gain.wait()
            ln_bias.wait()

        mid = tokens[seq, :].astype(F32) + dot_nn(blended, w_all[3])
        middle[seq, :] = mid
        unit, _ = row_norm(mid)
        low2 = (unit * ln_gain[...] + ln_bias[...]).astype(LOW)
        normed2[seq, :] = low2
        normed2_t[:, seq] = low2.T
        return carry

    lax.fori_loop(0, count, one, 0)
    for out in (q_out, k_out, v_out, sk_out, sv_out, p_out):
        out.send()
    for value in (up, grad_hidden, cot_t, down, cotangent):
        value.wait()
    units = up.shape[1] // PART // 2
    quarter = normed.shape[1] // 4
    ups, hids, gups = (up0, up1), (hid0, hid1), (gup0, gup1)

    def columns(c):
        unit = ((c // units) ^ (1 - core)) * units + c % units
        return pl.ds(pl.multiple_of(unit * PART, PART), PART)

    def expand(c, side):
        ups[side][...] = dot_nn(normed2[...], up[:, columns(c)])

    def gate_rows(c, side, rows):
        v = ups[side][rows, :]
        share, bell = normal_parts(v)
        hids[side][rows, :] = (v * share).astype(LOW)
        gh = grad_hidden[rows, columns(c)].astype(F32)
        gups[side][rows, :] = (gh * (share + v * bell)).astype(LOW)

    def gate(c, side):
        for r in range(up0.shape[0] // PIECE):
            gate_rows(c, side, slice(r * PIECE, (r + 1) * PIECE))

    def gate_alone(c, side):
        def piece(r, carry):
            gate_rows(c, side, pl.ds(pl.multiple_of(r * PIECE, PIECE), PIECE))
            return carry

        lax.fori_loop(0, up0.shape[0] // PIECE, piece, 0)

    def reduce(c, side):
        hidden, gup = hids[side][...], gups[side][...]
        for color, (left, right) in enumerate(((normed2_t, gup), (cot_t, hidden))):
            grad = dot_nn(left[...], right).astype(LOW)
            for j in range(PART // 128):
                for i in range(4):
                    tile = grad[quarter * i : quarter * (i + 1), 128 * j : 128 * (j + 1)]
                    at = slice(quarter * j, quarter * (j + 1))
                    parts[c // units, color, c % units, i, at, :] = tile
        out_s[...] += dot_nn(hidden, down[columns(c), :])
        gn_s[...] += dot_nt(gup, up[:, columns(c)])

    def part_copy(n, u):
        at = (slice(None), u, slice(None), slice(0, PART))
        return pltpu.make_async_copy(
            parts.at[n].at[at], (sent, kept)[n].at[at], part_sems.at[n * units + u]
        )

    out_s[...] = jnp.zeros_like(out_s)
    gn_s[...] = jnp.zeros_like(gn_s)
    last = 2 * units - 1
    expand(0, 0)
    expand(1, 1)
    gate_alone(0, 0)

    def steps(i, carry):
        for h in range(2):
            c = 2 * i + 1 + h
            expand(c + 1, h)
            gate(c, 1 - h)
            reduce(c - 1, h)
        return carry

    lax.fori_loop(0, units - 1, steps, 0)
    for u in range(units):
        part_copy(0, u).start()
    gate(last, 1)
    reduce(last - 1, 0)
    reduce(last, 1)

    def pull(s, carry):
        gain, bias = carry
        seq = pl.ds(pl.multiple_of(s * LMAX, LMAX), LMAX)
        gn, mid = gn_s[seq, :], middle[seq, :]
        unit, scale = row_norm(mid)
        gmid = cotangent[seq, :].astype(F32) + norm_pull(gn * ln_gain[...], unit, scale)
        grad_middle[seq, :] = gmid
        grad_att[seq, :] = gmid.astype(LOW)
        output[seq, :] = (mid + out_s[seq, :]).astype(LOW)
        gain = gain + jnp.sum(gn * unit, axis=0, keepdims=True)
        return gain, bias + jnp.sum(gn, axis=0, keepdims=True)

    zero = jnp.zeros((1, middle.shape[1]), F32)
    gain, bias = lax.fori_loop(0, count, pull, (zero, zero))
    for out in (grad_att, grad_middle, output):
        out.send()
    grad_vecs[0:1, :] = gain
    grad_vecs[1:2, :] = bias
    for u in range(units):
        part_copy(1, u).start()
    grad_s[...] = dot_nn(mixed_t[...], grad_att[...])
    tails = []
    for n, target in enumerate((sent, kept)):
        base = (core ^ (1 - n)) * units
        for j in range(units):
            for m in range(4):
                for h in range(2):
                    at = pl.multiple_of((base + j) * 64 + 32 * h, 32)
                    tile = grad_s[pl.ds(at, 32), 128 * m : 128 * (m + 1)].astype(LOW)
                    parts[n, m // 2, j, 2 * (m % 2) + h, PART : PART + 32, :] = tile
        at = (slice(None), slice(None), slice(None), slice(PART, PART + 32))
        tail = pltpu.make_async_copy(
            parts.at[n].at[at], target.at[at], part_sems.at[2 * units + n]
        )
        tail.start()
        tails.append(tail)
    for u in range(units):
        part_copy(0, u).wait()
        part_copy(1, u).wait()
    for tail in tails:
        tail.wait()


def scatter_tiles(core, sent, kept, wide, base):
    for n, target in enumerate((sent, kept)):

        def unit(k, carry, n=n, target=target):
            color, u = k // 4, k % 4
            at = (color * 8 + (core ^ (1 - n)) * 4 + u) * 32
            tile = wide[pl.ds(pl.multiple_of(at, 32), 32), :].astype(LOW)
            for p in range(4):
                for m in range(4):
                    part = tile[8 * p : 8 * (p + 1), 128 * m : 128 * (m + 1)]
                    target[color, u, p, base + 8 * m : base + 8 * (m + 1), :] = part
            return carry

        lax.fori_loop(0, 8, unit, 0)


def backward_one(
    local, plan_at, span, grad_att, w_o, q_in, k_in, v_in, sk_in, sv_in, p_in, plan,
    grad_q, grad_k, grad_v, grad_plan, mask, go_s, dks, dvs, dk_own, dv_own,
):
    base = local * LMAX
    seq = pl.ds(pl.multiple_of(base, LMAX), LMAX)
    gmixed = dot_nt(grad_att[seq, :], w_o[...]).astype(LOW)
    keep = iota((LMAX, 8 * HD), 0) < span
    go_s[...] = jnp.where(keep, gmixed, jnp.zeros_like(gmixed))
    lane_low = iota((BL, 2 * HD), 1) < HD
    rows = [pl.ds(pl.multiple_of(base + i * BL, BL), BL) for i in range(NB)]
    probs = [pl.ds(pl.multiple_of(2 * base + i * 2 * BL, 2 * BL), 2 * BL) for i in range(NB)]
    own_rows = [slice(i * BL, (i + 1) * BL) for i in range(NB)]
    grads, scores = [], []
    for r, at, mine in zip(rows, probs, own_rows):
        values = jnp.concatenate([v_in[r, :], sv_in[r, :]], 0)
        gwide = jnp.concatenate([go_s[mine, :]] * 8, 0) * mask[...]
        grads.append(dot_nt(values, gwide))
        dv = dot_nn(p_in[at, :], gwide)
        dv_own[mine, :] = dv[:BL]
        dvs[mine, :] = dv[BL:]
    for at, gweights in zip(probs, grads):
        wide = p_in[at, :].astype(F32)
        total = jnp.sum(wide * gweights, axis=0, keepdims=True)
        scores.append(wide * (gweights - total))
    turned = [gscores.T.astype(LOW) for gscores in scores]
    for r, mine, gscores in zip(rows, own_rows, scores):
        qwide = jnp.concatenate([q_in[r, :]] * 8, 0) * mask[...]
        dk = dot_nn(gscores.astype(LOW), qwide) * HD**-0.5
        dk_own[mine, :] = dk[:BL]
        dks[mine, :] = dk[BL:]
    for r, gscores_t in zip(rows, turned):
        keys = jnp.concatenate([k_in[r, :], sk_in[r, :]], 0)
        dq = jnp.concatenate([pair_rows(gscores_t, keys, m, lane_low) for m in range(4)], 1)
        grad_q[r, :] = (dq * HD**-0.5).astype(LOW)
    same = (iota((LMAX, LMAX), 0) % BL) == (iota((LMAX, LMAX), 1) % BL)
    high, low = spread_plan(plan[plan_at], True)
    cross = jnp.zeros((LMAX, LMAX), F32)
    for own, sorted_part, kept, target in (
        (dk_own, dks, k_in, grad_k),
        (dv_own, dvs, v_in, grad_v),
    ):
        g_high, g_low = split2(sorted_part[...])
        kept_rows = kept[seq, :]
        cross += dot_nt(g_high, kept_rows) + dot_nt(g_low, kept_rows)
        total = own[...] + (dot_nn(high, g_high) + (dot_nn(high, g_low) + dot_nn(low, g_high)))
        target[seq, :] = jnp.where(keep, total, 0.0).astype(LOW)
    cross = jnp.where(same, cross, 0.0)
    rows8 = jnp.sum(cross.reshape(NB, BL, LMAX), axis=1)
    pick = jnp.where(iota((LMAX, NB), 0) // BL == iota((LMAX, NB), 1), 1.0, 0.0).astype(LOW)
    grad_plan[local] = exact_right(dot_nn, rows8, pick)


def backward_kernel(
    first, count, lens, ids, grad_att, w_all, q_in, k_in, v_in, sk_in, sv_in, p_in, plan,
    grad_q, grad_k, grad_v, grad_plan, mask, *own,
):
    mask[...] = head_mask(1.0)
    ins = (grad_att, w_all, q_in, k_in, v_in, sk_in, sv_in, p_in, plan)
    for value in ins:
        value.wait()
    ins = (grad_att, w_all.buffer.at[0], *ins[2:])

    def one(n, carry):
        span = lens[ids[2] * count + first + n]
        backward_one(
            n, first + n, span, *ins, grad_q, grad_k, grad_v, grad_plan, mask, *own
        )
        return carry

    lax.fori_loop(0, grad_q.shape[0] // LMAX, one, 0)


def last_kernel(cuts, count, lens, ids, grad_att, w_all, q_in, k_in, v_in, sk_in, sv_in, p_in, plan, *refs):
    first, groups = cuts[-2], len(cuts) - 2
    early, refs = refs[: 4 * groups], refs[4 * groups :]
    normed_t, steps, pre, summary, sort_one, sort_two, ln_gain, vecs2, tokens, grad_middle = refs[:10]
    sent, kept, input_grad, mask, go_s, dks, dvs, dk_own, dv_own = refs[10:19]
    grad_q, grad_k, grad_v, grad_plan, gsum, small, grad_s = refs[19:]
    mask[...] = head_mask(1.0)
    ins = (grad_att, w_all, q_in, k_in, v_in, sk_in, sv_in, p_in, plan)
    for value in ins:
        value.wait()
    ins = (grad_att, w_all.buffer.at[3], *ins[2:])
    own = (mask, go_s, dks, dvs, dk_own, dv_own)

    def one(n, carry):
        span = lens[ids[2] * count + first + n]
        backward_one(n, first + n, span, *ins, grad_q, grad_k, grad_v, grad_plan, *own)
        return carry

    lax.fori_loop(0, count - first, one, 0)
    for value in (*early, normed_t, steps):
        value.wait()
    kinds = [list(early[n::4]) + [late] for n, late in enumerate((grad_q, grad_k, grad_v, grad_plan))]
    spans = [lens[ids[2] * count + c] for c in range(count)]
    g = jnp.concatenate([r[...] for r in kinds[3]], 0) * plan[...]
    for k in range(2 * ITERS - 1, -1, -1):
        axis = 2 - k % 2
        g = g - jnp.exp(steps[k]) * jnp.sum(g, axis=axis, keepdims=True)
    g = jnp.where(plan_allowed(count, spans), g, 0.0).reshape(count * NB, NB)
    d = normed_t.shape[0]
    for slot in range(3):
        grad = jnp.zeros((d, d), F32)
        for n, rows in enumerate(kinds[slot]):
            grad += dot_nn(normed_t[:, cuts[n] * LMAX : cuts[n + 1] * LMAX], rows[...])
        grad_s[...] = grad
        scatter_tiles(ids[0], sent, kept, grad_s, 32 * slot)
    for value in (pre, summary, sort_one, sort_two, ln_gain, vecs2, tokens, grad_middle):
        value.wait()
    before = pre[...]
    share, bell = normal_parts(before)
    small[...] = jnp.zeros_like(small)
    small[0:NB, :] = exact_both(dot_tn, g, before * share)
    small[10:12, :] = vecs2[...]
    gpre = exact_right(dot_nn, g, sort_two[...]) * (share + before * bell)
    grad_s[...] = exact_both(dot_tn, summary[...], gpre)
    scatter_tiles(ids[0], sent, kept, grad_s, 96)
    gsum[...] = exact_right(dot_nt, gpre, sort_one[...]) * SUMMARY_SCALE
    gain, bias = jnp.zeros((1, d), F32), jnp.zeros((1, d), F32)
    token, block = iota((LMAX, NB), 0), iota((LMAX, NB), 1)
    for s in range(count):
        seq = slice(s * LMAX, (s + 1) * LMAX)
        unit, scale = row_norm(tokens[seq, :].astype(F32))
        member = (token // BL == block) & (token < spans[s])
        picked = jnp.where(member, 1.0, 0.0).astype(LOW)
        high, mid, low = split3(gsum[s * NB : (s + 1) * NB, :])
        gn = dot_nn(picked, high) + dot_nn(picked, mid) + dot_nn(picked, low)
        for slot in range(3):
            group = max(n for n in range(groups + 1) if cuts[n] <= s)
            at = (s - cuts[group]) * LMAX
            gn += dot_nt(kinds[slot][group][at : at + LMAX, :], w_all[slot])
        gain += jnp.sum(gn * unit, axis=0, keepdims=True)
        bias += jnp.sum(gn, axis=0, keepdims=True)
        pulled = norm_pull(gn * ln_gain[...], unit, scale)
        input_grad[seq, :] = (grad_middle[seq, :] + pulled).astype(LOW)
    small[8:9, :] = gain
    small[9:10, :] = bias
    zeros = jnp.zeros((8, 128), LOW)
    for n, target in enumerate((sent, kept)):
        at = pl.ds(pl.multiple_of((ids[0] ^ (1 - n)) * 8, 8), 8)
        for u in range(4):
            tile = small[at, 128 * u : 128 * (u + 1)].astype(LOW)
            for color in range(2):
                for i in range(4):
                    target[color, u, i, 128:136, :] = tile if color == 0 and i == 0 else zeros


def each_piece(ids, near, far, place, looped):
    core, x, head = ids[0], ids[1], ids[2]
    for color in range(2):
        one, two = ((head, x), (x, head))[color]
        for n, source in enumerate((near, far)):

            def pieces(r, carry, color=color, one=one, two=two, n=n, source=source):
                unit = (core ^ n) * 4 + (one ^ (r // 2)) * 2 + (two ^ (r % 2))
                for i in range(4):
                    part = (ids[3] ^ (i // 2)) * 2 + (ids[4] ^ (i % 2))
                    place(color, unit, part, source.buffer.at[color, r, i // 2, i % 2])
                return carry

            if looped:
                lax.fori_loop(0, 4, pieces, 0)
            else:
                for r in range(4):
                    pieces(r, 0)


def place_ffn_kernel(ids, near, far, grad_up, grad_down, grad_o, o_s):
    near.wait()
    far.wait()

    def place(color, unit, part, source):
        quarter = pl.ds(pl.multiple_of(part * 128, 128), 128)
        for j in range(2):
            at = pl.ds(pl.multiple_of(unit * PART + 128 * j, 128), 128)
            block = source[128 * j : 128 * (j + 1), :].astype(F32)
            if color == 0:
                grad_up[quarter, at] = block
            else:
                grad_down[at, quarter] = block.T
        rows = pl.ds(pl.multiple_of(unit * 64 + (part % 2) * 32, 32), 32)
        lanes = pl.ds(pl.multiple_of(256 * color + (part // 2) * 128, 128), 128)
        o_s[rows, lanes] = source[PART : PART + 32, :].astype(F32)

    each_piece(ids, near, far, place, True)
    grad_o[...] = o_s[pl.ds(pl.multiple_of(ids[2] * 256, 256), 256), :]


def place_last_kernel(
    ids, near, far, grad_q, grad_k, grad_v, grad_first, second, gain1, bias1, gain2, bias2, wide, small
):
    near.wait()
    far.wait()
    head = ids[2]

    def place(color, unit, part, source):
        rows = pl.ds(pl.multiple_of(color * 256 + unit * 32 + part * 8, 8), 8)
        wide[...] = source[...].astype(F32)
        for slot, out in enumerate((grad_q, grad_k, grad_v)):
            for t in range(2):
                at = pl.ds(pl.multiple_of((4 * slot + 2 * head + t) * 8, 8), 8)
                out[rows, 128 * t : 128 * (t + 1)] = wide[at, :]
        for m in range(4):
            grad_first[rows, 128 * m : 128 * (m + 1)] = wide[96 + 8 * m : 104 + 8 * m, :]
        if color == 0:
            high = pl.ds(pl.multiple_of((unit // 4) * 8, 8), 8)
            lanes = pl.ds(pl.multiple_of((unit % 4) * 128, 128), 128)
            small[part, high, lanes] = wide[128:136, :]

    each_piece(ids, near, far, place, False)
    second[...] = small[0, 0:NB, :]
    for n, out in enumerate((gain1, bias1, gain2, bias2)):
        out[...] = small[0, 8 + n : 9 + n, :]


def slice_kernel(ids, w_q, w_k, w_v, w_o, mine):
    core = ids[0]
    lanes = pl.ds(pl.multiple_of(core * 2 * HD, 2 * HD), 2 * HD)
    for slot, w in enumerate((w_q, w_k, w_v)):
        w.wait()
        mine[512 * slot : 512 * (slot + 1), :] = w[:, lanes]
    w_o.wait()
    for m in range(4):
        mine[1536 + 128 * m : 1664 + 128 * m, :] = w_o[lanes, 128 * m : 128 * (m + 1)]


def swap(values, bit, dp_size):
    if bit == "head":
        pairs = [(d * 2 + h, d * 2 + (1 - h)) for d in range(dp_size) for h in range(2)]
    else:
        pairs = [(d * 2 + h, (d ^ bit) * 2 + h) for d in range(dp_size) for h in range(2)]
    return lax.ppermute(values, AXES, pairs)


def side_of(bit):
    if bit == "head":
        return lax.axis_index("head")
    return (lax.axis_index("dp") // bit) % 2


def pick(values, index, axis=0):
    return lax.dynamic_index_in_dim(values, index, axis, keepdims=False)


def pick_all(arrays, index):
    return [pick(a, index) for a in arrays]


def low_sum(arrays):
    total = arrays[0].astype(F32)
    for a in arrays[1:]:
        total = total + a.astype(F32)
    return total.astype(LOW)


def line_bits(dp_size):
    bits, bit = [], 4
    while bit < dp_size:
        bits.append(bit)
        bit *= 2
    return bits


def sum_chain(sent, kept, dp_size):
    order = (("head", 2), (2, "head"))
    line = line_bits(dp_size)
    got = swap(sent, 1, dp_size)
    got, = yield [sent], [got]
    shape = (2, 2, 2, 2) + kept.shape[3:]
    sums = [[kept[c].reshape(shape), got[c].reshape(shape)] for c in range(2)]
    for turn in range(2):
        sides = [side_of(order[c][turn]) for c in range(2)]
        sents = [low_sum(pick_all(sums[c], 1 - sides[c])) for c in range(2)]
        gots = [swap(sents[c], order[c][turn], dp_size) for c in range(2)]
        gots = yield sents, gots
        sums = [pick_all(sums[c], sides[c]) + [gots[c]] for c in range(2)]
    for bit in line[:2]:
        side = side_of(bit)
        sent = jnp.stack([low_sum(pick_all(sums[c], 1 - side)) for c in range(2)])
        got = swap(sent, bit, dp_size)
        got, = yield [sent], [got]
        sums = [pick_all(sums[c], side) + [got[c]] for c in range(2)]
    near = jnp.stack([low_sum(sums[c]) for c in range(2)])
    for bit in line[2:]:
        got = swap(near, bit, dp_size)
        got, = yield [near], [got]
        near = (near.astype(F32) + got.astype(F32)).astype(LOW)
    near = near[:, None]
    got = swap(near, line[1], dp_size)
    got, = yield [near], [got]
    near = jnp.concatenate([near, got], 1)[:, None]
    got = swap(near, line[0], dp_size)
    got, = yield [near], [got]
    near = jnp.concatenate([near, got], 1)
    near = [near[c][None] for c in range(2)]
    for turn in (1, 0):
        gots = [swap(near[c], order[c][turn], dp_size) for c in range(2)]
        gots = yield near, gots
        near = [jnp.concatenate([near[c], gots[c]], 0) for c in range(2)]
    near = jnp.stack(near)
    far = swap(near, 1, dp_size)
    far, = yield [near], [far]
    return near, far


class Slots:
    def __init__(self):
        self.running, self.done, self.got = {}, {}, {}

    def start(self, name, chain):
        self.running[name], self.got[name] = chain, None

    def step(self):
        sent = []
        for name, chain in list(self.running.items()):
            try:
                new, self.got[name] = chain.send(self.got[name])
                sent += new
            except StopIteration as end:
                self.done[name] = end.value
                del self.running[name], self.got[name]
        return sent

    def before(self, value):
        return lax.optimization_barrier((value, *self.step()))[0]

    def after(self, value):
        names = list(self.running)
        sizes = [len(self.got[n]) for n in names]
        flat = [g for n in names for g in self.got[n]]
        flat = lax.optimization_barrier((value, *flat))[1:]
        for name, size in zip(names, sizes):
            self.got[name], flat = list(flat[:size]), flat[size:]

    def turn(self, name, last):
        if name not in self.running:
            return last
        got = self.got[name]
        if got is not None:
            self.got[name] = list(lax.optimization_barrier((*got, *last))[: len(got)])
        try:
            sent, self.got[name] = self.running[name].send(self.got[name])
            return sent
        except StopIteration as end:
            self.done[name] = end.value
            del self.running[name]
            return last


def shaped(shape, kind):
    return jax.ShapeDtypeStruct(shape, kind)


class Staged:
    def __init__(self, buffer, copy):
        self.buffer, self.copy, self.sent = buffer, copy, False

    def wait(self):
        self.copy.wait()

    def send(self):
        if not self.sent:
            self.copy.start()
            self.sent = True

    shape = property(lambda self: self.buffer.shape)
    dtype = property(lambda self: self.buffer.dtype)

    def __getitem__(self, at):
        return self.buffer[at]

    def __setitem__(self, at, value):
        self.buffer[at] = value


def call(body, scalars, args, outs, scratch, flops, by_parts=(), limit=VMEM_LIMIT):
    args = [a if isinstance(a, tuple) else (a, None) for a in args]
    views = [jax.eval_shape(lambda v, i=i: v if i is None else v[i], a) for a, i in args]
    n_scalars, n_in, n_out = len(scalars), len(args), len(outs)

    def kernel(*refs):
        head, refs = refs[:n_scalars], refs[n_scalars:]
        sources, refs = refs[:n_in], refs[n_in:]
        targets, refs = refs[:n_out], refs[n_out:]
        taken, refs = refs[:n_in], refs[n_in:]
        made, refs = refs[: n_out - len(by_parts)], refs[n_out - len(by_parts) :]
        sems, own = refs[-1], refs[:-1]
        ins, results = [], []
        for n, (source, (_, index)) in enumerate(zip(sources, args)):
            source = source if index is None else source.at[index]
            copy = pltpu.make_async_copy(source, taken[n], sems.at[n])
            copy.start()
            ins.append(Staged(taken[n], copy))
        made = list(made)
        for n, target in enumerate(targets):
            if n in by_parts:
                results.append(target)
            else:
                buffer = made.pop(0)
                copy = pltpu.make_async_copy(buffer, target, sems.at[n_in + n])
                results.append(Staged(buffer, copy))
        body(*head, *ins, *results, *own)
        results = [r for n, r in enumerate(results) if n not in by_parts]
        for result in results:
            result.send()
        for result in results:
            result.wait()

    space = pltpu.HBM if limit == VMEM_LIMIT else pl.ANY
    smem, hbm = pl.BlockSpec(memory_space=pltpu.SMEM), pl.BlockSpec(memory_space=pltpu.HBM)
    whole = [v for n, v in enumerate(outs) if n not in by_parts]
    buffers = [pltpu.VMEM(v.shape, v.dtype) for v in (*views, *whole)]
    return pl.pallas_call(
        kernel,
        in_specs=[smem] * n_scalars + [pl.BlockSpec(memory_space=space)] * n_in,
        out_specs=[hbm] * n_out,
        out_shape=outs,
        scratch_shapes=buffers + scratch + [pltpu.SemaphoreType.DMA((n_in + n_out,))],
        compiler_params=pltpu.CompilerParams(vmem_limit_bytes=limit),
        cost_estimate=pl.CostEstimate(flops=1 << 34, bytes_accessed=1 << 24, transcendentals=0),
    )(*scalars, *[a for a, _ in args])


def on_device(
    dp_size,
    tokens,
    lengths,
    ln1_gain,
    ln1_bias,
    w_query,
    w_key,
    w_value,
    w_out,
    sort_first,
    sort_second,
    ln2_gain,
    ln2_bias,
    w_up,
    w_down,
    cotangent,
):
    rows_all, d = tokens.shape
    count = rows_all // LMAX
    ff = w_up.shape[1]
    core = side_of(1)
    ids = jnp.stack([core, side_of(2), side_of("head"), side_of(4), side_of(8)]).astype(jnp.int32)

    gain1, bias1, gain2, bias2 = (v.reshape(1, d) for v in (ln1_gain, ln1_bias, ln2_gain, ln2_bias))
    second_t = sort_second.T
    mine = call(
        slice_kernel, (ids,), (w_query, w_key, w_value, w_out), [shaped((4 * d, 2 * HD), LOW)], [],
        1 << 20,
    )[0]
    near_w = swap(mine, "head", dp_size)

    low_rows, wide_rows = shaped((rows_all, d), LOW), shaped((rows_all, d), F32)
    low_cols = shaped((d, rows_all), LOW)
    small_plan = shaped((count, NB, NB), F32)
    blocks = shaped((count * NB, d), F32)

    normed, normed_t, summary, pre, steps, plan, cot_t, grad_hidden = call(
        functools.partial(prepare_kernel, count), (lengths, ids),
        (tokens, gain1, bias1, sort_first, second_t, cotangent, w_down),
        [low_rows, low_cols, blocks, blocks, shaped((2 * ITERS, count, NB, NB), F32), small_plan]
        + [low_cols, shaped((rows_all, ff), LOW)],
        [], 2 * rows_all * d * ff,
    )
    near_w, normed = lax.optimization_barrier((near_w, normed))
    far_w = swap(near_w, 1, dp_size)

    (
        q, k, v, sk, sv, p, w_all, sent, kept, output, grad_middle, grad_att, vecs2
    ) = call(
        functools.partial(forward_kernel, count), (lengths, ids),
        (w_query, w_key, w_value, w_out, near_w, far_w, normed, plan, tokens, gain2, bias2)
        + (w_up, grad_hidden, cot_t, w_down, cotangent),
        [low_rows] * 5 + [shaped((count * 2 * LMAX, LMAX), LOW), shaped((4, d, d), LOW)]
        + [shaped((2, 4, 4, PART + 32, 128), LOW)] * 2 + [low_rows, wide_rows, low_rows, shaped((2, d), F32)],
        [pltpu.VMEM((LMAX, d), LOW)] * 2
        + [pltpu.VMEM((d, rows_all), LOW), pltpu.VMEM((rows_all, d), F32)]
        + [pltpu.VMEM((rows_all, d), LOW), pltpu.VMEM((d, rows_all), LOW)]
        + [pltpu.VMEM((rows_all, PART), F32)] * 2 + [pltpu.VMEM((rows_all, PART), LOW)] * 4
        + [pltpu.VMEM((rows_all, d), F32)] * 2 + [pltpu.VMEM((d, d), F32)]
        + [pltpu.VMEM((2, 2, 4, 4, PART + 32, 128), LOW)]
        + [pltpu.SemaphoreType.DMA((ff // PART + 2,))],
        24 * rows_all * d * d, by_parts=(7, 8),
    )
    slots = Slots()
    slots.start("ffn", sum_chain(sent, kept, dp_size))
    work = [pltpu.VMEM((LMAX, d), LOW)] * 2 + [pltpu.VMEM((LMAX, d), F32)] * 4
    cuts = (0, 1, 3, count)

    def inputs_of(first, end, w):
        rows, probs = slice(first * LMAX, end * LMAX), slice(first * 2 * LMAX, end * 2 * LMAX)
        args = ((slots.before(grad_att), rows), w) + tuple((a, rows) for a in (q, k, v, sk, sv))
        return args + ((p, probs), plan)

    grads = []
    for first, end in zip(cuts[:-2], cuts[1:-1]):
        out = call(
            functools.partial(backward_kernel, first, count), (lengths, ids),
            inputs_of(first, end, (w_all, slice(3, 4))),
            [shaped(((end - first) * LMAX, d), LOW)] * 3 + [shaped((end - first, NB, NB), F32)],
            work, 4 << 30,
        )
        slots.after(out[-1])
        grads.append(out)
    first, late = cuts[-2], count - cuts[-2]
    sent, kept, input_grad = call(
        functools.partial(last_kernel, cuts, count), (lengths, ids),
        inputs_of(first, count, w_all)
        + (*(g for out in grads for g in out), normed_t, steps, pre, summary, sort_first, second_t)
        + (gain1, vecs2, tokens, grad_middle),
        [shaped((2, 4, 4, 136, 128), LOW)] * 2 + [low_rows],
        work + [pltpu.VMEM((late * LMAX, d), LOW)] * 3 + [pltpu.VMEM((late, NB, NB), F32)]
        + [pltpu.VMEM((count * NB, d), F32), pltpu.VMEM((16, d), F32), pltpu.VMEM((d, d), F32)],
        16 << 30,
    )
    slots.after(sent)
    slots.start("last", sum_chain(sent, kept, dp_size))
    last = [input_grad]
    for name in TURNS:
        last = slots.turn(name, last)
    while "ffn" in slots.running:
        last = slots.turn("ffn", last)
    up_sum, down_sum, o_sum = call(
        place_ffn_kernel, (ids,), slots.done["ffn"],
        [shaped(s, F32) for s in ((d, ff), (ff, d), w_out.shape)],
        [pltpu.VMEM((d, d), F32)], 1 << 28, limit=20 << 20,
    )
    last = [o_sum]
    while "last" in slots.running:
        last = slots.turn("last", last)
    q_sum, k_sum, v_sum, first_sum, second_sum, *vec_sums = call(
        place_last_kernel, (ids,), slots.done["last"],
        [shaped(w_query.shape, F32)] * 3 + [shaped((d, d), F32), shaped((NB, d), F32)]
        + [shaped((1, d), F32)] * 4,
        [pltpu.VMEM((136, 128), F32), pltpu.VMEM((4, 16, d), F32)], 1 << 26, limit=8 << 20,
    )
    vec_sums = [v.reshape(d) for v in vec_sums]
    return (
        output,
        input_grad,
        vec_sums[0],
        vec_sums[1],
        q_sum,
        k_sum,
        v_sum,
        o_sum,
        first_sum,
        second_sum.T,
        vec_sums[2],
        vec_sums[3],
        up_sum,
        down_sum,
    )


def solution(mesh):
    tokens, copied, columns = P(AXES, None), P(), P(None, "head")
    return jax.shard_map(
        functools.partial(on_device, mesh.shape["dp"]),
        mesh=mesh,
        in_specs=(tokens, P("dp"), copied, copied, columns, columns, columns, P("head", None))
        + (copied,) * 6
        + (tokens,),
        out_specs=(tokens, tokens, copied, copied, columns, columns, columns, P("head", None))
        + (copied,) * 6,
        check_vma=False,
    )
```

profile of v0, /device:TPU:0, one launch (start us, length us, event | category | flops | bytes accessed | tf_op | source)
XLA Modules:
  0.0 198.3 jit_solution(10122925622363807768)
XLA Ops:
  1.3 2.7 %shard_map.254 = bf16[2048,128]{1,0:T(8,128)(2,1)} custom-call(s32[5]{0:T(128)} %stack.71.refs_0_.refs_1_, bf16[512,256]{1,0:T(8,128)(2,1)} %refs_2_.5, bf16[512,256]{1,0:T(8,128)(2,1)} %refs_3_.3, bf16[512,256]{1,0:T(8,128)(2,1)} %refs_4_.3, bf16[256,512]{1,0:T(8,128)(2,1)} %refs_5_.3), custom_call_target="tpu_custom_call" | custom-call | flops 17179869184 | bytes 16777216 | tf_op jit(solution)/shard_map/pallas_call | solution.py:817
  4.0 3.0 %collective-permute-start = (bf16[2048,128]{1,0:T(8,128)(2,1)}, bf16[2048,128]{1,0:T(8,128)(2,1)S(1)}, u32[]{:S(2)}, u32[]{:S(2)}) collective-permute-start(bf16[2048,128]{1,0:T(8,128)(2,1)} %shard_map.254), channel_id=1, source_target_pairs={{0,1},{1,0},{2,3},{3,2},{4,5},{5,4},{6,7},{7,6},{8,9},{9,8},{10,11... | collective-permute-start | bytes 1572872 | tf_op jit(solution)/shard_map/ppermute | solution.py:636
  7.1 11.6 %shard_map.255 = (bf16[1024,512]{1,0:T(8,128)(2,1)}, bf16[512,1024]{1,0:T(8,128)(2,1)}, f32[32,512]{1,0:T(8,128)}, f32[32,512]{1,0:T(8,128)}, f32[16,4,8,8]{3,2,...) custom-call(s32[8]{0:T(128)} %refs_0_.9, s32[5]{0:T(128)} %stack.71.refs_0_.refs_1_, ...), custom_call_target="tpu_custom_call" | custom-call | flops 17179869184 | bytes 16777216 | tf_op jit(solution)/shard_map/pallas_call | solution.py:817
  19.2 1.9 collective-permute-done.1.refs_7_
  21.9 37.0 %shard_map.256 = (bf16[1024,512]{1,0:T(8,128)(2,1)}, bf16[1024,512]{1,0:T(8,128)(2,1)}, bf16[1024,512]{1,0:T(8,128)(2,1)}, bf16[1024,512]{1,0:T(8,128)(2,1)}, bf...) custom-call(s32[8]{0:T(128)} %refs_0_.9, ...), custom_call_target="tpu_custom_call" | custom-call | flops 17179869184 | bytes 16777216 | tf_op jit(solution)/shard_map/pallas_call | solution.py:817
  59.1 1.8 fusion.30
  60.9 6.1 %shard_map.257 = (bf16[256,512]{1,0:T(8,128)(2,1)}, bf16[256,512]{1,0:T(8,128)(2,1)}, bf16[256,512]{1,0:T(8,128)(2,1)}, f32[1,8,8]{2,1,0:T(8,128)}) custom-call(s32[8]{0:T(128)} %refs_0_.9, s32[5]{0:T(128)} %stack.71.refs_0_.refs_1_, bf16[1024,512]{1,0:T(8,128)(2,1)} %get-tuple-element.117.refs_2_, bf16[4,512,512]{2,1,0:T(8,128)(2,1)} %get-tuple-element.104.refs_3_, ...), custom_call_target="tpu_custom_call" | custom-call | flops 17179869184 | bytes 16777216 | tf_op jit(solution)/shard_map/pallas_call | solution.py:817
  67.0 1.8 fusion.31
  69.0 1.8 collective-permute-start.3
  71.0 1.6 collective-permute-start.4
  72.6 9.8 %shard_map.258 = (bf16[512,512]{1,0:T(8,128)(2,1)}, bf16[512,512]{1,0:T(8,128)(2,1)}, bf16[512,512]{1,0:T(8,128)(2,1)}, f32[2,8,8]{2,1,0:T(8,128)}) custom-call(s32[8]{0:T(128)} %refs_0_.9, s32[5]{0:T(128)} %stack.71.refs_0_.refs_1_, bf16[1024,512]{1,0:T(8,128)(2,1)} %get-tuple-element.117.refs_2_, bf16[4,512,512]{2,1,0:T(8,128)(2,1)} %get-tuple-element.104.refs_3_, ...), custom_call_target="tpu_custom_call" | custom-call | flops 17179869184 | bytes 16777216 | tf_op jit(solution)/shard_map/pallas_call | solution.py:817
  82.4 2.4 %collective-permute-done.3 = bf16[2,2,2,288,128]{4,3,2,1,0:T(8,128)(2,1)S(1)} collective-permute-done((bf16[2,2,2,288,128]{4,3,2,1,0:T(8,128)(2,1)S(1)}, bf16[2,2,2,288,128]{4,3,2,1,0:T(8,128)(2,1)S(1)}, u32[]{:S(2)}, u32[]{:S(2)}) %collective-permute-start.3) | collective-permute-done | bytes 589856 | tf_op jit(solution)/shard_map/ppermute | solution.py:636
  84.7 1.7 collective-permute-done.4
  88.1 17.2 %shard_map.259 = (bf16[2,4,4,136,128]{4,3,2,1,0:T(8,128)(2,1)}, bf16[2,4,4,136,128]{4,3,2,1,0:T(8,128)(2,1)}, bf16[1024,512]{1,0:T(8,128)(2,1)}) custom-call(s32[8]{0:T(128)} %refs_0_.9, s32[5]{0:T(128)} %stack.71.refs_0_.refs_1_, bf16[1024,512]{1,0:T(8,128)(2,1)} %get-tuple-element.117.refs_2_, bf16[4,512,512]{2,1,0:T(8,128)(2,1)} %get-tuple-element.104.refs_3_, ...), custom_call_target="tpu_custom_call" | custom-call | flops 17179869184 | bytes 16777216 | tf_op jit(solution)/shard_map/pallas_call | solution.py:817
  108.9 6.3 %collective-permute-done.8 = bf16[2,2,288,128]{3,2,1,0:T(8,128)(2,1)} collective-permute-done((bf16[2,2,288,128]{3,2,1,0:T(8,128)(2,1)}, bf16[2,2,288,128]{3,2,1,0:T(8,128)(2,1)}, u32[]{:S(2)}, u32[]{:S(2)}) %collective-permute-start.8) | collective-permute-done | bytes 294944 | tf_op jit(solution)/shard_map/ppermute | solution.py:636
  117.6 1.6 collective-permute-start.10
  121.9 4.0 %collective-permute-done.10 = bf16[2,2,288,128]{3,2,1,0:T(8,128)(2,1)S(1)} collective-permute-done((bf16[2,2,288,128]{3,2,1,0:T(8,128)(2,1)S(1)}, bf16[2,2,288,128]{3,2,1,0:T(8,128)(2,1)S(1)}, u32[]{:S(2)}, u32[]{:S(2)}) %collective-permute-start.10) | collective-permute-done | bytes 294944 | tf_op jit(solution)/shard_map/ppermute | solution.py:636
  127.9 2.7 %collective-permute-start.13 = (bf16[2,288,128]{2,1,0:T(8,128)(2,1)S(1)}, bf16[2,288,128]{2,1,0:T(8,128)(2,1)S(1)}, u32[]{:S(2)}, u32[]{:S(2)}) collective-permute-start(bf16[2,288,128]{2,1,0:T(8,128)(2,1)S(1)} %pad_maximum_fusion.8), channel_id=1, source_target_pairs={{0,16},{1,17},{2,18},{3,19},{4,20},{5,21},{6,22},{7,23},{8,24},{9,... | collective-permute-start | bytes 442376 | tf_op jit(solution)/shard_map/ppermute | solution.py:636
  132.0 4.2 %collective-permute-done.13 = bf16[2,288,128]{2,1,0:T(8,128)(2,1)S(1)} collective-permute-done((bf16[2,288,128]{2,1,0:T(8,128)(2,1)S(1)}, bf16[2,288,128]{2,1,0:T(8,128)(2,1)S(1)}, u32[]{:S(2)}, u32[]{:S(2)}) %collective-permute-start.13) | collective-permute-done | bytes 147488 | tf_op jit(solution)/shard_map/ppermute | solution.py:636
  138.3 3.3 %collective-permute-start.16 = (bf16[2,1,288,128]{3,2,1,0:T(8,128)(2,1)S(1)}, bf16[2,1,288,128]{3,2,1,0:T(8,128)(2,1)S(1)}, u32[]{:S(2)}, u32[]{:S(2)}) collective-permute-start(bf16[2,1,288,128]{3,2,1,0:T(8,128)(2,1)S(1)} %maximum_bitcast_fusion.5), channel_id=1, source_target_pairs={{0,16},{1,17},{2,18},{3,19},{4,20},{5,21},{6,22},{7,23},{8,24},{9,... | collective-permute-start | bytes 442376 | tf_op jit(solution)/shard_map/ppermute | solution.py:636
  141.6 3.3 %collective-permute-done.14 = bf16[2,2,136,128]{3,2,1,0:T(8,128)(2,1)S(1)} collective-permute-done((bf16[2,2,136,128]{3,2,1,0:T(8,128)(2,1)S(1)}, bf16[2,2,136,128]{3,2,1,0:T(8,128)(2,1)S(1)}, u32[]{:S(2)}, u32[]{:S(2)}) %collective-permute-start.14) | collective-permute-done | bytes 139296 | tf_op jit(solution)/shard_map/ppermute | solution.py:636
  146.2 2.8 %collective-permute-done.16 = bf16[2,1,288,128]{3,2,1,0:T(8,128)(2,1)S(1)} collective-permute-done((bf16[2,1,288,128]{3,2,1,0:T(8,128)(2,1)S(1)}, bf16[2,1,288,128]{3,2,1,0:T(8,128)(2,1)S(1)}, u32[]{:S(2)}, u32[]{:S(2)}) %collective-permute-start.16) | collective-permute-done | bytes 147488 | tf_op jit(solution)/shard_map/ppermute | solution.py:636
  149.2 1.7 collective-permute-done.15
  152.4 5.6 %collective-permute-done.18 = bf16[2,1,2,288,128]{4,3,2,1,0:T(8,128)(2,1)S(1)} collective-permute-done((bf16[2,1,2,288,128]{4,3,2,1,0:T(8,128)(2,1)S(1)}, bf16[2,1,2,288,128]{4,3,2,1,0:T(8,128)(2,1)S(1)}, u32[]{:S(2)}, u32[]{:S(2)}) %collective-permute-start.18) | collective-permute-done | bytes 294944 | tf_op jit(solution)/shard_map/ppermute | solution.py:636
  159.2 5.0 %collective-permute-done.19 = bf16[2,1,2,136,128]{4,3,2,1,0:T(8,128)(2,1)S(1)} collective-permute-done((bf16[2,1,2,136,128]{4,3,2,1,0:T(8,128)(2,1)S(1)}, bf16[2,1,2,136,128]{4,3,2,1,0:T(8,128)(2,1)S(1)}, u32[]{:S(2)}, u32[]{:S(2)}) %collective-permute-start.19) | collective-permute-done | bytes 139296 | tf_op jit(solution)/shard_map/ppermute | solution.py:636
  164.3 3.7 %collective-permute-done.22 = bf16[1,2,2,288,128]{4,3,2,1,0:T(8,128)(2,1)S(1)} collective-permute-done((bf16[1,2,2,288,128]{4,3,2,1,0:T(8,128)(2,1)S(1)}, bf16[1,2,2,288,128]{4,3,2,1,0:T(8,128)(2,1)S(1)}, u32[]{:S(2)}, u32[]{:S(2)}) %collective-permute-start.22) | collective-permute-done | bytes 294944 | tf_op jit(solution)/shard_map/ppermute | solution.py:636
  171.3 1.9 collective-permute-start.21
  173.2 7.4 %collective-permute-done.20 = bf16[1,2,2,136,128]{4,3,2,1,0:T(8,128)(2,1)S(1)} collective-permute-done((bf16[1,2,2,136,128]{4,3,2,1,0:T(8,128)(2,1)S(1)}, bf16[1,2,2,136,128]{4,3,2,1,0:T(8,128)(2,1)S(1)}, u32[]{:S(2)}, u32[]{:S(2)}) %collective-permute-start.20) | collective-permute-done | bytes 139296 | tf_op jit(solution)/shard_map/ppermute | solution.py:636
  181.3 2.0 %collective-permute-start.24 = (bf16[2,2,2,136,128]{4,3,2,1,0:T(8,128)(2,1)S(1)}, bf16[2,2,2,136,128]{4,3,2,1,0:T(8,128)(2,1)S(1)}, u32[]{:S(2)}, u32[]{:S(2)}) collective-permute-start(bf16[2,2,2,136,128]{4,3,2,1,0:T(8,128)(2,1)S(1)} %pad_maximum_fusion.6), channel_id=1, source_target_pairs={{0,1},{1,0},{2,3},{3,2},{4,5},{5,4},{6,7},{7,6},{8,9},{9,8},{10,11... | collective-permute-start | bytes 835592 | tf_op jit(solution)/shard_map/ppermute | solution.py:636
  185.8 6.1 %shard_map.260 = (f32[512,2048]{1,0:T(8,128)}, f32[2048,512]{1,0:T(8,128)}, f32[256,512]{1,0:T(8,128)}) custom-call(s32[5]{0:T(128)S(1)} %copy-done, bf16[2,4,2,2,288,128]{5,4,3,2,1,0:T(8,128)(2,1)S(1)} %pad_maximum_fusion.refs_1_, bf16[2,4,2,2,288,128]{5,4,3,2,1,0:T(8,128)(2,1)S(1)} %collective-permute-done.28.refs_2_), custom_call_target="tpu_custom_call" | custom-call | flops 17179869184 | bytes 16777216 | tf_op jit(solution)/shard_map/pallas_call | solution.py:817
  192.4 2.7 %collective-permute-done.29.refs_2_ = bf16[2,4,2,2,136,128]{5,4,3,2,1,0:T(8,128)(2,1)S(1)} collective-permute-done((bf16[2,4,2,2,136,128]{5,4,3,2,1,0:T(8,128)(2,1)S(1)}, bf16[2,4,2,2,136,128]{5,4,3,2,1,0:T(8,128)(2,1)S(1)}, u32[]{:S(2)}, u32[]{:S(2)}) %collective-permute-start.29) | collective-permute-done | bytes 1114144 | tf_op jit(solution)/shard_map/ppermute | solution.py:636
  195.1 3.0 %shard_map.261 = (f32[512,256]{1,0:T(8,128)}, f32[512,256]{1,0:T(8,128)}, f32[512,256]{1,0:T(8,128)}, f32[512,512]{1,0:T(8,128)}, f32[8,512]{1,0:T(8,128)}, /*in...) custom-call(s32[5]{0:T(128)S(1)} %copy-done, ...), custom_call_target="tpu_custom_call" | custom-call | flops 17179869184 | bytes 16777216 | tf_op jit(solution)/shard_map/pallas_call | solution.py:817
  (96 shorter events, 29.1 us)
Async XLA Ops:
  4.0 15.2 %collective-permute-start = (bf16[2048,128]{1,0:T(8,128)(2,1)}, bf16[2048,128]{1,0:T(8,128)(2,1)S(1)}, u32[]{:S(2)}, u32[]{:S(2)}) collective-permute-start(bf16[2048,128]{1,0:T(8,128)(2,1)} %shard_map.254), channel_id=1, source_target_pairs={{0,1},{1,0},{2,3},{3,2},{4,5},{5,4},{6,7},{7,6},{8,9},{9,8},{10,11... | collective-permute-start | bytes 1572872 | tf_op jit(solution)/shard_map/ppermute | solution.py:636
  19.2 1.9 collective-permute-start.1
  58.9 8.1 %collective-permute-start.2 = (bf16[2,4,4,288,128]{4,3,2,1,0:T(8,128)(2,1)}, bf16[2,4,4,288,128]{4,3,2,1,0:T(8,128)(2,1)}, u32[]{:S(2)}, u32[]{:S(2)}) collective-permute-start(bf16[2,4,4,288,128]{4,3,2,1,0:T(8,128)(2,1)} %get-tuple-element.102), channel_id=1, source_target_pairs={{0,2},{1,3},{2,0},{3,1},{4,6},{5,7},{6,4},{7,5},{8,10},{9,11},{10,... | collective-permute-start | bytes 7077896 | tf_op jit(solution)/shard_map/ppermute | solution.py:636
  68.8 17.6 %copy-start.1 = (bf16[1,4,4,288,128]{4,3,2,1,0:T(8,128)(2,1)}, bf16[1,4,4,288,128]{4,3,2,1,0:T(8,128)(2,1)S(1)}, u32[]{:S(2)}) copy-start(bf16[1,4,4,288,128]{4,3,2,1,0:T(8,128)(2,1)S(1)} %get-tuple-element.175) | copy-start | bytes 3538948
  69.0 15.7 %collective-permute-start.3 = (bf16[2,2,2,288,128]{4,3,2,1,0:T(8,128)(2,1)S(1)}, bf16[2,2,2,288,128]{4,3,2,1,0:T(8,128)(2,1)S(1)}, u32[]{:S(2)}, u32[]{:S(2)}) collective-permute-start(bf16[2,2,2,288,128]{4,3,2,1,0:T(8,128)(2,1)S(1)} %fusion), channel_id=1, source_target_pairs={{0,1},{1,0},{2,3},{3,2},{4,5},{5,4},{6,7},{7,6},{8,9},{9,8},{10,11... | collective-permute-start | bytes 1769480 | tf_op jit(solution)/shard_map/ppermute | solution.py:636
  71.0 15.4 %collective-permute-start.4 = (bf16[2,2,2,288,128]{4,3,2,1,0:T(8,128)(2,1)S(1)}, bf16[2,2,2,288,128]{4,3,2,1,0:T(8,128)(2,1)S(1)}, u32[]{:S(2)}, u32[]{:S(2)}) collective-permute-start(bf16[2,2,2,288,128]{4,3,2,1,0:T(8,128)(2,1)S(1)} %fusion.1), channel_id=1, source_target_pairs={{0,4},{1,5},{2,6},{3,7},{4,0},{5,1},{6,2},{7,3},{8,12},{9,13},{10,... | collective-permute-start | bytes 1769480 | tf_op jit(solution)/shard_map/ppermute | solution.py:636
  105.3 13.9 %collective-permute-start.5 = (bf16[2,4,4,136,128]{4,3,2,1,0:T(8,128)(2,1)}, bf16[2,4,4,136,128]{4,3,2,1,0:T(8,128)(2,1)}, u32[]{:S(2)}, u32[]{:S(2)}) collective-permute-start(bf16[2,4,4,136,128]{4,3,2,1,0:T(8,128)(2,1)} %get-tuple-element.132), channel_id=1, source_target_pairs={{0,2},{1,3},{2,0},{3,1},{4,6},{5,7},{6,4},{7,5},{8,10},{9,11},{10,... | collective-permute-start | bytes 3342344 | tf_op jit(solution)/shard_map/ppermute | solution.py:636
  105.4 9.7 %collective-permute-start.8 = (bf16[2,2,288,128]{3,2,1,0:T(8,128)(2,1)}, bf16[2,2,288,128]{3,2,1,0:T(8,128)(2,1)}, u32[]{:S(2)}, u32[]{:S(2)}) collective-permute-start(bf16[2,2,288,128]{3,2,1,0:T(8,128)(2,1)} %fusion.3), channel_id=1, source_target_pairs={{0,4},{1,5},{2,6},{3,7},{4,0},{5,1},{6,2},{7,3},{8,12},{9,13},{10,... | collective-permute-start | bytes 884744 | tf_op jit(solution)/shard_map/ppermute | solution.py:636
  107.0 9.4 %collective-permute-start.9 = (bf16[2,2,288,128]{3,2,1,0:T(8,128)(2,1)}, bf16[2,2,288,128]{3,2,1,0:T(8,128)(2,1)}, u32[]{:S(2)}, u32[]{:S(2)}) collective-permute-start(bf16[2,2,288,128]{3,2,1,0:T(8,128)(2,1)} %fusion.2), channel_id=1, source_target_pairs={{0,1},{1,0},{2,3},{3,2},{4,5},{5,4},{6,7},{7,6},{8,9},{9,8},{10,11... | collective-permute-start | bytes 884744 | tf_op jit(solution)/shard_map/ppermute | solution.py:636
  107.5 8.9 %copy-start.5 = (bf16[2,2,2,288,128]{4,3,2,1,0:T(8,128)(2,1)S(1)}, bf16[2,2,2,288,128]{4,3,2,1,0:T(8,128)(2,1)}, u32[]{:S(2)}) copy-start(bf16[2,2,2,288,128]{4,3,2,1,0:T(8,128)(2,1)} %copy-done.4) | copy-start | bytes 1769476
  117.6 8.3 %collective-permute-start.10 = (bf16[2,2,288,128]{3,2,1,0:T(8,128)(2,1)S(1)}, bf16[2,2,288,128]{3,2,1,0:T(8,128)(2,1)S(1)}, u32[]{:S(2)}, u32[]{:S(2)}) collective-permute-start(bf16[2,2,288,128]{3,2,1,0:T(8,128)(2,1)S(1)} %pad_maximum_fusion.5), channel_id=1, source_target_pairs={{0,8},{1,9},{2,10},{3,11},{4,12},{5,13},{6,14},{7,15},{8,0},{9,1},... | collective-permute-start | bytes 884744 | tf_op jit(solution)/shard_map/ppermute | solution.py:636
  120.6 9.9 %collective-permute-start.6 = (bf16[2,2,2,136,128]{4,3,2,1,0:T(8,128)(2,1)S(1)}, bf16[2,2,2,136,128]{4,3,2,1,0:T(8,128)(2,1)S(1)}, u32[]{:S(2)}, u32[]{:S(2)}) collective-permute-start(bf16[2,2,2,136,128]{4,3,2,1,0:T(8,128)(2,1)S(1)} %fusion.9), channel_id=1, source_target_pairs={{0,1},{1,0},{2,3},{3,2},{4,5},{5,4},{6,7},{7,6},{8,9},{9,8},{10,11... | collective-permute-start | bytes 835592 | tf_op jit(solution)/shard_map/ppermute | solution.py:636
  121.3 9.3 %collective-permute-start.7 = (bf16[2,2,2,136,128]{4,3,2,1,0:T(8,128)(2,1)S(1)}, bf16[2,2,2,136,128]{4,3,2,1,0:T(8,128)(2,1)S(1)}, u32[]{:S(2)}, u32[]{:S(2)}) collective-permute-start(bf16[2,2,2,136,128]{4,3,2,1,0:T(8,128)(2,1)S(1)} %fusion.10), channel_id=1, source_target_pairs={{0,4},{1,5},{2,6},{3,7},{4,0},{5,1},{6,2},{7,3},{8,12},{9,13},{10,... | collective-permute-start | bytes 835592 | tf_op jit(solution)/shard_map/ppermute | solution.py:636
  127.9 8.3 %collective-permute-start.13 = (bf16[2,288,128]{2,1,0:T(8,128)(2,1)S(1)}, bf16[2,288,128]{2,1,0:T(8,128)(2,1)S(1)}, u32[]{:S(2)}, u32[]{:S(2)}) collective-permute-start(bf16[2,288,128]{2,1,0:T(8,128)(2,1)S(1)} %pad_maximum_fusion.8), channel_id=1, source_target_pairs={{0,16},{1,17},{2,18},{3,19},{4,20},{5,21},{6,22},{7,23},{8,24},{9,... | collective-permute-start | bytes 442376 | tf_op jit(solution)/shard_map/ppermute | solution.py:636
  130.6 6.7 %collective-permute-start.11 = (bf16[2,2,136,128]{3,2,1,0:T(8,128)(2,1)S(1)}, bf16[2,2,136,128]{3,2,1,0:T(8,128)(2,1)S(1)}, u32[]{:S(2)}, u32[]{:S(2)}) collective-permute-start(bf16[2,2,136,128]{3,2,1,0:T(8,128)(2,1)S(1)} %fusion.12), channel_id=1, source_target_pairs={{0,4},{1,5},{2,6},{3,7},{4,0},{5,1},{6,2},{7,3},{8,12},{9,13},{10,... | collective-permute-start | bytes 417800 | tf_op jit(solution)/shard_map/ppermute | solution.py:636
  131.4 5.9 %collective-permute-start.12 = (bf16[2,2,136,128]{3,2,1,0:T(8,128)(2,1)S(1)}, bf16[2,2,136,128]{3,2,1,0:T(8,128)(2,1)S(1)}, u32[]{:S(2)}, u32[]{:S(2)}) collective-permute-start(bf16[2,2,136,128]{3,2,1,0:T(8,128)(2,1)S(1)} %fusion.11), channel_id=1, source_target_pairs={{0,1},{1,0},{2,3},{3,2},{4,5},{5,4},{6,7},{7,6},{8,9},{9,8},{10,11... | collective-permute-start | bytes 417800 | tf_op jit(solution)/shard_map/ppermute | solution.py:636
  137.5 7.4 %collective-permute-start.14 = (bf16[2,2,136,128]{3,2,1,0:T(8,128)(2,1)S(1)}, bf16[2,2,136,128]{3,2,1,0:T(8,128)(2,1)S(1)}, u32[]{:S(2)}, u32[]{:S(2)}) collective-permute-start(bf16[2,2,136,128]{3,2,1,0:T(8,128)(2,1)S(1)} %pad_maximum_fusion.10), channel_id=1, source_target_pairs={{0,8},{1,9},{2,10},{3,11},{4,12},{5,13},{6,14},{7,15},{8,0},{9,1},... | collective-permute-start | bytes 417800 | tf_op jit(solution)/shard_map/ppermute | solution.py:636
  138.3 10.8 %collective-permute-start.16 = (bf16[2,1,288,128]{3,2,1,0:T(8,128)(2,1)S(1)}, bf16[2,1,288,128]{3,2,1,0:T(8,128)(2,1)S(1)}, u32[]{:S(2)}, u32[]{:S(2)}) collective-permute-start(bf16[2,1,288,128]{3,2,1,0:T(8,128)(2,1)S(1)} %maximum_bitcast_fusion.5), channel_id=1, source_target_pairs={{0,16},{1,17},{2,18},{3,19},{4,20},{5,21},{6,22},{7,23},{8,24},{9,... | collective-permute-start | bytes 442376 | tf_op jit(solution)/shard_map/ppermute | solution.py:636
  145.0 5.8 %collective-permute-start.15 = (bf16[2,136,128]{2,1,0:T(8,128)(2,1)S(1)}, bf16[2,136,128]{2,1,0:T(8,128)(2,1)S(1)}, u32[]{:S(2)}, u32[]{:S(2)}) collective-permute-start(bf16[2,136,128]{2,1,0:T(8,128)(2,1)S(1)} %pad_maximum_fusion.11), channel_id=1, source_target_pairs={{0,16},{1,17},{2,18},{3,19},{4,20},{5,21},{6,22},{7,23},{8,24},{9,... | collective-permute-start | bytes 208904 | tf_op jit(solution)/shard_map/ppermute | solution.py:636
  149.1 8.9 %collective-permute-start.18 = (bf16[2,1,2,288,128]{4,3,2,1,0:T(8,128)(2,1)S(1)}, bf16[2,1,2,288,128]{4,3,2,1,0:T(8,128)(2,1)S(1)}, u32[]{:S(2)}, u32[]{:S(2)}) collective-permute-start(bf16[2,1,2,288,128]{4,3,2,1,0:T(8,128)(2,1)S(1)} %maximum_bitcast_fusion.4), channel_id=1, source_target_pairs={{0,8},{1,9},{2,10},{3,11},{4,12},{5,13},{6,14},{7,15},{8,0},{9,1},... | collective-permute-start | bytes 884744 | tf_op jit(solution)/shard_map/ppermute | solution.py:636
  151.0 8.1 %collective-permute-start.17 = (bf16[2,1,136,128]{3,2,1,0:T(8,128)(2,1)S(1)}, bf16[2,1,136,128]{3,2,1,0:T(8,128)(2,1)S(1)}, u32[]{:S(2)}, u32[]{:S(2)}) collective-permute-start(bf16[2,1,136,128]{3,2,1,0:T(8,128)(2,1)S(1)} %maximum_bitcast_fusion.7), channel_id=1, source_target_pairs={{0,16},{1,17},{2,18},{3,19},{4,20},{5,21},{6,22},{7,23},{8,24},{9,... | collective-permute-start | bytes 208904 | tf_op jit(solution)/shard_map/ppermute | solution.py:636
  158.1 9.9 %collective-permute-start.22 = (bf16[1,2,2,288,128]{4,3,2,1,0:T(8,128)(2,1)S(1)}, bf16[1,2,2,288,128]{4,3,2,1,0:T(8,128)(2,1)S(1)}, u32[]{:S(2)}, u32[]{:S(2)}) collective-permute-start(bf16[1,2,2,288,128]{4,3,2,1,0:T(8,128)(2,1)S(1)} %get-tuple-element.181), channel_id=1, source_target_pairs={{0,4},{1,5},{2,6},{3,7},{4,0},{5,1},{6,2},{7,3},{8,12},{9,13},{10,... | collective-permute-start | bytes 884744 | tf_op jit(solution)/shard_map/ppermute | solution.py:636
  159.1 9.9 %collective-permute-start.23 = (bf16[1,2,2,288,128]{4,3,2,1,0:T(8,128)(2,1)S(1)}, bf16[1,2,2,288,128]{4,3,2,1,0:T(8,128)(2,1)S(1)}, u32[]{:S(2)}, u32[]{:S(2)}) collective-permute-start(bf16[1,2,2,288,128]{4,3,2,1,0:T(8,128)(2,1)S(1)} %get-tuple-element.180), channel_id=1, source_target_pairs={{0,1},{1,0},{2,3},{3,2},{4,5},{5,4},{6,7},{7,6},{8,9},{9,8},{10,11... | collective-permute-start | bytes 884744 | tf_op jit(solution)/shard_map/ppermute | solution.py:636
  159.1 5.1 %collective-permute-start.19 = (bf16[2,1,2,136,128]{4,3,2,1,0:T(8,128)(2,1)S(1)}, bf16[2,1,2,136,128]{4,3,2,1,0:T(8,128)(2,1)S(1)}, u32[]{:S(2)}, u32[]{:S(2)}) collective-permute-start(bf16[2,1,2,136,128]{4,3,2,1,0:T(8,128)(2,1)S(1)} %maximum_bitcast_fusion.6), channel_id=1, source_target_pairs={{0,8},{1,9},{2,10},{3,11},{4,12},{5,13},{6,14},{7,15},{8,0},{9,1},... | collective-permute-start | bytes 417800 | tf_op jit(solution)/shard_map/ppermute | solution.py:636
  169.1 11.6 %collective-permute-start.26 = (bf16[2,2,2,288,128]{4,3,2,1,0:T(8,128)(2,1)S(1)}, bf16[2,2,2,288,128]{4,3,2,1,0:T(8,128)(2,1)S(1)}, u32[]{:S(2)}, u32[]{:S(2)}) collective-permute-start(bf16[2,2,2,288,128]{4,3,2,1,0:T(8,128)(2,1)S(1)} %pad_maximum_fusion.2), channel_id=1, source_target_pairs={{0,1},{1,0},{2,3},{3,2},{4,5},{5,4},{6,7},{7,6},{8,9},{9,8},{10,11... | collective-permute-start | bytes 1769480 | tf_op jit(solution)/shard_map/ppermute | solution.py:636
  169.2 11.5 %collective-permute-start.27 = (bf16[2,2,2,288,128]{4,3,2,1,0:T(8,128)(2,1)S(1)}, bf16[2,2,2,288,128]{4,3,2,1,0:T(8,128)(2,1)S(1)}, u32[]{:S(2)}, u32[]{:S(2)}) collective-permute-start(bf16[2,2,2,288,128]{4,3,2,1,0:T(8,128)(2,1)S(1)} %pad_maximum_fusion.3), channel_id=1, source_target_pairs={{0,4},{1,5},{2,6},{3,7},{4,0},{5,1},{6,2},{7,3},{8,12},{9,13},{10,... | collective-permute-start | bytes 1769480 | tf_op jit(solution)/shard_map/ppermute | solution.py:636
  170.4 10.3 %collective-permute-start.20 = (bf16[1,2,2,136,128]{4,3,2,1,0:T(8,128)(2,1)S(1)}, bf16[1,2,2,136,128]{4,3,2,1,0:T(8,128)(2,1)S(1)}, u32[]{:S(2)}, u32[]{:S(2)}) collective-permute-start(bf16[1,2,2,136,128]{4,3,2,1,0:T(8,128)(2,1)S(1)} %get-tuple-element.185), channel_id=1, source_target_pairs={{0,4},{1,5},{2,6},{3,7},{4,0},{5,1},{6,2},{7,3},{8,12},{9,13},{10,... | collective-permute-start | bytes 417800 | tf_op jit(solution)/shard_map/ppermute | solution.py:636
  171.3 9.4 %collective-permute-start.21 = (bf16[1,2,2,136,128]{4,3,2,1,0:T(8,128)(2,1)S(1)}, bf16[1,2,2,136,128]{4,3,2,1,0:T(8,128)(2,1)S(1)}, u32[]{:S(2)}, u32[]{:S(2)}) collective-permute-start(bf16[1,2,2,136,128]{4,3,2,1,0:T(8,128)(2,1)S(1)} %get-tuple-element.184), channel_id=1, source_target_pairs={{0,1},{1,0},{2,3},{3,2},{4,5},{5,4},{6,7},{7,6},{8,9},{9,8},{10,11... | collective-permute-start | bytes 417800 | tf_op jit(solution)/shard_map/ppermute | solution.py:636
  181.2 4.6 %collective-permute-start.28 = (bf16[2,4,2,2,288,128]{5,4,3,2,1,0:T(8,128)(2,1)S(1)}, bf16[2,4,2,2,288,128]{5,4,3,2,1,0:T(8,128)(2,1)S(1)}, u32[]{:S(2)}, u32[]{:S(2)}) collective-permute-start(bf16[2,4,2,2,288,128]{5,4,3,2,1,0:T(8,128)(2,1)S(1)} %pad_maximum_fusion.refs_1_), channel_id=1, source_target_pairs={{0,2},{1,3},{2,0},{3,1},{4,6},{5,7},{6,4},{7,5},{8,10},{9,11},{10,... | collective-permute-start | bytes 7077896 | tf_op jit(solution)/shard_map/ppermute | solution.py:636
  181.3 10.6 %collective-permute-start.24 = (bf16[2,2,2,136,128]{4,3,2,1,0:T(8,128)(2,1)S(1)}, bf16[2,2,2,136,128]{4,3,2,1,0:T(8,128)(2,1)S(1)}, u32[]{:S(2)}, u32[]{:S(2)}) collective-permute-start(bf16[2,2,2,136,128]{4,3,2,1,0:T(8,128)(2,1)S(1)} %pad_maximum_fusion.6), channel_id=1, source_target_pairs={{0,1},{1,0},{2,3},{3,2},{4,5},{5,4},{6,7},{7,6},{8,9},{9,8},{10,11... | collective-permute-start | bytes 835592 | tf_op jit(solution)/shard_map/ppermute | solution.py:636
  183.3 8.7 %collective-permute-start.25 = (bf16[2,2,2,136,128]{4,3,2,1,0:T(8,128)(2,1)S(1)}, bf16[2,2,2,136,128]{4,3,2,1,0:T(8,128)(2,1)S(1)}, u32[]{:S(2)}, u32[]{:S(2)}) collective-permute-start(bf16[2,2,2,136,128]{4,3,2,1,0:T(8,128)(2,1)S(1)} %pad_maximum_fusion.7), channel_id=1, source_target_pairs={{0,4},{1,5},{2,6},{3,7},{4,0},{5,1},{6,2},{7,3},{8,12},{9,13},{10,... | collective-permute-start | bytes 835592 | tf_op jit(solution)/shard_map/ppermute | solution.py:636
  192.3 2.8 %collective-permute-start.29 = (bf16[2,4,2,2,136,128]{5,4,3,2,1,0:T(8,128)(2,1)S(1)}, bf16[2,4,2,2,136,128]{5,4,3,2,1,0:T(8,128)(2,1)S(1)}, u32[]{:S(2)}, u32[]{:S(2)}) collective-permute-start(bf16[2,4,2,2,136,128]{5,4,3,2,1,0:T(8,128)(2,1)S(1)} %pad_maximum_fusion.1.refs_1_), channel_id=1, source_target_pairs={{0,2},{1,3},{2,0},{3,1},{4,6},{5,7},{6,4},{7,5},{8,10},{9,11},{10,... | collective-permute-start | bytes 3342344 | tf_op jit(solution)/shard_map/ppermute | solution.py:636
  (6 other events, 21.6 us)
where the time goes:
time: 199 us; the launch traced here: 198 us
  Pallas kernels  93.4 us (47%)
  waiting for transfers between devices  57.2 us (29%)
  starting transfers between devices  30.7 us (15%)
  other arithmetic  7.88 us (4%)
  local copies, waits for them, and re-layouts  7.79 us (4%)
    pallas_call x8, Pallas kernels, call(): pl.pallas_call(kernel, in_specs=[smem] * n_scalars + [pl.BlockSpec(memory...  93.4 us
    ppermute x30, waiting for transfers between devices, swap(): return lax.ppermute(values, AXES, pairs)  57.2 us
    ppermute x30, starting transfers between devices, swap(): return lax.ppermute(values, AXES, pairs)  30.7 us
    convert_element_type x17, other arithmetic, low_sum(): return total.astype(LOW)  6.81 us
    slice x4, local copies, waits for them, and re-layouts, sum_chain(): sums = [[kept[c].reshape(shape), got[c].reshape(shape)] for c in range(2)]  6.34 us
  transfers between devices with their start and end apart: 30, of which 19 were waited for; matrix products, arithmetic and copies ran while one was open for 5% of the time, Pallas kernels for 17%

commit v1 on v0

--- a/solution.py
+++ b/solution.py
@@ -17,7 +17,8 @@
 LOW = jnp.bfloat16
 AXES = ("dp", "head")
 VMEM_LIMIT = 56 * 1024 * 1024
-TURNS = ["ffn", "last", "last", "ffn", "last", "ffn", "last", "last", "ffn", "last", "ffn", "last", "last", "ffn", "last", "ffn"]
+TURNS = ["last", "last", "ffn", "output", "last", "ffn", "input", "last", "ffn", "ffn", "last"]
+LAST_HALVED = False
 
 ERF_P = 0.3875
 ERF_C = (
@@ -188,10 +189,10 @@
 
 def forward_kernel(
     count, lens, ids, w_q, w_k, w_v, w_o, near_w, far_w, normed, plan, tokens, ln_gain, ln_bias,
-    up, grad_hidden, cot_t, down, cotangent,
-    q_out, k_out, v_out, sk_out, sv_out, p_out, w_all, sent, kept, output, grad_middle, grad_att,
-    grad_vecs,
-    mask, mixed, mixed_t, middle, normed2, normed2_t, up0, up1, hid0, hid1, gup0, gup1, out_s, gn_s,
+    up, grad_hidden, cot_t, cotangent,
+    q_out, k_out, v_out, sk_out, sv_out, p_out, w_all, sent, kept, hidden_out, middle, grad_middle,
+    grad_att, grad_vecs,
+    mask, mixed, mixed_t, normed2, normed2_t, up0, up1, hid0, hid1, gup0, gup1, gn_s,
     grad_s, parts, part_sems,
 ):
     mask[...] = head_mask(HD**-0.5)
@@ -269,9 +270,9 @@
         return carry
 
     lax.fori_loop(0, count, one, 0)
-    for out in (q_out, k_out, v_out, sk_out, sv_out, p_out):
+    for out in (q_out, k_out, v_out, sk_out, sv_out, p_out, middle):
         out.send()
-    for value in (up, grad_hidden, cot_t, down, cotangent):
+    for value in (up, grad_hidden, cot_t, cotangent):
         value.wait()
     units = up.shape[1] // PART // 2
     quarter = normed.shape[1] // 4
@@ -287,7 +288,9 @@
     def gate_rows(c, side, rows):
         v = ups[side][rows, :]
         share, bell = normal_parts(v)
-        hids[side][rows, :] = (v * share).astype(LOW)
+        hidden = (v * share).astype(LOW)
+        hids[side][rows, :] = hidden
+        hidden_out[rows, columns(c)] = hidden
         gh = grad_hidden[rows, columns(c)].astype(F32)
         gups[side][rows, :] = (gh * (share + v * bell)).astype(LOW)
 
@@ -310,17 +313,15 @@
                 for i in range(4):
                     tile = grad[quarter * i : quarter * (i + 1), 128 * j : 128 * (j + 1)]
                     at = slice(quarter * j, quarter * (j + 1))
-                    parts[c // units, color, c % units, i, at, :] = tile
-        out_s[...] += dot_nn(hidden, down[columns(c), :])
+                    parts[c // units, c % units, i, color, at, :] = tile
         gn_s[...] += dot_nt(gup, up[:, columns(c)])
 
     def part_copy(n, u):
-        at = (slice(None), u, slice(None), slice(0, PART))
+        at = (u, slice(None), slice(None), slice(0, PART))
         return pltpu.make_async_copy(
             parts.at[n].at[at], (sent, kept)[n].at[at], part_sems.at[n * units + u]
         )
 
-    out_s[...] = jnp.zeros_like(out_s)
     gn_s[...] = jnp.zeros_like(gn_s)
     last = 2 * units - 1
     expand(0, 0)
@@ -339,6 +340,7 @@
     for u in range(units):
         part_copy(0, u).start()
     gate(last, 1)
+    hidden_out.send()
     reduce(last - 1, 0)
     reduce(last, 1)
 
@@ -350,13 +352,12 @@
         gmid = cotangent[seq, :].astype(F32) + norm_pull(gn * ln_gain[...], unit, scale)
         grad_middle[seq, :] = gmid
         grad_att[seq, :] = gmid.astype(LOW)
-        output[seq, :] = (mid + out_s[seq, :]).astype(LOW)
         gain = gain + jnp.sum(gn * unit, axis=0, keepdims=True)
         return gain, bias + jnp.sum(gn, axis=0, keepdims=True)
 
     zero = jnp.zeros((1, middle.shape[1]), F32)
     gain, bias = lax.fori_loop(0, count, pull, (zero, zero))
-    for out in (grad_att, grad_middle, output):
+    for out in (grad_att, grad_middle):
         out.send()
     grad_vecs[0:1, :] = gain
     grad_vecs[1:2, :] = bias
@@ -371,7 +372,7 @@
                 for h in range(2):
                     at = pl.multiple_of((base + j) * 64 + 32 * h, 32)
                     tile = grad_s[pl.ds(at, 32), 128 * m : 128 * (m + 1)].astype(LOW)
-                    parts[n, m // 2, j, 2 * (m % 2) + h, PART : PART + 32, :] = tile
+                    parts[n, j, 2 * (m % 2) + h, m // 2, PART : PART + 32, :] = tile
         at = (slice(None), slice(None), slice(None), slice(PART, PART + 32))
         tail = pltpu.make_async_copy(
             parts.at[n].at[at], target.at[at], part_sems.at[2 * units + n]
@@ -395,7 +396,7 @@
             for p in range(4):
                 for m in range(4):
                     part = tile[8 * p : 8 * (p + 1), 128 * m : 128 * (m + 1)]
-                    target[color, u, p, base + 8 * m : base + 8 * (m + 1), :] = part
+                    target[u, p, color, base + 8 * m : base + 8 * (m + 1), :] = part
             return carry
 
         lax.fori_loop(0, 8, unit, 0)
@@ -477,9 +478,9 @@
 def last_kernel(cuts, count, lens, ids, grad_att, w_all, q_in, k_in, v_in, sk_in, sv_in, p_in, plan, *refs):
     first, groups = cuts[-2], len(cuts) - 2
     early, refs = refs[: 4 * groups], refs[4 * groups :]
-    normed_t, steps, pre, summary, sort_one, sort_two, ln_gain, vecs2, tokens, grad_middle = refs[:10]
-    sent, kept, input_grad, mask, go_s, dks, dvs, dk_own, dv_own = refs[10:19]
-    grad_q, grad_k, grad_v, grad_plan, gsum, small, grad_s = refs[19:]
+    normed_t, steps, pre, summary, sort_one, sort_two, ln_gain, ln_bias, vecs2 = refs[:9]
+    sent, kept, grad_q, grad_k, grad_v, gsum = refs[9:15]
+    mask, go_s, dks, dvs, dk_own, dv_own, grad_plan, small, grad_s, prod_s = refs[15:]
     mask[...] = head_mask(1.0)
     ins = (grad_att, w_all, q_in, k_in, v_in, sk_in, sv_in, p_in, plan)
     for value in ins:
@@ -502,14 +503,22 @@
         axis = 2 - k % 2
         g = g - jnp.exp(steps[k]) * jnp.sum(g, axis=axis, keepdims=True)
     g = jnp.where(plan_allowed(count, spans), g, 0.0).reshape(count * NB, NB)
+    for out in (grad_q, grad_k, grad_v):
+        out.send()
     d = normed_t.shape[0]
+    bias = jnp.zeros((8, d), F32)
     for slot in range(3):
         grad = jnp.zeros((d, d), F32)
         for n, rows in enumerate(kinds[slot]):
             grad += dot_nn(normed_t[:, cuts[n] * LMAX : cuts[n + 1] * LMAX], rows[...])
         grad_s[...] = grad
         scatter_tiles(ids[0], sent, kept, grad_s, 32 * slot)
-    for value in (pre, summary, sort_one, sort_two, ln_gain, vecs2, tokens, grad_middle):
+        prod = grad * w_all[slot].astype(F32)
+        prod_s[...] = prod if slot == 0 else prod_s[...] + prod
+        rows = [dot_nn(jnp.ones((8, part.shape[0]), LOW), part[...]) for part in kinds[slot]]
+        for part in split2(sum(rows[1:], rows[0])):
+            bias += dot_nt(part, w_all[slot])
+    for value in (pre, summary, sort_one, sort_two, ln_gain, ln_bias, vecs2):
         value.wait()
     before = pre[...]
     share, bell = normal_parts(before)
@@ -519,24 +528,18 @@
     gpre = exact_right(dot_nn, g, sort_two[...]) * (share + before * bell)
     grad_s[...] = exact_both(dot_tn, summary[...], gpre)
     scatter_tiles(ids[0], sent, kept, grad_s, 96)
-    gsum[...] = exact_right(dot_nt, gpre, sort_one[...]) * SUMMARY_SCALE
-    gain, bias = jnp.zeros((1, d), F32), jnp.zeros((1, d), F32)
-    token, block = iota((LMAX, NB), 0), iota((LMAX, NB), 1)
+    spread = exact_right(dot_nt, gpre, sort_one[...]) * SUMMARY_SCALE
+    gsum[...] = spread
+    gsum.send()
+    block = iota((count * NB, 1), 0)
+    valid = jnp.zeros((count * NB, 1), jnp.int32)
     for s in range(count):
-        seq = slice(s * LMAX, (s + 1) * LMAX)
-        unit, scale = row_norm(tokens[seq, :].astype(F32))
-        member = (token // BL == block) & (token < spans[s])
-        picked = jnp.where(member, 1.0, 0.0).astype(LOW)
-        high, mid, low = split3(gsum[s * NB : (s + 1) * NB, :])
-        gn = dot_nn(picked, high) + dot_nn(picked, mid) + dot_nn(picked, low)
-        for slot in range(3):
-            group = max(n for n in range(groups + 1) if cuts[n] <= s)
-            at = (s - cuts[group]) * LMAX
-            gn += dot_nt(kinds[slot][group][at : at + LMAX, :], w_all[slot])
-        gain += jnp.sum(gn * unit, axis=0, keepdims=True)
-        bias += jnp.sum(gn, axis=0, keepdims=True)
-        pulled = norm_pull(gn * ln_gain[...], unit, scale)
-        input_grad[seq, :] = (grad_middle[seq, :] + pulled).astype(LOW)
+        valid = jnp.where(block // NB == s, jnp.clip(spans[s] - block % NB * BL, 0, BL), valid)
+    bias = bias[0:1] + jnp.sum(spread * valid.astype(F32), axis=0, keepdims=True)
+    gain = jnp.sum(spread * summary[...], axis=0, keepdims=True) * (1.0 / SUMMARY_SCALE)
+    for part in split2(prod_s[...]):
+        gain += dot_nt(jnp.ones((8, d), LOW), part)[0:1]
+    gain = (gain - ln_bias[...] * bias) / ln_gain[...]
     small[8:9, :] = gain
     small[9:10, :] = bias
     zeros = jnp.zeros((8, 128), LOW)
@@ -546,23 +549,59 @@
             tile = small[at, 128 * u : 128 * (u + 1)].astype(LOW)
             for color in range(2):
                 for i in range(4):
-                    target[color, u, i, 128:136, :] = tile if color == 0 and i == 0 else zeros
-
-
-def each_piece(ids, near, far, place, looped):
-    core, x, head = ids[0], ids[1], ids[2]
-    for color in range(2):
-        one, two = ((head, x), (x, head))[color]
-        for n, source in enumerate((near, far)):
-
-            def pieces(r, carry, color=color, one=one, two=two, n=n, source=source):
-                unit = (core ^ n) * 4 + (one ^ (r // 2)) * 2 + (two ^ (r % 2))
+                    target[u, i, color, 128:136, :] = tile if color == 0 and i == 0 else zeros
+
+
+def input_kernel(cuts, count, lens, ids, gsum, w_all, ln_gain, *refs):
+    groups = len(cuts) - 1
+    kinds = [refs[n : 3 * groups : 3] for n in range(3)]
+    tokens, grad_middle = refs[3 * groups : 3 * groups + count], refs[3 * groups + count : -1]
+    input_grad = refs[-1]
+    for value in (gsum, w_all, ln_gain):
+        value.wait()
+    token, block = iota((LMAX, NB), 0), iota((LMAX, NB), 1)
+    for s in range(count):
+        group = max(n for n in range(groups) if cuts[n] <= s)
+        if cuts[group] == s:
+            for slot in range(3):
+                kinds[slot][group].wait()
+        tokens[s].wait()
+        grad_middle[s].wait()
+        unit, scale = row_norm(tokens[s][...].astype(F32))
+        member = (token // BL == block) & (token < lens[ids[2] * count + s])
+        picked = jnp.where(member, 1.0, 0.0).astype(LOW)
+        high, mid, low = split3(gsum[s * NB : (s + 1) * NB, :])
+        gn = dot_nn(picked, high) + dot_nn(picked, mid) + dot_nn(picked, low)
+        at = (s - cuts[group]) * LMAX
+        for slot in range(3):
+            gn += dot_nt(kinds[slot][group][at : at + LMAX, :], w_all[slot])
+        pulled = norm_pull(gn * ln_gain[...], unit, scale)
+        input_grad[s * LMAX : (s + 1) * LMAX, :] = (grad_middle[s][...] + pulled).astype(LOW)
+
+
+def output_kernel(count, down, *refs):
+    hidden, middle, output = refs[:count], refs[count:-1], refs[-1]
+    down.wait()
+    for s in range(count):
+        hidden[s].wait()
+        middle[s].wait()
+        total = middle[s][...] + dot_nn(hidden[s][...], down[...])
+        output[s * LMAX : (s + 1) * LMAX, :] = total.astype(LOW)
+
+
+def each_piece(ids, near, far, place, halved):
+    core, mine = ids[0], ids[1] * 2 + ids[2]
+    for n, source in enumerate((near, far)):
+        for color in range(2):
+
+            def pieces(r, carry, n=n, source=source, color=color):
+                unit = (core ^ n) * 4 + (mine ^ r)
                 for i in range(4):
-                    part = (ids[3] ^ (i // 2)) * 2 + (ids[4] ^ (i % 2))
-                    place(color, unit, part, source.buffer.at[color, r, i // 2, i % 2])
+                    part = (ids[3] ^ (i // 2)) * 2 + (ids[4] ^ (i % 2)) if halved else i
+                    place(color, unit, part, source.buffer.at[r, i // 2, i % 2, color])
                 return carry
 
-            if looped:
+            if halved:
                 lax.fori_loop(0, 4, pieces, 0)
             else:
                 for r in range(4):
@@ -611,7 +650,7 @@
             lanes = pl.ds(pl.multiple_of((unit % 4) * 128, 128), 128)
             small[part, high, lanes] = wide[128:136, :]
 
-    each_piece(ids, near, far, place, False)
+    each_piece(ids, near, far, place, LAST_HALVED)
     second[...] = small[0, 0:NB, :]
     for n, out in enumerate((gain1, bias1, gain2, bias2)):
         out[...] = small[0, 8 + n : 9 + n, :]
@@ -628,11 +667,10 @@
         mine[1536 + 128 * m : 1664 + 128 * m, :] = w_o[lanes, 128 * m : 128 * (m + 1)]
 
 
-def swap(values, bit, dp_size):
-    if bit == "head":
-        pairs = [(d * 2 + h, d * 2 + (1 - h)) for d in range(dp_size) for h in range(2)]
-    else:
-        pairs = [(d * 2 + h, (d ^ bit) * 2 + h) for d in range(dp_size) for h in range(2)]
+def swap(values, bits, dp_size):
+    dp_bits = sum(bit for bit in bits if bit != "head")
+    flip = int("head" in bits)
+    pairs = [(d * 2 + h, (d ^ dp_bits) * 2 + (h ^ flip)) for d in range(dp_size) for h in range(2)]
     return lax.ppermute(values, AXES, pairs)
 
 
@@ -665,44 +703,41 @@
     return bits
 
 
-def sum_chain(sent, kept, dp_size):
-    order = (("head", 2), (2, "head"))
+PLANE = (["head"], [2], [2, "head"])
+
+
+def sum_chain(sent, kept, dp_size, halve):
     line = line_bits(dp_size)
-    got = swap(sent, 1, dp_size)
+    got = swap(sent, [1], dp_size)
     got, = yield [sent], [got]
-    shape = (2, 2, 2, 2) + kept.shape[3:]
-    sums = [[kept[c].reshape(shape), got[c].reshape(shape)] for c in range(2)]
-    for turn in range(2):
-        sides = [side_of(order[c][turn]) for c in range(2)]
-        sents = [low_sum(pick_all(sums[c], 1 - sides[c])) for c in range(2)]
-        gots = [swap(sents[c], order[c][turn], dp_size) for c in range(2)]
-        gots = yield sents, gots
-        sums = [pick_all(sums[c], sides[c]) + [gots[c]] for c in range(2)]
-    for bit in line[:2]:
-        side = side_of(bit)
-        sent = jnp.stack([low_sum(pick_all(sums[c], 1 - side)) for c in range(2)])
-        got = swap(sent, bit, dp_size)
-        got, = yield [sent], [got]
-        sums = [pick_all(sums[c], side) + [got[c]] for c in range(2)]
-    near = jnp.stack([low_sum(sums[c]) for c in range(2)])
-    for bit in line[2:]:
-        got = swap(near, bit, dp_size)
+    shape = (4, 2, 2) + kept.shape[2:]
+    sums = [kept.reshape(shape), got.reshape(shape)]
+    mine = side_of(2) * 2 + side_of("head")
+    sents = [low_sum(pick_all(sums, mine ^ (n + 1))) for n in range(3)]
+    gots = [swap(v, bits, dp_size) for v, bits in zip(sents, PLANE)]
+    gots = yield sents, gots
+    sums = pick_all(sums, mine) + list(gots)
+    if halve:
+        for bit in line[:2]:
+            side = side_of(bit)
+            sent = low_sum(pick_all(sums, 1 - side))
+            got = swap(sent, [bit], dp_size)
+            got, = yield [sent], [got]
+            sums = pick_all(sums, side) + [got]
+    near = low_sum(sums)
+    for bit in line[2:] if halve else line:
+        got = swap(near, [bit], dp_size)
         got, = yield [near], [got]
-        near = (near.astype(F32) + got.astype(F32)).astype(LOW)
-    near = near[:, None]
-    got = swap(near, line[1], dp_size)
-    got, = yield [near], [got]
-    near = jnp.concatenate([near, got], 1)[:, None]
-    got = swap(near, line[0], dp_size)
-    got, = yield [near], [got]
-    near = jnp.concatenate([near, got], 1)
-    near = [near[c][None] for c in range(2)]
-    for turn in (1, 0):
-        gots = [swap(near[c], order[c][turn], dp_size) for c in range(2)]
-        gots = yield near, gots
-        near = [jnp.concatenate([near[c], gots[c]], 0) for c in range(2)]
-    near = jnp.stack(near)
-    far = swap(near, 1, dp_size)
+        near = low_sum([near, got])
+    if halve:
+        for bit in (line[1], line[0]):
+            got = swap(near, [bit], dp_size)
+            got, = yield [near], [got]
+            near = jnp.stack([near, got])
+    gots = [swap(near, bits, dp_size) for bits in PLANE]
+    gots = yield [near], gots
+    near = jnp.stack([near, *gots])
+    far = swap(near, [1], dp_size)
     far, = yield [near], [far]
     return near, far
 
@@ -855,7 +890,7 @@
         slice_kernel, (ids,), (w_query, w_key, w_value, w_out), [shaped((4 * d, 2 * HD), LOW)], [],
         1 << 20,
     )[0]
-    near_w = swap(mine, "head", dp_size)
+    near_w = swap(mine, ["head"], dp_size)
 
     low_rows, wide_rows = shaped((rows_all, d), LOW), shaped((rows_all, d), F32)
     low_cols = shaped((d, rows_all), LOW)
@@ -870,61 +905,86 @@
         [], 2 * rows_all * d * ff,
     )
     near_w, normed = lax.optimization_barrier((near_w, normed))
-    far_w = swap(near_w, 1, dp_size)
+    far_w = swap(near_w, [1], dp_size)
 
     (
-        q, k, v, sk, sv, p, w_all, sent, kept, output, grad_middle, grad_att, vecs2
+        q, k, v, sk, sv, p, w_all, sent, kept, hidden, middle, grad_middle, grad_att, vecs2
     ) = call(
         functools.partial(forward_kernel, count), (lengths, ids),
         (w_query, w_key, w_value, w_out, near_w, far_w, normed, plan, tokens, gain2, bias2)
-        + (w_up, grad_hidden, cot_t, w_down, cotangent),
+        + (w_up, grad_hidden, cot_t, cotangent),
         [low_rows] * 5 + [shaped((count * 2 * LMAX, LMAX), LOW), shaped((4, d, d), LOW)]
-        + [shaped((2, 4, 4, PART + 32, 128), LOW)] * 2 + [low_rows, wide_rows, low_rows, shaped((2, d), F32)],
+        + [shaped((4, 4, 2, PART + 32, 128), LOW)] * 2
+        + [shaped((rows_all, ff), LOW), wide_rows, wide_rows, low_rows, shaped((2, d), F32)],
         [pltpu.VMEM((LMAX, d), LOW)] * 2
-        + [pltpu.VMEM((d, rows_all), LOW), pltpu.VMEM((rows_all, d), F32)]
-        + [pltpu.VMEM((rows_all, d), LOW), pltpu.VMEM((d, rows_all), LOW)]
+        + [pltpu.VMEM((d, rows_all), LOW), pltpu.VMEM((rows_all, d), LOW)]
+        + [pltpu.VMEM((d, rows_all), LOW)]
         + [pltpu.VMEM((rows_all, PART), F32)] * 2 + [pltpu.VMEM((rows_all, PART), LOW)] * 4
-        + [pltpu.VMEM((rows_all, d), F32)] * 2 + [pltpu.VMEM((d, d), F32)]
-        + [pltpu.VMEM((2, 2, 4, 4, PART + 32, 128), LOW)]
+        + [pltpu.VMEM((rows_all, d), F32)] + [pltpu.VMEM((d, d), F32)]
+        + [pltpu.VMEM((2, 4, 4, 2, PART + 32, 128), LOW)]
         + [pltpu.SemaphoreType.DMA((ff // PART + 2,))],
         24 * rows_all * d * d, by_parts=(7, 8),
     )
     slots = Slots()
-    slots.start("ffn", sum_chain(sent, kept, dp_size))
+    slots.start("ffn", sum_chain(sent, kept, dp_size, True))
     work = [pltpu.VMEM((LMAX, d), LOW)] * 2 + [pltpu.VMEM((LMAX, d), F32)] * 4
     cuts = (0, 1, 3, count)
 
-    def inputs_of(first, end, w):
+    def inputs_of(first, end, w, grad_att):
         rows, probs = slice(first * LMAX, end * LMAX), slice(first * 2 * LMAX, end * 2 * LMAX)
-        args = ((slots.before(grad_att), rows), w) + tuple((a, rows) for a in (q, k, v, sk, sv))
+        args = ((grad_att, rows), w) + tuple((a, rows) for a in (q, k, v, sk, sv))
         return args + ((p, probs), plan)
+
+    def after(value, last):
+        return lax.optimization_barrier((value, *last))[0]
 
     grads = []
     for first, end in zip(cuts[:-2], cuts[1:-1]):
         out = call(
             functools.partial(backward_kernel, first, count), (lengths, ids),
-            inputs_of(first, end, (w_all, slice(3, 4))),
+            inputs_of(first, end, (w_all, slice(3, 4)), slots.before(grad_att)),
             [shaped(((end - first) * LMAX, d), LOW)] * 3 + [shaped((end - first, NB, NB), F32)],
             work, 4 << 30,
         )
         slots.after(out[-1])
         grads.append(out)
     first, late = cuts[-2], count - cuts[-2]
-    sent, kept, input_grad = call(
+    late_rows = shaped((late * LMAX, d), LOW)
+    sent, kept, *late_grads, gsum = call(
         functools.partial(last_kernel, cuts, count), (lengths, ids),
-        inputs_of(first, count, w_all)
+        inputs_of(first, count, w_all, after(grad_att, out[:1]))
         + (*(g for out in grads for g in out), normed_t, steps, pre, summary, sort_first, second_t)
-        + (gain1, vecs2, tokens, grad_middle),
-        [shaped((2, 4, 4, 136, 128), LOW)] * 2 + [low_rows],
-        work + [pltpu.VMEM((late * LMAX, d), LOW)] * 3 + [pltpu.VMEM((late, NB, NB), F32)]
-        + [pltpu.VMEM((count * NB, d), F32), pltpu.VMEM((16, d), F32), pltpu.VMEM((d, d), F32)],
+        + (gain1, bias1, vecs2),
+        [shaped((4, 4, 2, 136, 128), LOW)] * 2 + [late_rows] * 3 + [blocks],
+        work + [pltpu.VMEM((late, NB, NB), F32), pltpu.VMEM((16, d), F32)]
+        + [pltpu.VMEM((d, d), F32)] * 2,
         16 << 30,
     )
     slots.after(sent)
-    slots.start("last", sum_chain(sent, kept, dp_size))
-    last = [input_grad]
+    grads.append(late_grads)
+    seqs = [slice(s * LMAX, (s + 1) * LMAX) for s in range(count)]
+
+    last = slots.turn("ffn", [gsum])
+    slots.start("last", sum_chain(after(sent, last), kept, dp_size, LAST_HALVED))
     for name in TURNS:
-        last = slots.turn(name, last)
+        if name == "output":
+            output = call(
+                functools.partial(output_kernel, count), (),
+                (after(w_down, last), *((hidden, r) for r in seqs), *((middle, r) for r in seqs)),
+                [low_rows], [], 1 << 30,
+            )[0]
+            last = [output]
+        elif name == "input":
+            input_grad = call(
+                functools.partial(input_kernel, cuts, count), (lengths, ids),
+                (after(gsum, last), (w_all, slice(0, 3)), gain1)
+                + tuple(g for out in grads for g in out[:3])
+                + tuple((tokens, r) for r in seqs) + tuple((grad_middle, r) for r in seqs),
+                [low_rows], [], 1 << 30,
+            )[0]
+            last = [input_grad]
+        else:
+            last = slots.turn(name, last)
     while "ffn" in slots.running:
         last = slots.turn("ffn", last)
     up_sum, down_sum, o_sum = call(

time: 199 us -> 188 us (0.945)
  waiting for transfers between devices: 57.2 us -> 44.9 us
  Pallas kernels: 93.4 us -> 104 us
  local copies, waits for them, and re-layouts: 7.79 us -> 1.47 us
  starting transfers between devices: 30.7 us -> 27.3 us
    ppermute x30 -> x24, waiting for transfers between devices: 57.2 us -> 44.9 us  [swap(): return lax.ppermute(values, AXES, pairs)]
    pallas_call x8 -> x10, Pallas kernels: 93.4 us -> 104 us  [call(): pl.pallas_call(kernel, in_specs=[smem] * n_scalars + [pl.BlockSpec(memory...]
    slice x6 -> x0, local copies, waits for them, and re-layouts: 6.37 us -> none  [the longest x4 6.34 us: sum_chain(): sums = [[kept[c].reshape(shape), got[c].reshape(shape)] for c in range(2)]]
    ppermute x30 -> x24, starting transfers between devices: 30.7 us -> 27.3 us  [swap(): return lax.ppermute(values, AXES, pairs)]
    convert_element_type x17 -> x8, other arithmetic: 6.81 us -> 8.86 us  [low_sum(): return total.astype(LOW)]
  transfers between devices with their start and end apart: 30 -> 24, of which waited for: 19 -> 14; matrix products, arithmetic and copies ran while one was open for 5% -> 3% of each run, Pallas kernels for 17% -> 34%
where the time goes in v1:
time: 188 us
  Pallas kernels  104 us (55%)
  waiting for transfers between devices  44.9 us (24%)
  starting transfers between devices  27.3 us (15%)
  other arithmetic  9.41 us (5%)
    pallas_call x10, Pallas kernels, call(): pl.pallas_call(kernel, in_specs=[smem] * n_scalars + [pl.BlockSpec(memory...  104 us
    ppermute x24, waiting for transfers between devices, swap(): return lax.ppermute(values, AXES, pairs)  44.9 us
    ppermute x24, starting transfers between devices, swap(): return lax.ppermute(values, AXES, pairs)  27.3 us
    convert_element_type x8, other arithmetic, low_sum(): return total.astype(LOW)  8.86 us
  transfers between devices with their start and end apart: 24, of which 14 were waited for; matrix products, arithmetic and copies ran while one was open for 3% of the time, Pallas kernels for 34%

profile of v1, /device:TPU:0, one launch (start us, length us, event | category | flops | bytes accessed | tf_op | source)
XLA Modules:
  0.0 187.9 jit_solution(25453401500013233)
XLA Ops:
  1.4 2.7 %shard_map.254 = bf16[2048,128]{1,0:T(8,128)(2,1)} custom-call(s32[5]{0:T(128)} %stack.71.refs_0_.refs_1_, bf16[512,256]{1,0:T(8,128)(2,1)} %refs_2_.5, bf16[512,256]{1,0:T(8,128)(2,1)} %refs_3_.3, bf16[512,256]{1,0:T(8,128)(2,1)} %refs_4_.3, bf16[256,512]{1,0:T(8,128)(2,1)} %refs_5_.3), custom_call_target="tpu_custom_call" | custom-call | flops 17179869184 | bytes 16777216 | tf_op jit(solution)/shard_map/pallas_call | solution.py:852
  4.1 3.0 %collective-permute-start = (bf16[2048,128]{1,0:T(8,128)(2,1)}, bf16[2048,128]{1,0:T(8,128)(2,1)S(1)}, u32[]{:S(2)}, u32[]{:S(2)}) collective-permute-start(bf16[2048,128]{1,0:T(8,128)(2,1)} %shard_map.254), channel_id=1, source_target_pairs={{0,1},{1,0},{2,3},{3,2},{4,5},{5,4},{6,7},{7,6},{8,9},{9,8},{10,11... | collective-permute-start | bytes 1572872 | tf_op jit(solution)/shard_map/ppermute | solution.py:674
  7.1 11.6 %shard_map.255 = (bf16[1024,512]{1,0:T(8,128)(2,1)}, bf16[512,1024]{1,0:T(8,128)(2,1)}, f32[32,512]{1,0:T(8,128)}, f32[32,512]{1,0:T(8,128)}, f32[16,4,8,8]{3,2,...) custom-call(s32[8]{0:T(128)} %refs_0_.12, s32[5]{0:T(128)} %stack.71.refs_0_.refs_1_, ...), custom_call_target="tpu_custom_call" | custom-call | flops 17179869184 | bytes 16777216 | tf_op jit(solution)/shard_map/pallas_call | solution.py:852
  19.2 1.9 %collective-permute-done.1.refs_7_ = bf16[2048,128]{1,0:T(8,128)(2,1)S(1)} collective-permute-done((bf16[2048,128]{1,0:T(8,128)(2,1)S(1)}, bf16[2048,128]{1,0:T(8,128)(2,1)S(1)}, u32[]{:S(2)}, u32[]{:S(2)}) %collective-permute-start.1) | collective-permute-done | bytes 524320 | tf_op jit(solution)/shard_map/ppermute | solution.py:674
  21.9 34.4 %shard_map.256 = (bf16[1024,512]{1,0:T(8,128)(2,1)}, bf16[1024,512]{1,0:T(8,128)(2,1)}, bf16[1024,512]{1,0:T(8,128)(2,1)}, bf16[1024,512]{1,0:T(8,128)(2,1)}, bf...) custom-call(s32[8]{0:T(128)} %refs_0_.12, ...), custom_call_target="tpu_custom_call" | custom-call | flops 17179869184 | bytes 16777216 | tf_op jit(solution)/shard_map/pallas_call | solution.py:852
  56.5 6.2 %shard_map.257 = (bf16[256,512]{1,0:T(8,128)(2,1)}, bf16[256,512]{1,0:T(8,128)(2,1)}, bf16[256,512]{1,0:T(8,128)(2,1)}, f32[1,8,8]{2,1,0:T(8,128)}) custom-call(s32[8]{0:T(128)} %refs_0_.12, s32[5]{0:T(128)} %stack.71.refs_0_.refs_1_, bf16[1024,512]{1,0:T(8,128)(2,1)} %get-tuple-element.119.refs_2_, bf16[4,512,512]{2,1,0:T(8,128)(2,1)} %get-tuple-element.108.refs_3_, ...), custom_call_target="tpu_custom_call" | custom-call | flops 17179869184 | bytes 16777216 | tf_op jit(solution)/shard_map/pallas_call | solution.py:852
  62.8 1.9 %fusion.2 = (bf16[2,2,2,288,128]{4,3,2,1,0:T(8,128)(2,1)S(1)}, bf16[2,2,2,288,128]{4,3,2,1,0:T(8,128)(2,1)S(1)}, bf16[2,2,2,288,128]{4,3,2,1,0:T(8,128)(2,1)S(1)}) fusion(bf16[4,2,2,2,288,128]{5,4,3,2,1,0:T(8,128)(2,1)} %bitcast.11, s32[]{:T(128)S(6)} %select_n.125, bf16[4,2,2,2,288,128]{5,4,3,2,1,0:T(8,128)(2,1)S(1)} %bitcast.92, s32[]{:T(128)S(6)} %select_n.124, ...), kind=kLoop, calls=%fused_computation.7 | loop fusion | flops 3538944 | bytes 5308428 | tf_op jit(solution)/shard_map/convert_element_type | solution.py:695
  64.7 1.8 collective-permute-start.3
  66.5 1.5 collective-permute-start.4
  68.3 9.8 %shard_map.258 = (bf16[512,512]{1,0:T(8,128)(2,1)}, bf16[512,512]{1,0:T(8,128)(2,1)}, bf16[512,512]{1,0:T(8,128)(2,1)}, f32[2,8,8]{2,1,0:T(8,128)}) custom-call(s32[8]{0:T(128)} %refs_0_.12, s32[5]{0:T(128)} %stack.71.refs_0_.refs_1_, bf16[1024,512]{1,0:T(8,128)(2,1)} %get-tuple-element.119.refs_2_, bf16[4,512,512]{2,1,0:T(8,128)(2,1)} %get-tuple-element.108.refs_3_, ...), custom_call_target="tpu_custom_call" | custom-call | flops 17179869184 | bytes 16777216 | tf_op jit(solution)/shard_map/pallas_call | solution.py:852
  78.1 14.9 %shard_map.259 = (bf16[4,4,2,136,128]{4,3,2,1,0:T(8,128)(2,1)}, bf16[4,4,2,136,128]{4,3,2,1,0:T(8,128)(2,1)}, bf16[256,512]{1,0:T(8,128)(2,1)}, bf16[256,512]{1,...) custom-call(s32[8]{0:T(128)} %refs_0_.12, s32[5]{0:T(128)} %stack.71.refs_0_.refs_1_, ...), custom_call_target="tpu_custom_call" | custom-call | flops 17179869184 | bytes 16777216 | tf_op jit(solution)/shard_map/pallas_call | solution.py:852
  94.3 2.1 %fusion.3 = bf16[2,2,288,128]{3,2,1,0:T(8,128)(2,1)} fusion(bf16[2,2,2,288,128]{4,3,2,1,0:T(8,128)(2,1)S(1)} %collective-permute-done.5, s32[]{:T(128)S(6)} %select_n.126, bf16[2,2,2,288,128]{4,3,2,1,0:T(8,128)(2,1)S(1)} %collective-permute-done.4, bf16[2,2,2,288,128]{4,3,2,1,0:T(8,128)(2,1)S(1)} %collective-permute-done.3, ...), kind=kLoop, calls=%fused_computation.10 | loop fusion | flops 1474560 | bytes 1769484 | tf_op jit(solution)/shard_map/convert_element_type | solution.py:695
  96.3 1.8 collective-permute-start.6
  100.8 1.7 collective-permute-start.10
  102.5 1.5 collective-permute-start.11
  104.3 1.7 collective-permute-done.6
  107.2 2.8 %collective-permute-start.8 = (bf16[2,288,128]{2,1,0:T(8,128)(2,1)S(1)}, bf16[2,288,128]{2,1,0:T(8,128)(2,1)S(1)}, u32[]{:S(2)}, u32[]{:S(2)}) collective-permute-start(bf16[2,288,128]{2,1,0:T(8,128)(2,1)S(1)} %fusion.9), channel_id=1, source_target_pairs={{0,16},{1,17},{2,18},{3,19},{4,20},{5,21},{6,22},{7,23},{8,24},{9,... | collective-permute-start | bytes 442376 | tf_op jit(solution)/shard_map/ppermute | solution.py:674
  110.0 6.8 %shard_map.260 = bf16[1024,512]{1,0:T(8,128)(2,1)} custom-call(bf16[2048,512]{1,0:T(8,128)(2,1)} %refs_0_.11, bf16[1024,2048]{1,0:T(8,128)(2,1)} %get-tuple-element.147.refs_1_.refs_2_.refs_3_.refs_4_, bf16[1024,2048]{1,0:T(8,128)(2,1)} %get-tuple-element.147.refs_1_.refs_2_.refs_3_.refs_4_, ...), custom_call_target="tpu_custom_call" | custom-call | flops 17179869184 | bytes 16777216 | tf_op jit(solution)/shard_map/pallas_call | solution.py:852
  119.2 1.6 collective-permute-start.12
  122.0 2.7 %collective-permute-start.14 = (bf16[2,288,128]{2,1,0:T(8,128)(2,1)S(1)}, bf16[2,288,128]{2,1,0:T(8,128)(2,1)S(1)}, u32[]{:S(2)}, u32[]{:S(2)}) collective-permute-start(bf16[2,288,128]{2,1,0:T(8,128)(2,1)S(1)} %fusion.8), channel_id=1, source_target_pairs={{0,16},{1,17},{2,18},{3,19},{4,20},{5,21},{6,22},{7,23},{8,24},{9,... | collective-permute-start | bytes 442376 | tf_op jit(solution)/shard_map/ppermute | solution.py:674
  124.7 8.1 %shard_map.261 = bf16[1024,512]{1,0:T(8,128)(2,1)} custom-call(s32[8]{0:T(128)} %refs_0_.12, s32[5]{0:T(128)} %stack.71.refs_0_.refs_1_, f32[32,512]{1,0:T(8,128)} %get-tuple-element.153.refs_2_, bf16[4,512,512]{2,1,0:T(8,128)(2,1)} %get-tuple-element.108.refs_3_, f32[1,512]{1,0:T(1,128)} %bitcast.116, bf16[256,512]{1,0:T(8,128)(2,1)} %get-tuple-element.120.refs_11_.refs_5_, ...), custom_call_target="tpu_custom_call" | custom-call | flops 17179869184 | bytes 16777216 | tf_op jit(solution)/shard_map/pallas_call | solution.py:852
  133.5 6.3 %collective-permute-done.15 = bf16[2,2,288,128]{3,2,1,0:T(8,128)(2,1)S(1)} collective-permute-done((bf16[2,2,288,128]{3,2,1,0:T(8,128)(2,1)S(1)}, bf16[2,2,288,128]{3,2,1,0:T(8,128)(2,1)S(1)}, u32[]{:S(2)}, u32[]{:S(2)}) %collective-permute-start.15) | collective-permute-done | bytes 294944 | tf_op jit(solution)/shard_map/ppermute | solution.py:674
  140.4 1.5 collective-permute-start.20
  141.9 1.5 collective-permute-start.21
  143.7 10.3 %collective-permute-done.13 = bf16[2,2,2,136,128]{4,3,2,1,0:T(8,128)(2,1)S(1)} collective-permute-done((bf16[2,2,2,136,128]{4,3,2,1,0:T(8,128)(2,1)S(1)}, bf16[2,2,2,136,128]{4,3,2,1,0:T(8,128)(2,1)S(1)}, u32[]{:S(2)}, u32[]{:S(2)}) %collective-permute-start.13) | collective-permute-done | bytes 278560 | tf_op jit(solution)/shard_map/ppermute | solution.py:674
  156.7 8.5 %collective-permute-done.21 = bf16[2,2,2,288,128]{4,3,2,1,0:T(8,128)(2,1)S(1)} collective-permute-done((bf16[2,2,2,288,128]{4,3,2,1,0:T(8,128)(2,1)S(1)}, bf16[2,2,2,288,128]{4,3,2,1,0:T(8,128)(2,1)S(1)}, u32[]{:S(2)}, u32[]{:S(2)}) %collective-permute-start.21) | collective-permute-done | bytes 589856 | tf_op jit(solution)/shard_map/ppermute | solution.py:674
  166.1 1.5 collective-permute-start.17
  167.6 1.5 collective-permute-start.18
  170.0 6.1 %shard_map.262 = (f32[512,2048]{1,0:T(8,128)}, f32[2048,512]{1,0:T(8,128)}, f32[256,512]{1,0:T(8,128)}) custom-call(s32[5]{0:T(128)S(1)} %copy-done, bf16[4,2,2,2,288,128]{5,4,3,2,1,0:T(8,128)(2,1)S(1)} %pad_maximum_fusion.refs_1_, bf16[4,2,2,2,288,128]{5,4,3,2,1,0:T(8,128)(2,1)S(1)} %collective-permute-done.22.refs_2_), custom_call_target="tpu_custom_call" | custom-call | flops 17179869184 | bytes 16777216 | tf_op jit(solution)/shard_map/pallas_call | solution.py:852
  176.1 5.6 %collective-permute-done.18 = bf16[2,2,2,136,128]{4,3,2,1,0:T(8,128)(2,1)S(1)} collective-permute-done((bf16[2,2,2,136,128]{4,3,2,1,0:T(8,128)(2,1)S(1)}, bf16[2,2,2,136,128]{4,3,2,1,0:T(8,128)(2,1)S(1)}, u32[]{:S(2)}, u32[]{:S(2)}) %collective-permute-start.18) | collective-permute-done | bytes 278560 | tf_op jit(solution)/shard_map/ppermute | solution.py:674
  182.0 2.7 %collective-permute-done.23.refs_2_ = bf16[4,2,2,2,136,128]{5,4,3,2,1,0:T(8,128)(2,1)S(1)} collective-permute-done((bf16[4,2,2,2,136,128]{5,4,3,2,1,0:T(8,128)(2,1)S(1)}, bf16[4,2,2,2,136,128]{5,4,3,2,1,0:T(8,128)(2,1)S(1)}, u32[]{:S(2)}, u32[]{:S(2)}) %collective-permute-start.23) | collective-permute-done | bytes 1114144 | tf_op jit(solution)/shard_map/ppermute | solution.py:674
  184.7 3.0 %shard_map.263 = (f32[512,256]{1,0:T(8,128)}, f32[512,256]{1,0:T(8,128)}, f32[512,256]{1,0:T(8,128)}, f32[512,512]{1,0:T(8,128)}, f32[8,512]{1,0:T(8,128)}, /*in...) custom-call(s32[5]{0:T(128)S(1)} %copy-done, ...), custom_call_target="tpu_custom_call" | custom-call | flops 17179869184 | bytes 16777216 | tf_op jit(solution)/shard_map/pallas_call | solution.py:852
  (61 shorter events, 17.6 us)
Async XLA Ops:
  4.1 15.2 %collective-permute-start = (bf16[2048,128]{1,0:T(8,128)(2,1)}, bf16[2048,128]{1,0:T(8,128)(2,1)S(1)}, u32[]{:S(2)}, u32[]{:S(2)}) collective-permute-start(bf16[2048,128]{1,0:T(8,128)(2,1)} %shard_map.254), channel_id=1, source_target_pairs={{0,1},{1,0},{2,3},{3,2},{4,5},{5,4},{6,7},{7,6},{8,9},{9,8},{10,11... | collective-permute-start | bytes 1572872 | tf_op jit(solution)/shard_map/ppermute | solution.py:674
  19.2 1.9 %collective-permute-start.1 = (bf16[2048,128]{1,0:T(8,128)(2,1)S(1)}, bf16[2048,128]{1,0:T(8,128)(2,1)S(1)}, u32[]{:S(2)}, u32[]{:S(2)}) collective-permute-start(bf16[2048,128]{1,0:T(8,128)(2,1)S(1)} %collective-permute-done.refs_6_), channel_id=1, source_target_pairs={{0,2},{1,3},{2,0},{3,1},{4,6},{5,7},{6,4},{7,5},{8,10},{9,11},{10,... | collective-permute-start | bytes 1572872 | tf_op jit(solution)/shard_map/ppermute | solution.py:674
  56.3 6.4 %collective-permute-start.2 = (bf16[4,4,2,288,128]{4,3,2,1,0:T(8,128)(2,1)}, bf16[4,4,2,288,128]{4,3,2,1,0:T(8,128)(2,1)}, u32[]{:S(2)}, u32[]{:S(2)}) collective-permute-start(bf16[4,4,2,288,128]{4,3,2,1,0:T(8,128)(2,1)} %get-tuple-element.106), channel_id=1, source_target_pairs={{0,2},{1,3},{2,0},{3,1},{4,6},{5,7},{6,4},{7,5},{8,10},{9,11},{10,... | collective-permute-start | bytes 7077896 | tf_op jit(solution)/shard_map/ppermute | solution.py:674
  56.5 6.3 %copy-start.1 = (bf16[4,4,2,288,128]{4,3,2,1,0:T(8,128)(2,1)S(1)}, bf16[4,4,2,288,128]{4,3,2,1,0:T(8,128)(2,1)}, u32[]{:S(2)}) copy-start(bf16[4,4,2,288,128]{4,3,2,1,0:T(8,128)(2,1)} %get-tuple-element.104) | copy-start | bytes 7077892
  64.7 28.3 %collective-permute-start.3 = (bf16[2,2,2,288,128]{4,3,2,1,0:T(8,128)(2,1)S(1)}, bf16[2,2,2,288,128]{4,3,2,1,0:T(8,128)(2,1)S(1)}, u32[]{:S(2)}, u32[]{:S(2)}) collective-permute-start(bf16[2,2,2,288,128]{4,3,2,1,0:T(8,128)(2,1)S(1)} %get-tuple-element.184), channel_id=1, source_target_pairs={{0,1},{1,0},{2,3},{3,2},{4,5},{5,4},{6,7},{7,6},{8,9},{9,8},{10,11... | collective-permute-start | bytes 1769480 | tf_op jit(solution)/shard_map/ppermute | solution.py:674
  66.5 26.5 %collective-permute-start.4 = (bf16[2,2,2,288,128]{4,3,2,1,0:T(8,128)(2,1)S(1)}, bf16[2,2,2,288,128]{4,3,2,1,0:T(8,128)(2,1)S(1)}, u32[]{:S(2)}, u32[]{:S(2)}) collective-permute-start(bf16[2,2,2,288,128]{4,3,2,1,0:T(8,128)(2,1)S(1)} %get-tuple-element.183), channel_id=1, source_target_pairs={{0,4},{1,5},{2,6},{3,7},{4,0},{5,1},{6,2},{7,3},{8,12},{9,13},{10,... | collective-permute-start | bytes 1769480 | tf_op jit(solution)/shard_map/ppermute | solution.py:674
  68.0 26.3 %collective-permute-start.5 = (bf16[2,2,2,288,128]{4,3,2,1,0:T(8,128)(2,1)S(1)}, bf16[2,2,2,288,128]{4,3,2,1,0:T(8,128)(2,1)S(1)}, u32[]{:S(2)}, u32[]{:S(2)}) collective-permute-start(bf16[2,2,2,288,128]{4,3,2,1,0:T(8,128)(2,1)S(1)} %get-tuple-element.182), channel_id=1, source_target_pairs={{0,5},{1,4},{2,7},{3,6},{4,1},{5,0},{6,3},{7,2},{8,13},{9,12},{10,... | collective-permute-start | bytes 1769480 | tf_op jit(solution)/shard_map/ppermute | solution.py:674
  93.0 6.4 %copy-start.2 = (bf16[4,4,2,136,128]{4,3,2,1,0:T(8,128)(2,1)S(1)}, bf16[4,4,2,136,128]{4,3,2,1,0:T(8,128)(2,1)}, u32[]{:S(2)}) copy-start(bf16[4,4,2,136,128]{4,3,2,1,0:T(8,128)(2,1)} %get-tuple-element.142) | copy-start | bytes 3342340
  93.1 3.3 %copy-start.5 = (bf16[2,2,2,288,128]{4,3,2,1,0:T(8,128)(2,1)}, bf16[2,2,2,288,128]{4,3,2,1,0:T(8,128)(2,1)S(1)}, u32[]{:S(2)}) copy-start(bf16[2,2,2,288,128]{4,3,2,1,0:T(8,128)(2,1)S(1)} %collective-permute-done.4) | copy-start | bytes 1769476
  94.3 2.1 %copy-start.7 = (bf16[2,2,2,288,128]{4,3,2,1,0:T(8,128)(2,1)}, bf16[2,2,2,288,128]{4,3,2,1,0:T(8,128)(2,1)S(1)}, u32[]{:S(2)}) copy-start(bf16[2,2,2,288,128]{4,3,2,1,0:T(8,128)(2,1)S(1)} %collective-permute-done.5) | copy-start | bytes 1769476
  96.3 3.1 %collective-permute-start.7 = (bf16[4,4,2,136,128]{4,3,2,1,0:T(8,128)(2,1)}, bf16[4,4,2,136,128]{4,3,2,1,0:T(8,128)(2,1)}, u32[]{:S(2)}, u32[]{:S(2)}) collective-permute-start(bf16[4,4,2,136,128]{4,3,2,1,0:T(8,128)(2,1)} %get-tuple-element.143), channel_id=1, source_target_pairs={{0,2},{1,3},{2,0},{3,1},{4,6},{5,7},{6,4},{7,5},{8,10},{9,11},{10,... | collective-permute-start | bytes 3342344 | tf_op jit(solution)/shard_map/ppermute | solution.py:674
  96.3 9.7 %collective-permute-start.6 = (bf16[2,2,288,128]{3,2,1,0:T(8,128)(2,1)}, bf16[2,2,288,128]{3,2,1,0:T(8,128)(2,1)}, u32[]{:S(2)}, u32[]{:S(2)}) collective-permute-start(bf16[2,2,288,128]{3,2,1,0:T(8,128)(2,1)} %fusion.3), channel_id=1, source_target_pairs={{0,8},{1,9},{2,10},{3,11},{4,12},{5,13},{6,14},{7,15},{8,0},{9,1},... | collective-permute-start | bytes 884744 | tf_op jit(solution)/shard_map/ppermute | solution.py:674
  98.1 7.9 %copy-start.4 = (bf16[2,2,2,288,128]{4,3,2,1,0:T(8,128)(2,1)S(1)}, bf16[2,2,2,288,128]{4,3,2,1,0:T(8,128)(2,1)}, u32[]{:S(2)}) copy-start(bf16[2,2,2,288,128]{4,3,2,1,0:T(8,128)(2,1)} %copy-done.3) | copy-start | bytes 1769476
  98.1 7.9 %copy-start.6 = (bf16[2,2,2,288,128]{4,3,2,1,0:T(8,128)(2,1)S(1)}, bf16[2,2,2,288,128]{4,3,2,1,0:T(8,128)(2,1)}, u32[]{:S(2)}) copy-start(bf16[2,2,2,288,128]{4,3,2,1,0:T(8,128)(2,1)} %copy-done.5) | copy-start | bytes 1769476
  98.1 7.9 %copy-start.8 = (bf16[2,2,2,288,128]{4,3,2,1,0:T(8,128)(2,1)S(1)}, bf16[2,2,2,288,128]{4,3,2,1,0:T(8,128)(2,1)}, u32[]{:S(2)}) copy-start(bf16[2,2,2,288,128]{4,3,2,1,0:T(8,128)(2,1)} %copy-done.7) | copy-start | bytes 1769476
  100.8 16.0 %collective-permute-start.10 = (bf16[2,2,2,136,128]{4,3,2,1,0:T(8,128)(2,1)S(1)}, bf16[2,2,2,136,128]{4,3,2,1,0:T(8,128)(2,1)S(1)}, u32[]{:S(2)}, u32[]{:S(2)}) collective-permute-start(bf16[2,2,2,136,128]{4,3,2,1,0:T(8,128)(2,1)S(1)} %get-tuple-element.186), channel_id=1, source_target_pairs={{0,4},{1,5},{2,6},{3,7},{4,0},{5,1},{6,2},{7,3},{8,12},{9,13},{10,... | collective-permute-start | bytes 835592 | tf_op jit(solution)/shard_map/ppermute | solution.py:674
  102.5 14.4 %collective-permute-start.11 = (bf16[2,2,2,136,128]{4,3,2,1,0:T(8,128)(2,1)S(1)}, bf16[2,2,2,136,128]{4,3,2,1,0:T(8,128)(2,1)S(1)}, u32[]{:S(2)}, u32[]{:S(2)}) collective-permute-start(bf16[2,2,2,136,128]{4,3,2,1,0:T(8,128)(2,1)S(1)} %get-tuple-element.185), channel_id=1, source_target_pairs={{0,5},{1,4},{2,7},{3,6},{4,1},{5,0},{6,3},{7,2},{8,13},{9,12},{10,... | collective-permute-start | bytes 835592 | tf_op jit(solution)/shard_map/ppermute | solution.py:674
  104.0 14.1 %collective-permute-start.9 = (bf16[2,2,2,136,128]{4,3,2,1,0:T(8,128)(2,1)S(1)}, bf16[2,2,2,136,128]{4,3,2,1,0:T(8,128)(2,1)S(1)}, u32[]{:S(2)}, u32[]{:S(2)}) collective-permute-start(bf16[2,2,2,136,128]{4,3,2,1,0:T(8,128)(2,1)S(1)} %get-tuple-element.187), channel_id=1, source_target_pairs={{0,1},{1,0},{2,3},{3,2},{4,5},{5,4},{6,7},{7,6},{8,9},{9,8},{10,11... | collective-permute-start | bytes 835592 | tf_op jit(solution)/shard_map/ppermute | solution.py:674
  107.2 13.7 %collective-permute-start.8 = (bf16[2,288,128]{2,1,0:T(8,128)(2,1)S(1)}, bf16[2,288,128]{2,1,0:T(8,128)(2,1)S(1)}, u32[]{:S(2)}, u32[]{:S(2)}) collective-permute-start(bf16[2,288,128]{2,1,0:T(8,128)(2,1)S(1)} %fusion.9), channel_id=1, source_target_pairs={{0,16},{1,17},{2,18},{3,19},{4,20},{5,21},{6,22},{7,23},{8,24},{9,... | collective-permute-start | bytes 442376 | tf_op jit(solution)/shard_map/ppermute | solution.py:674
  119.2 13.6 %collective-permute-start.12 = (bf16[2,2,2,136,128]{4,3,2,1,0:T(8,128)(2,1)S(1)}, bf16[2,2,2,136,128]{4,3,2,1,0:T(8,128)(2,1)S(1)}, u32[]{:S(2)}, u32[]{:S(2)}) collective-permute-start(bf16[2,2,2,136,128]{4,3,2,1,0:T(8,128)(2,1)S(1)} %fusion.6), channel_id=1, source_target_pairs={{0,8},{1,9},{2,10},{3,11},{4,12},{5,13},{6,14},{7,15},{8,0},{9,1},... | collective-permute-start | bytes 835592 | tf_op jit(solution)/shard_map/ppermute | solution.py:674
  122.0 10.9 %collective-permute-start.14 = (bf16[2,288,128]{2,1,0:T(8,128)(2,1)S(1)}, bf16[2,288,128]{2,1,0:T(8,128)(2,1)S(1)}, u32[]{:S(2)}, u32[]{:S(2)}) collective-permute-start(bf16[2,288,128]{2,1,0:T(8,128)(2,1)S(1)} %fusion.8), channel_id=1, source_target_pairs={{0,16},{1,17},{2,18},{3,19},{4,20},{5,21},{6,22},{7,23},{8,24},{9,... | collective-permute-start | bytes 442376 | tf_op jit(solution)/shard_map/ppermute | solution.py:674
  133.0 6.8 %collective-permute-start.15 = (bf16[2,2,288,128]{3,2,1,0:T(8,128)(2,1)S(1)}, bf16[2,2,288,128]{3,2,1,0:T(8,128)(2,1)S(1)}, u32[]{:S(2)}, u32[]{:S(2)}) collective-permute-start(bf16[2,2,288,128]{3,2,1,0:T(8,128)(2,1)S(1)} %get-tuple-element.191), channel_id=1, source_target_pairs={{0,8},{1,9},{2,10},{3,11},{4,12},{5,13},{6,14},{7,15},{8,0},{9,1},... | collective-permute-start | bytes 884744 | tf_op jit(solution)/shard_map/ppermute | solution.py:674
  139.8 15.4 %collective-permute-start.19 = (bf16[2,2,2,288,128]{4,3,2,1,0:T(8,128)(2,1)S(1)}, bf16[2,2,2,288,128]{4,3,2,1,0:T(8,128)(2,1)S(1)}, u32[]{:S(2)}, u32[]{:S(2)}) collective-permute-start(bf16[2,2,2,288,128]{4,3,2,1,0:T(8,128)(2,1)S(1)} %get-tuple-element.189), channel_id=1, source_target_pairs={{0,1},{1,0},{2,3},{3,2},{4,5},{5,4},{6,7},{7,6},{8,9},{9,8},{10,11... | collective-permute-start | bytes 1769480 | tf_op jit(solution)/shard_map/ppermute | solution.py:674
  140.4 16.3 %collective-permute-start.20 = (bf16[2,2,2,288,128]{4,3,2,1,0:T(8,128)(2,1)S(1)}, bf16[2,2,2,288,128]{4,3,2,1,0:T(8,128)(2,1)S(1)}, u32[]{:S(2)}, u32[]{:S(2)}) collective-permute-start(bf16[2,2,2,288,128]{4,3,2,1,0:T(8,128)(2,1)S(1)} %get-tuple-element.189), channel_id=1, source_target_pairs={{0,4},{1,5},{2,6},{3,7},{4,0},{5,1},{6,2},{7,3},{8,12},{9,13},{10,... | collective-permute-start | bytes 1769480 | tf_op jit(solution)/shard_map/ppermute | solution.py:674
  141.9 23.2 %collective-permute-start.21 = (bf16[2,2,2,288,128]{4,3,2,1,0:T(8,128)(2,1)S(1)}, bf16[2,2,2,288,128]{4,3,2,1,0:T(8,128)(2,1)S(1)}, u32[]{:S(2)}, u32[]{:S(2)}) collective-permute-start(bf16[2,2,2,288,128]{4,3,2,1,0:T(8,128)(2,1)S(1)} %get-tuple-element.189), channel_id=1, source_target_pairs={{0,5},{1,4},{2,7},{3,6},{4,1},{5,0},{6,3},{7,2},{8,13},{9,12},{10,... | collective-permute-start | bytes 1769480 | tf_op jit(solution)/shard_map/ppermute | solution.py:674
  143.4 10.7 %collective-permute-start.13 = (bf16[2,2,2,136,128]{4,3,2,1,0:T(8,128)(2,1)S(1)}, bf16[2,2,2,136,128]{4,3,2,1,0:T(8,128)(2,1)S(1)}, u32[]{:S(2)}, u32[]{:S(2)}) collective-permute-start(bf16[2,2,2,136,128]{4,3,2,1,0:T(8,128)(2,1)S(1)} %add_convert_fusion.4), channel_id=1, source_target_pairs={{0,16},{1,17},{2,18},{3,19},{4,20},{5,21},{6,22},{7,23},{8,24},{9,... | collective-permute-start | bytes 835592 | tf_op jit(solution)/shard_map/ppermute | solution.py:674
  165.1 4.9 %copy-start = (s32[5]{0:T(128)S(1)}, s32[5]{0:T(128)}, u32[]{:S(2)}) copy-start(s32[5]{0:T(128)} %stack.71.refs_0_.refs_1_) | copy-start | bytes 64
  165.4 4.6 %collective-permute-start.22 = (bf16[4,2,2,2,288,128]{5,4,3,2,1,0:T(8,128)(2,1)S(1)}, bf16[4,2,2,2,288,128]{5,4,3,2,1,0:T(8,128)(2,1)S(1)}, u32[]{:S(2)}, u32[]{:S(2)}) collective-permute-start(bf16[4,2,2,2,288,128]{5,4,3,2,1,0:T(8,128)(2,1)S(1)} %pad_maximum_fusion.refs_1_), channel_id=1, source_target_pairs={{0,2},{1,3},{2,0},{3,1},{4,6},{5,7},{6,4},{7,5},{8,10},{9,11},{10,... | collective-permute-start | bytes 7077896 | tf_op jit(solution)/shard_map/ppermute | solution.py:674
  165.5 10.6 %collective-permute-start.16 = (bf16[2,2,2,136,128]{4,3,2,1,0:T(8,128)(2,1)S(1)}, bf16[2,2,2,136,128]{4,3,2,1,0:T(8,128)(2,1)S(1)}, u32[]{:S(2)}, u32[]{:S(2)}) collective-permute-start(bf16[2,2,2,136,128]{4,3,2,1,0:T(8,128)(2,1)S(1)} %add_convert_fusion.3), channel_id=1, source_target_pairs={{0,1},{1,0},{2,3},{3,2},{4,5},{5,4},{6,7},{7,6},{8,9},{9,8},{10,11... | collective-permute-start | bytes 835592 | tf_op jit(solution)/shard_map/ppermute | solution.py:674
  166.1 10.0 %collective-permute-start.17 = (bf16[2,2,2,136,128]{4,3,2,1,0:T(8,128)(2,1)S(1)}, bf16[2,2,2,136,128]{4,3,2,1,0:T(8,128)(2,1)S(1)}, u32[]{:S(2)}, u32[]{:S(2)}) collective-permute-start(bf16[2,2,2,136,128]{4,3,2,1,0:T(8,128)(2,1)S(1)} %add_convert_fusion.3), channel_id=1, source_target_pairs={{0,4},{1,5},{2,6},{3,7},{4,0},{5,1},{6,2},{7,3},{8,12},{9,13},{10,... | collective-permute-start | bytes 835592 | tf_op jit(solution)/shard_map/ppermute | solution.py:674
  167.6 14.2 %collective-permute-start.18 = (bf16[2,2,2,136,128]{4,3,2,1,0:T(8,128)(2,1)S(1)}, bf16[2,2,2,136,128]{4,3,2,1,0:T(8,128)(2,1)S(1)}, u32[]{:S(2)}, u32[]{:S(2)}) collective-permute-start(bf16[2,2,2,136,128]{4,3,2,1,0:T(8,128)(2,1)S(1)} %add_convert_fusion.3), channel_id=1, source_target_pairs={{0,5},{1,4},{2,7},{3,6},{4,1},{5,0},{6,3},{7,2},{8,13},{9,12},{10,... | collective-permute-start | bytes 835592 | tf_op jit(solution)/shard_map/ppermute | solution.py:674
  181.9 2.8 %collective-permute-start.23 = (bf16[4,2,2,2,136,128]{5,4,3,2,1,0:T(8,128)(2,1)S(1)}, bf16[4,2,2,2,136,128]{5,4,3,2,1,0:T(8,128)(2,1)S(1)}, u32[]{:S(2)}, u32[]{:S(2)}) collective-permute-start(bf16[4,2,2,2,136,128]{5,4,3,2,1,0:T(8,128)(2,1)S(1)} %pad_maximum_fusion.1.refs_1_), channel_id=1, source_target_pairs={{0,2},{1,3},{2,0},{3,1},{4,6},{5,7},{6,4},{7,5},{8,10},{9,11},{10,... | collective-permute-start | bytes 3342344 | tf_op jit(solution)/shard_map/ppermute | solution.py:674
  (3 other events, 4.0 us)

commit v2 on v1

--- a/solution.py
+++ b/solution.py
@@ -17,7 +17,7 @@
 LOW = jnp.bfloat16
 AXES = ("dp", "head")
 VMEM_LIMIT = 56 * 1024 * 1024
-TURNS = ["last", "last", "ffn", "output", "last", "ffn", "input", "last", "ffn", "ffn", "last"]
+TURNS = ["last", "last", "ffn", "output", "last", "ffn", "input", "ffn", "ffn", "last", "last"]
 LAST_HALVED = False
 
 ERF_P = 0.3875
@@ -928,7 +928,7 @@
     slots = Slots()
     slots.start("ffn", sum_chain(sent, kept, dp_size, True))
     work = [pltpu.VMEM((LMAX, d), LOW)] * 2 + [pltpu.VMEM((LMAX, d), F32)] * 4
-    cuts = (0, 1, 3, count)
+    cuts = (0, 1, count)
 
     def inputs_of(first, end, w, grad_att):
         rows, probs = slice(first * LMAX, end * LMAX), slice(first * 2 * LMAX, end * 2 * LMAX)
@@ -952,7 +952,7 @@
     late_rows = shaped((late * LMAX, d), LOW)
     sent, kept, *late_grads, gsum = call(
         functools.partial(last_kernel, cuts, count), (lengths, ids),
-        inputs_of(first, count, w_all, after(grad_att, out[:1]))
+        inputs_of(first, count, w_all, slots.before(grad_att))
         + (*(g for out in grads for g in out), normed_t, steps, pre, summary, sort_first, second_t)
         + (gain1, bias1, vecs2),
         [shaped((4, 4, 2, 136, 128), LOW)] * 2 + [late_rows] * 3 + [blocks],

time: 188 us -> 187 us (level)
  Pallas kernels: 104 us -> 101 us
    pallas_call x10 -> x9, Pallas kernels: 104 us -> 101 us  [call(): pl.pallas_call(kernel, in_specs=[smem] * n_scalars + [pl.BlockSpec(memory...]
  transfers between devices with their start and end apart: 24 -> 24, of which waited for: 14 -> 15; matrix products, arithmetic and copies ran while one was open for 3% -> 2% of each run, Pallas kernels for 34% -> 33%
where the time goes in v2:
time: 187 us; the launch traced here: 186 us
  Pallas kernels  101 us (54%)
  waiting for transfers between devices  46 us (25%)
  starting transfers between devices  27.6 us (15%)
  other arithmetic  9.42 us (5%)
    pallas_call x9, Pallas kernels, call(): pl.pallas_call(kernel, in_specs=[smem] * n_scalars + [pl.BlockSpec(memory...  101 us
    ppermute x24, waiting for transfers between devices, swap(): return lax.ppermute(values, AXES, pairs)  46 us
    ppermute x24, starting transfers between devices, swap(): return lax.ppermute(values, AXES, pairs)  27.6 us
    convert_element_type x8, other arithmetic, low_sum(): return total.astype(LOW)  8.86 us
  transfers between devices with their start and end apart: 24, of which 15 were waited for; matrix products, arithmetic and copies ran while one was open for 2% of the time, Pallas kernels for 33%

profile of v2, /device:TPU:0, one launch (start us, length us, event | category | flops | bytes accessed | tf_op | source)
XLA Modules:
  0.0 186.4 jit_solution(4178674992999780476)
XLA Ops:
  1.4 2.7 %shard_map.254 = bf16[2048,128]{1,0:T(8,128)(2,1)} custom-call(s32[5]{0:T(128)} %stack.71.refs_0_.refs_1_, bf16[512,256]{1,0:T(8,128)(2,1)} %refs_2_.5, bf16[512,256]{1,0:T(8,128)(2,1)} %refs_3_.3, bf16[512,256]{1,0:T(8,128)(2,1)} %refs_4_.3, bf16[256,512]{1,0:T(8,128)(2,1)} %refs_5_.3), custom_call_target="tpu_custom_call" | custom-call | flops 17179869184 | bytes 16777216 | tf_op jit(solution)/shard_map/pallas_call | solution.py:852
  4.1 3.0 %collective-permute-start = (bf16[2048,128]{1,0:T(8,128)(2,1)}, bf16[2048,128]{1,0:T(8,128)(2,1)S(1)}, u32[]{:S(2)}, u32[]{:S(2)}) collective-permute-start(bf16[2048,128]{1,0:T(8,128)(2,1)} %shard_map.254), channel_id=1, source_target_pairs={{0,1},{1,0},{2,3},{3,2},{4,5},{5,4},{6,7},{7,6},{8,9},{9,8},{10,11... | collective-permute-start | bytes 1572872 | tf_op jit(solution)/shard_map/ppermute | solution.py:674
  7.1 11.6 %shard_map.255 = (bf16[1024,512]{1,0:T(8,128)(2,1)}, bf16[512,1024]{1,0:T(8,128)(2,1)}, f32[32,512]{1,0:T(8,128)}, f32[32,512]{1,0:T(8,128)}, f32[16,4,8,8]{3,2,...) custom-call(s32[8]{0:T(128)} %refs_0_.10, s32[5]{0:T(128)} %stack.71.refs_0_.refs_1_, ...), custom_call_target="tpu_custom_call" | custom-call | flops 17179869184 | bytes 16777216 | tf_op jit(solution)/shard_map/pallas_call | solution.py:852
  19.2 1.9 %collective-permute-done.1.refs_7_ = bf16[2048,128]{1,0:T(8,128)(2,1)S(1)} collective-permute-done((bf16[2048,128]{1,0:T(8,128)(2,1)S(1)}, bf16[2048,128]{1,0:T(8,128)(2,1)S(1)}, u32[]{:S(2)}, u32[]{:S(2)}) %collective-permute-start.1) | collective-permute-done | bytes 524320 | tf_op jit(solution)/shard_map/ppermute | solution.py:674
  21.9 34.4 %shard_map.256 = (bf16[1024,512]{1,0:T(8,128)(2,1)}, bf16[1024,512]{1,0:T(8,128)(2,1)}, bf16[1024,512]{1,0:T(8,128)(2,1)}, bf16[1024,512]{1,0:T(8,128)(2,1)}, bf...) custom-call(s32[8]{0:T(128)} %refs_0_.10, ...), custom_call_target="tpu_custom_call" | custom-call | flops 17179869184 | bytes 16777216 | tf_op jit(solution)/shard_map/pallas_call | solution.py:852
  56.5 6.2 %shard_map.257 = (bf16[256,512]{1,0:T(8,128)(2,1)}, bf16[256,512]{1,0:T(8,128)(2,1)}, bf16[256,512]{1,0:T(8,128)(2,1)}, f32[1,8,8]{2,1,0:T(8,128)}) custom-call(s32[8]{0:T(128)} %refs_0_.10, s32[5]{0:T(128)} %stack.71.refs_0_.refs_1_, bf16[1024,512]{1,0:T(8,128)(2,1)} %get-tuple-element.109.refs_2_, bf16[4,512,512]{2,1,0:T(8,128)(2,1)} %get-tuple-element.100.refs_3_, ...), custom_call_target="tpu_custom_call" | custom-call | flops 17179869184 | bytes 16777216 | tf_op jit(solution)/shard_map/pallas_call | solution.py:852
  62.7 1.9 %fusion.2 = (bf16[2,2,2,288,128]{4,3,2,1,0:T(8,128)(2,1)S(1)}, bf16[2,2,2,288,128]{4,3,2,1,0:T(8,128)(2,1)S(1)}, bf16[2,2,2,288,128]{4,3,2,1,0:T(8,128)(2,1)S(1)}) fusion(bf16[4,2,2,2,288,128]{5,4,3,2,1,0:T(8,128)(2,1)} %bitcast.11, s32[]{:T(128)S(6)} %select_n.125, bf16[4,2,2,2,288,128]{5,4,3,2,1,0:T(8,128)(2,1)S(1)} %bitcast.92, s32[]{:T(128)S(6)} %select_n.124, ...), kind=kLoop, calls=%fused_computation.7 | loop fusion | flops 3538944 | bytes 5308428 | tf_op jit(solution)/shard_map/convert_element_type | solution.py:695
  64.7 1.8 collective-permute-start.3
  66.5 1.5 collective-permute-start.4
  68.2 22.0 %shard_map.258 = (bf16[4,4,2,136,128]{4,3,2,1,0:T(8,128)(2,1)}, bf16[4,4,2,136,128]{4,3,2,1,0:T(8,128)(2,1)}, bf16[768,512]{1,0:T(8,128)(2,1)}, bf16[768,512]{1,...) custom-call(s32[8]{0:T(128)} %refs_0_.10, s32[5]{0:T(128)} %stack.71.refs_0_.refs_1_, ...), custom_call_target="tpu_custom_call" | custom-call | flops 17179869184 | bytes 16777216 | tf_op jit(solution)/shard_map/pallas_call | solution.py:852
  90.2 4.0 %collective-permute-done.5 = bf16[2,2,2,288,128]{4,3,2,1,0:T(8,128)(2,1)S(1)} collective-permute-done((bf16[2,2,2,288,128]{4,3,2,1,0:T(8,128)(2,1)S(1)}, bf16[2,2,2,288,128]{4,3,2,1,0:T(8,128)(2,1)S(1)}, u32[]{:S(2)}, u32[]{:S(2)}) %collective-permute-start.5) | collective-permute-done | bytes 589856 | tf_op jit(solution)/shard_map/ppermute | solution.py:674
  94.3 2.1 %fusion.3 = bf16[2,2,288,128]{3,2,1,0:T(8,128)(2,1)} fusion(bf16[2,2,2,288,128]{4,3,2,1,0:T(8,128)(2,1)S(1)} %collective-permute-done.5, s32[]{:T(128)S(6)} %select_n.126, bf16[2,2,2,288,128]{4,3,2,1,0:T(8,128)(2,1)S(1)} %collective-permute-done.4, bf16[2,2,2,288,128]{4,3,2,1,0:T(8,128)(2,1)S(1)} %collective-permute-done.3, ...), kind=kLoop, calls=%fused_computation.10 | loop fusion | flops 1474560 | bytes 1769484 | tf_op jit(solution)/shard_map/convert_element_type | solution.py:695
  96.3 1.8 collective-permute-start.6
  99.4 1.3 fusion.12
  100.8 1.7 collective-permute-start.10
  102.5 1.4 collective-permute-start.11
  104.3 1.7 collective-permute-done.6
  107.2 2.8 %collective-permute-start.8 = (bf16[2,288,128]{2,1,0:T(8,128)(2,1)S(1)}, bf16[2,288,128]{2,1,0:T(8,128)(2,1)S(1)}, u32[]{:S(2)}, u32[]{:S(2)}) collective-permute-start(bf16[2,288,128]{2,1,0:T(8,128)(2,1)S(1)} %fusion.9), channel_id=1, source_target_pairs={{0,16},{1,17},{2,18},{3,19},{4,20},{5,21},{6,22},{7,23},{8,24},{9,... | collective-permute-start | bytes 442376 | tf_op jit(solution)/shard_map/ppermute | solution.py:674
  110.0 6.8 %shard_map.259 = bf16[1024,512]{1,0:T(8,128)(2,1)} custom-call(bf16[2048,512]{1,0:T(8,128)(2,1)} %refs_0_.9, bf16[1024,2048]{1,0:T(8,128)(2,1)} %get-tuple-element.131.refs_1_.refs_2_.refs_3_.refs_4_, bf16[1024,2048]{1,0:T(8,128)(2,1)} %get-tuple-element.131.refs_1_.refs_2_.refs_3_.refs_4_, ...), custom_call_target="tpu_custom_call" | custom-call | flops 17179869184 | bytes 16777216 | tf_op jit(solution)/shard_map/pallas_call | solution.py:852
  120.4 2.7 %collective-permute-start.13 = (bf16[2,288,128]{2,1,0:T(8,128)(2,1)S(1)}, bf16[2,288,128]{2,1,0:T(8,128)(2,1)S(1)}, u32[]{:S(2)}, u32[]{:S(2)}) collective-permute-start(bf16[2,288,128]{2,1,0:T(8,128)(2,1)S(1)} %fusion.8), channel_id=1, source_target_pairs={{0,16},{1,17},{2,18},{3,19},{4,20},{5,21},{6,22},{7,23},{8,24},{9,... | collective-permute-start | bytes 442376 | tf_op jit(solution)/shard_map/ppermute | solution.py:674
  123.0 8.1 %shard_map.260 = bf16[1024,512]{1,0:T(8,128)(2,1)} custom-call(s32[8]{0:T(128)} %refs_0_.10, s32[5]{0:T(128)} %stack.71.refs_0_.refs_1_, f32[32,512]{1,0:T(8,128)} %get-tuple-element.137.refs_2_, bf16[4,512,512]{2,1,0:T(8,128)(2,1)} %get-tuple-element.100.refs_3_, f32[1,512]{1,0:T(1,128)} %bitcast.116, bf16[256,512]{1,0:T(8,128)(2,1)} %get-tuple-element.110.refs_11_.refs_5_, ...), custom_call_target="tpu_custom_call" | custom-call | flops 17179869184 | bytes 16777216 | tf_op jit(solution)/shard_map/pallas_call | solution.py:852
  131.2 1.7 collective-permute-start.14
  133.3 7.5 %collective-permute-done.14 = bf16[2,2,288,128]{3,2,1,0:T(8,128)(2,1)S(1)} collective-permute-done((bf16[2,2,288,128]{3,2,1,0:T(8,128)(2,1)S(1)}, bf16[2,2,288,128]{3,2,1,0:T(8,128)(2,1)S(1)}, u32[]{:S(2)}, u32[]{:S(2)}) %collective-permute-start.14) | collective-permute-done | bytes 294944 | tf_op jit(solution)/shard_map/ppermute | solution.py:674
  141.9 1.5 collective-permute-start.20
  145.2 10.8 %collective-permute-done.15 = bf16[2,2,2,136,128]{4,3,2,1,0:T(8,128)(2,1)S(1)} collective-permute-done((bf16[2,2,2,136,128]{4,3,2,1,0:T(8,128)(2,1)S(1)}, bf16[2,2,2,136,128]{4,3,2,1,0:T(8,128)(2,1)S(1)}, u32[]{:S(2)}, u32[]{:S(2)}) %collective-permute-start.15) | collective-permute-done | bytes 278560 | tf_op jit(solution)/shard_map/ppermute | solution.py:674
  157.3 6.3 %collective-permute-done.21 = bf16[2,2,2,288,128]{4,3,2,1,0:T(8,128)(2,1)S(1)} collective-permute-done((bf16[2,2,2,288,128]{4,3,2,1,0:T(8,128)(2,1)S(1)}, bf16[2,2,2,288,128]{4,3,2,1,0:T(8,128)(2,1)S(1)}, u32[]{:S(2)}, u32[]{:S(2)}) %collective-permute-start.21) | collective-permute-done | bytes 589856 | tf_op jit(solution)/shard_map/ppermute | solution.py:674
  164.1 1.5 collective-permute-start.16
  165.6 1.5 collective-permute-start.17
  168.6 6.1 %shard_map.261 = (f32[512,2048]{1,0:T(8,128)}, f32[2048,512]{1,0:T(8,128)}, f32[256,512]{1,0:T(8,128)}) custom-call(s32[5]{0:T(128)S(1)} %copy-done, bf16[4,2,2,2,288,128]{5,4,3,2,1,0:T(8,128)(2,1)S(1)} %pad_maximum_fusion.refs_1_, bf16[4,2,2,2,288,128]{5,4,3,2,1,0:T(8,128)(2,1)S(1)} %collective-permute-done.22.refs_2_), custom_call_target="tpu_custom_call" | custom-call | flops 17179869184 | bytes 16777216 | tf_op jit(solution)/shard_map/pallas_call | solution.py:852
  175.1 5.2 %collective-permute-done.18 = bf16[2,2,2,136,128]{4,3,2,1,0:T(8,128)(2,1)S(1)} collective-permute-done((bf16[2,2,2,136,128]{4,3,2,1,0:T(8,128)(2,1)S(1)}, bf16[2,2,2,136,128]{4,3,2,1,0:T(8,128)(2,1)S(1)}, u32[]{:S(2)}, u32[]{:S(2)}) %collective-permute-start.18) | collective-permute-done | bytes 278560 | tf_op jit(solution)/shard_map/ppermute | solution.py:674
  180.5 2.7 %collective-permute-done.23.refs_2_ = bf16[4,2,2,2,136,128]{5,4,3,2,1,0:T(8,128)(2,1)S(1)} collective-permute-done((bf16[4,2,2,2,136,128]{5,4,3,2,1,0:T(8,128)(2,1)S(1)}, bf16[4,2,2,2,136,128]{5,4,3,2,1,0:T(8,128)(2,1)S(1)}, u32[]{:S(2)}, u32[]{:S(2)}) %collective-permute-start.23) | collective-permute-done | bytes 1114144 | tf_op jit(solution)/shard_map/ppermute | solution.py:674
  183.2 3.0 %shard_map.262 = (f32[512,256]{1,0:T(8,128)}, f32[512,256]{1,0:T(8,128)}, f32[512,256]{1,0:T(8,128)}, f32[512,512]{1,0:T(8,128)}, f32[8,512]{1,0:T(8,128)}, /*in...) custom-call(s32[5]{0:T(128)S(1)} %copy-done, ...), custom_call_target="tpu_custom_call" | custom-call | flops 17179869184 | bytes 16777216 | tf_op jit(solution)/shard_map/pallas_call | solution.py:852
  (60 shorter events, 15.9 us)
Async XLA Ops:
  4.1 15.2 %collective-permute-start = (bf16[2048,128]{1,0:T(8,128)(2,1)}, bf16[2048,128]{1,0:T(8,128)(2,1)S(1)}, u32[]{:S(2)}, u32[]{:S(2)}) collective-permute-start(bf16[2048,128]{1,0:T(8,128)(2,1)} %shard_map.254), channel_id=1, source_target_pairs={{0,1},{1,0},{2,3},{3,2},{4,5},{5,4},{6,7},{7,6},{8,9},{9,8},{10,11... | collective-permute-start | bytes 1572872 | tf_op jit(solution)/shard_map/ppermute | solution.py:674
  19.2 1.9 %collective-permute-start.1 = (bf16[2048,128]{1,0:T(8,128)(2,1)S(1)}, bf16[2048,128]{1,0:T(8,128)(2,1)S(1)}, u32[]{:S(2)}, u32[]{:S(2)}) collective-permute-start(bf16[2048,128]{1,0:T(8,128)(2,1)S(1)} %collective-permute-done.refs_6_), channel_id=1, source_target_pairs={{0,2},{1,3},{2,0},{3,1},{4,6},{5,7},{6,4},{7,5},{8,10},{9,11},{10,... | collective-permute-start | bytes 1572872 | tf_op jit(solution)/shard_map/ppermute | solution.py:674
  56.3 6.4 %collective-permute-start.2 = (bf16[4,4,2,288,128]{4,3,2,1,0:T(8,128)(2,1)}, bf16[4,4,2,288,128]{4,3,2,1,0:T(8,128)(2,1)}, u32[]{:S(2)}, u32[]{:S(2)}) collective-permute-start(bf16[4,4,2,288,128]{4,3,2,1,0:T(8,128)(2,1)} %get-tuple-element.98), channel_id=1, source_target_pairs={{0,2},{1,3},{2,0},{3,1},{4,6},{5,7},{6,4},{7,5},{8,10},{9,11},{10,... | collective-permute-start | bytes 7077896 | tf_op jit(solution)/shard_map/ppermute | solution.py:674
  56.5 6.3 %copy-start.1 = (bf16[4,4,2,288,128]{4,3,2,1,0:T(8,128)(2,1)S(1)}, bf16[4,4,2,288,128]{4,3,2,1,0:T(8,128)(2,1)}, u32[]{:S(2)}) copy-start(bf16[4,4,2,288,128]{4,3,2,1,0:T(8,128)(2,1)} %get-tuple-element.96) | copy-start | bytes 7077892
  64.7 25.5 %collective-permute-start.3 = (bf16[2,2,2,288,128]{4,3,2,1,0:T(8,128)(2,1)S(1)}, bf16[2,2,2,288,128]{4,3,2,1,0:T(8,128)(2,1)S(1)}, u32[]{:S(2)}, u32[]{:S(2)}) collective-permute-start(bf16[2,2,2,288,128]{4,3,2,1,0:T(8,128)(2,1)S(1)} %get-tuple-element.168), channel_id=1, source_target_pairs={{0,1},{1,0},{2,3},{3,2},{4,5},{5,4},{6,7},{7,6},{8,9},{9,8},{10,11... | collective-permute-start | bytes 1769480 | tf_op jit(solution)/shard_map/ppermute | solution.py:674
  66.5 23.7 %collective-permute-start.4 = (bf16[2,2,2,288,128]{4,3,2,1,0:T(8,128)(2,1)S(1)}, bf16[2,2,2,288,128]{4,3,2,1,0:T(8,128)(2,1)S(1)}, u32[]{:S(2)}, u32[]{:S(2)}) collective-permute-start(bf16[2,2,2,288,128]{4,3,2,1,0:T(8,128)(2,1)S(1)} %get-tuple-element.167), channel_id=1, source_target_pairs={{0,4},{1,5},{2,6},{3,7},{4,0},{5,1},{6,2},{7,3},{8,12},{9,13},{10,... | collective-permute-start | bytes 1769480 | tf_op jit(solution)/shard_map/ppermute | solution.py:674
  68.0 26.3 %collective-permute-start.5 = (bf16[2,2,2,288,128]{4,3,2,1,0:T(8,128)(2,1)S(1)}, bf16[2,2,2,288,128]{4,3,2,1,0:T(8,128)(2,1)S(1)}, u32[]{:S(2)}, u32[]{:S(2)}) collective-permute-start(bf16[2,2,2,288,128]{4,3,2,1,0:T(8,128)(2,1)S(1)} %get-tuple-element.166), channel_id=1, source_target_pairs={{0,5},{1,4},{2,7},{3,6},{4,1},{5,0},{6,3},{7,2},{8,13},{9,12},{10,... | collective-permute-start | bytes 1769480 | tf_op jit(solution)/shard_map/ppermute | solution.py:674
  90.2 9.2 %copy-start.2 = (bf16[4,4,2,136,128]{4,3,2,1,0:T(8,128)(2,1)S(1)}, bf16[4,4,2,136,128]{4,3,2,1,0:T(8,128)(2,1)}, u32[]{:S(2)}) copy-start(bf16[4,4,2,136,128]{4,3,2,1,0:T(8,128)(2,1)} %get-tuple-element.126) | copy-start | bytes 3342340
  90.2 4.1 %copy-start.3 = (bf16[2,2,2,288,128]{4,3,2,1,0:T(8,128)(2,1)}, bf16[2,2,2,288,128]{4,3,2,1,0:T(8,128)(2,1)S(1)}, u32[]{:S(2)}) copy-start(bf16[2,2,2,288,128]{4,3,2,1,0:T(8,128)(2,1)S(1)} %collective-permute-done.3) | copy-start | bytes 1769476
  90.2 6.1 %copy-start.5 = (bf16[2,2,2,288,128]{4,3,2,1,0:T(8,128)(2,1)}, bf16[2,2,2,288,128]{4,3,2,1,0:T(8,128)(2,1)S(1)}, u32[]{:S(2)}) copy-start(bf16[2,2,2,288,128]{4,3,2,1,0:T(8,128)(2,1)S(1)} %collective-permute-done.4) | copy-start | bytes 1769476
  96.3 3.1 %collective-permute-start.7 = (bf16[4,4,2,136,128]{4,3,2,1,0:T(8,128)(2,1)}, bf16[4,4,2,136,128]{4,3,2,1,0:T(8,128)(2,1)}, u32[]{:S(2)}, u32[]{:S(2)}) collective-permute-start(bf16[4,4,2,136,128]{4,3,2,1,0:T(8,128)(2,1)} %get-tuple-element.127), channel_id=1, source_target_pairs={{0,2},{1,3},{2,0},{3,1},{4,6},{5,7},{6,4},{7,5},{8,10},{9,11},{10,... | collective-permute-start | bytes 3342344 | tf_op jit(solution)/shard_map/ppermute | solution.py:674
  96.3 9.7 %collective-permute-start.6 = (bf16[2,2,288,128]{3,2,1,0:T(8,128)(2,1)}, bf16[2,2,288,128]{3,2,1,0:T(8,128)(2,1)}, u32[]{:S(2)}, u32[]{:S(2)}) collective-permute-start(bf16[2,2,288,128]{3,2,1,0:T(8,128)(2,1)} %fusion.3), channel_id=1, source_target_pairs={{0,8},{1,9},{2,10},{3,11},{4,12},{5,13},{6,14},{7,15},{8,0},{9,1},... | collective-permute-start | bytes 884744 | tf_op jit(solution)/shard_map/ppermute | solution.py:674
  98.1 7.9 %copy-start.4 = (bf16[2,2,2,288,128]{4,3,2,1,0:T(8,128)(2,1)S(1)}, bf16[2,2,2,288,128]{4,3,2,1,0:T(8,128)(2,1)}, u32[]{:S(2)}) copy-start(bf16[2,2,2,288,128]{4,3,2,1,0:T(8,128)(2,1)} %copy-done.3) | copy-start | bytes 1769476
  98.1 7.9 %copy-start.6 = (bf16[2,2,2,288,128]{4,3,2,1,0:T(8,128)(2,1)S(1)}, bf16[2,2,2,288,128]{4,3,2,1,0:T(8,128)(2,1)}, u32[]{:S(2)}) copy-start(bf16[2,2,2,288,128]{4,3,2,1,0:T(8,128)(2,1)} %copy-done.5) | copy-start | bytes 1769476
  98.1 7.9 %copy-start.8 = (bf16[2,2,2,288,128]{4,3,2,1,0:T(8,128)(2,1)S(1)}, bf16[2,2,2,288,128]{4,3,2,1,0:T(8,128)(2,1)}, u32[]{:S(2)}) copy-start(bf16[2,2,2,288,128]{4,3,2,1,0:T(8,128)(2,1)} %copy-done.7) | copy-start | bytes 1769476
  100.8 16.1 %collective-permute-start.10 = (bf16[2,2,2,136,128]{4,3,2,1,0:T(8,128)(2,1)S(1)}, bf16[2,2,2,136,128]{4,3,2,1,0:T(8,128)(2,1)S(1)}, u32[]{:S(2)}, u32[]{:S(2)}) collective-permute-start(bf16[2,2,2,136,128]{4,3,2,1,0:T(8,128)(2,1)S(1)} %get-tuple-element.170), channel_id=1, source_target_pairs={{0,4},{1,5},{2,6},{3,7},{4,0},{5,1},{6,2},{7,3},{8,12},{9,13},{10,... | collective-permute-start | bytes 835592 | tf_op jit(solution)/shard_map/ppermute | solution.py:674
  102.5 14.3 %collective-permute-start.11 = (bf16[2,2,2,136,128]{4,3,2,1,0:T(8,128)(2,1)S(1)}, bf16[2,2,2,136,128]{4,3,2,1,0:T(8,128)(2,1)S(1)}, u32[]{:S(2)}, u32[]{:S(2)}) collective-permute-start(bf16[2,2,2,136,128]{4,3,2,1,0:T(8,128)(2,1)S(1)} %get-tuple-element.169), channel_id=1, source_target_pairs={{0,5},{1,4},{2,7},{3,6},{4,1},{5,0},{6,3},{7,2},{8,13},{9,12},{10,... | collective-permute-start | bytes 835592 | tf_op jit(solution)/shard_map/ppermute | solution.py:674
  104.0 14.1 %collective-permute-start.9 = (bf16[2,2,2,136,128]{4,3,2,1,0:T(8,128)(2,1)S(1)}, bf16[2,2,2,136,128]{4,3,2,1,0:T(8,128)(2,1)S(1)}, u32[]{:S(2)}, u32[]{:S(2)}) collective-permute-start(bf16[2,2,2,136,128]{4,3,2,1,0:T(8,128)(2,1)S(1)} %get-tuple-element.171), channel_id=1, source_target_pairs={{0,1},{1,0},{2,3},{3,2},{4,5},{5,4},{6,7},{7,6},{8,9},{9,8},{10,11... | collective-permute-start | bytes 835592 | tf_op jit(solution)/shard_map/ppermute | solution.py:674
  107.2 12.0 %collective-permute-start.8 = (bf16[2,288,128]{2,1,0:T(8,128)(2,1)S(1)}, bf16[2,288,128]{2,1,0:T(8,128)(2,1)S(1)}, u32[]{:S(2)}, u32[]{:S(2)}) collective-permute-start(bf16[2,288,128]{2,1,0:T(8,128)(2,1)S(1)} %fusion.9), channel_id=1, source_target_pairs={{0,16},{1,17},{2,18},{3,19},{4,20},{5,21},{6,22},{7,23},{8,24},{9,... | collective-permute-start | bytes 442376 | tf_op jit(solution)/shard_map/ppermute | solution.py:674
  120.4 10.8 %collective-permute-start.13 = (bf16[2,288,128]{2,1,0:T(8,128)(2,1)S(1)}, bf16[2,288,128]{2,1,0:T(8,128)(2,1)S(1)}, u32[]{:S(2)}, u32[]{:S(2)}) collective-permute-start(bf16[2,288,128]{2,1,0:T(8,128)(2,1)S(1)} %fusion.8), channel_id=1, source_target_pairs={{0,16},{1,17},{2,18},{3,19},{4,20},{5,21},{6,22},{7,23},{8,24},{9,... | collective-permute-start | bytes 442376 | tf_op jit(solution)/shard_map/ppermute | solution.py:674
  131.2 9.6 %collective-permute-start.14 = (bf16[2,2,288,128]{3,2,1,0:T(8,128)(2,1)S(1)}, bf16[2,2,288,128]{3,2,1,0:T(8,128)(2,1)S(1)}, u32[]{:S(2)}, u32[]{:S(2)}) collective-permute-start(bf16[2,2,288,128]{3,2,1,0:T(8,128)(2,1)S(1)} %get-tuple-element.175), channel_id=1, source_target_pairs={{0,8},{1,9},{2,10},{3,11},{4,12},{5,13},{6,14},{7,15},{8,0},{9,1},... | collective-permute-start | bytes 884744 | tf_op jit(solution)/shard_map/ppermute | solution.py:674
  132.9 11.5 %collective-permute-start.12 = (bf16[2,2,2,136,128]{4,3,2,1,0:T(8,128)(2,1)S(1)}, bf16[2,2,2,136,128]{4,3,2,1,0:T(8,128)(2,1)S(1)}, u32[]{:S(2)}, u32[]{:S(2)}) collective-permute-start(bf16[2,2,2,136,128]{4,3,2,1,0:T(8,128)(2,1)S(1)} %fusion.6), channel_id=1, source_target_pairs={{0,8},{1,9},{2,10},{3,11},{4,12},{5,13},{6,14},{7,15},{8,0},{9,1},... | collective-permute-start | bytes 835592 | tf_op jit(solution)/shard_map/ppermute | solution.py:674
  140.8 16.3 %collective-permute-start.19 = (bf16[2,2,2,288,128]{4,3,2,1,0:T(8,128)(2,1)S(1)}, bf16[2,2,2,288,128]{4,3,2,1,0:T(8,128)(2,1)S(1)}, u32[]{:S(2)}, u32[]{:S(2)}) collective-permute-start(bf16[2,2,2,288,128]{4,3,2,1,0:T(8,128)(2,1)S(1)} %get-tuple-element.173), channel_id=1, source_target_pairs={{0,1},{1,0},{2,3},{3,2},{4,5},{5,4},{6,7},{7,6},{8,9},{9,8},{10,11... | collective-permute-start | bytes 1769480 | tf_op jit(solution)/shard_map/ppermute | solution.py:674
  141.9 15.4 %collective-permute-start.20 = (bf16[2,2,2,288,128]{4,3,2,1,0:T(8,128)(2,1)S(1)}, bf16[2,2,2,288,128]{4,3,2,1,0:T(8,128)(2,1)S(1)}, u32[]{:S(2)}, u32[]{:S(2)}) collective-permute-start(bf16[2,2,2,288,128]{4,3,2,1,0:T(8,128)(2,1)S(1)} %get-tuple-element.173), channel_id=1, source_target_pairs={{0,4},{1,5},{2,6},{3,7},{4,0},{5,1},{6,2},{7,3},{8,12},{9,13},{10,... | collective-permute-start | bytes 1769480 | tf_op jit(solution)/shard_map/ppermute | solution.py:674
  143.3 20.3 %collective-permute-start.21 = (bf16[2,2,2,288,128]{4,3,2,1,0:T(8,128)(2,1)S(1)}, bf16[2,2,2,288,128]{4,3,2,1,0:T(8,128)(2,1)S(1)}, u32[]{:S(2)}, u32[]{:S(2)}) collective-permute-start(bf16[2,2,2,288,128]{4,3,2,1,0:T(8,128)(2,1)S(1)} %get-tuple-element.173), channel_id=1, source_target_pairs={{0,5},{1,4},{2,7},{3,6},{4,1},{5,0},{6,3},{7,2},{8,13},{9,12},{10,... | collective-permute-start | bytes 1769480 | tf_op jit(solution)/shard_map/ppermute | solution.py:674
  144.5 11.5 %collective-permute-start.15 = (bf16[2,2,2,136,128]{4,3,2,1,0:T(8,128)(2,1)S(1)}, bf16[2,2,2,136,128]{4,3,2,1,0:T(8,128)(2,1)S(1)}, u32[]{:S(2)}, u32[]{:S(2)}) collective-permute-start(bf16[2,2,2,136,128]{4,3,2,1,0:T(8,128)(2,1)S(1)} %add_convert_fusion.4), channel_id=1, source_target_pairs={{0,16},{1,17},{2,18},{3,19},{4,20},{5,21},{6,22},{7,23},{8,24},{9,... | collective-permute-start | bytes 835592 | tf_op jit(solution)/shard_map/ppermute | solution.py:674
  163.7 4.9 %copy-start = (s32[5]{0:T(128)S(1)}, s32[5]{0:T(128)}, u32[]{:S(2)}) copy-start(s32[5]{0:T(128)} %stack.71.refs_0_.refs_1_) | copy-start | bytes 64
  164.0 4.6 %collective-permute-start.22 = (bf16[4,2,2,2,288,128]{5,4,3,2,1,0:T(8,128)(2,1)S(1)}, bf16[4,2,2,2,288,128]{5,4,3,2,1,0:T(8,128)(2,1)S(1)}, u32[]{:S(2)}, u32[]{:S(2)}) collective-permute-start(bf16[4,2,2,2,288,128]{5,4,3,2,1,0:T(8,128)(2,1)S(1)} %pad_maximum_fusion.refs_1_), channel_id=1, source_target_pairs={{0,2},{1,3},{2,0},{3,1},{4,6},{5,7},{6,4},{7,5},{8,10},{9,11},{10,... | collective-permute-start | bytes 7077896 | tf_op jit(solution)/shard_map/ppermute | solution.py:674
  164.1 10.6 %collective-permute-start.16 = (bf16[2,2,2,136,128]{4,3,2,1,0:T(8,128)(2,1)S(1)}, bf16[2,2,2,136,128]{4,3,2,1,0:T(8,128)(2,1)S(1)}, u32[]{:S(2)}, u32[]{:S(2)}) collective-permute-start(bf16[2,2,2,136,128]{4,3,2,1,0:T(8,128)(2,1)S(1)} %add_convert_fusion.3), channel_id=1, source_target_pairs={{0,1},{1,0},{2,3},{3,2},{4,5},{5,4},{6,7},{7,6},{8,9},{9,8},{10,11... | collective-permute-start | bytes 835592 | tf_op jit(solution)/shard_map/ppermute | solution.py:674
  165.6 9.5 %collective-permute-start.17 = (bf16[2,2,2,136,128]{4,3,2,1,0:T(8,128)(2,1)S(1)}, bf16[2,2,2,136,128]{4,3,2,1,0:T(8,128)(2,1)S(1)}, u32[]{:S(2)}, u32[]{:S(2)}) collective-permute-start(bf16[2,2,2,136,128]{4,3,2,1,0:T(8,128)(2,1)S(1)} %add_convert_fusion.3), channel_id=1, source_target_pairs={{0,4},{1,5},{2,6},{3,7},{4,0},{5,1},{6,2},{7,3},{8,12},{9,13},{10,... | collective-permute-start | bytes 835592 | tf_op jit(solution)/shard_map/ppermute | solution.py:674
  167.1 13.2 %collective-permute-start.18 = (bf16[2,2,2,136,128]{4,3,2,1,0:T(8,128)(2,1)S(1)}, bf16[2,2,2,136,128]{4,3,2,1,0:T(8,128)(2,1)S(1)}, u32[]{:S(2)}, u32[]{:S(2)}) collective-permute-start(bf16[2,2,2,136,128]{4,3,2,1,0:T(8,128)(2,1)S(1)} %add_convert_fusion.3), channel_id=1, source_target_pairs={{0,5},{1,4},{2,7},{3,6},{4,1},{5,0},{6,3},{7,2},{8,13},{9,12},{10,... | collective-permute-start | bytes 835592 | tf_op jit(solution)/shard_map/ppermute | solution.py:674
  180.4 2.8 %collective-permute-start.23 = (bf16[4,2,2,2,136,128]{5,4,3,2,1,0:T(8,128)(2,1)S(1)}, bf16[4,2,2,2,136,128]{5,4,3,2,1,0:T(8,128)(2,1)S(1)}, u32[]{:S(2)}, u32[]{:S(2)}) collective-permute-start(bf16[4,2,2,2,136,128]{5,4,3,2,1,0:T(8,128)(2,1)S(1)} %pad_maximum_fusion.1.refs_1_), channel_id=1, source_target_pairs={{0,2},{1,3},{2,0},{3,1},{4,6},{5,7},{6,4},{7,5},{8,10},{9,11},{10,... | collective-permute-start | bytes 3342344 | tf_op jit(solution)/shard_map/ppermute | solution.py:674
  (3 other events, 4.8 us)

commit v3 on v2

--- a/solution.py
+++ b/solution.py
@@ -656,15 +656,22 @@
         out[...] = small[0, 8 + n : 9 + n, :]
 
 
-def slice_kernel(ids, w_q, w_k, w_v, w_o, mine):
-    core = ids[0]
-    lanes = pl.ds(pl.multiple_of(core * 2 * HD, 2 * HD), 2 * HD)
-    for slot, w in enumerate((w_q, w_k, w_v)):
-        w.wait()
-        mine[512 * slot : 512 * (slot + 1), :] = w[:, lanes]
-    w_o.wait()
-    for m in range(4):
-        mine[1536 + 128 * m : 1664 + 128 * m, :] = w_o[lanes, 128 * m : 128 * (m + 1)]
+def slice_kernel(ids, w_q, w_k, w_v, w_o, mine, taken, sems):
+    part = pl.ds(pl.multiple_of(ids[0] * 2 * HD, 2 * HD), 2 * HD)
+    sources = [w.at[:, part] for w in (w_q, w_k, w_v)]
+    sources += [w_o.at[part, 128 * m : 128 * (m + 1)] for m in range(4)]
+    copies, at = [], 0
+    for n, source in enumerate(sources):
+        target = taken.at[at : at + source.shape[0], :]
+        copies.append(pltpu.make_async_copy(source, target, sems.at[n]))
+        at += source.shape[0]
+    for copy in copies:
+        copy.start()
+    for copy in copies:
+        copy.wait()
+    out = pltpu.make_async_copy(taken, mine, sems.at[len(copies)])
+    out.start()
+    out.wait()
 
 
 def swap(values, bits, dp_size):
@@ -886,10 +893,14 @@
 
     gain1, bias1, gain2, bias2 = (v.reshape(1, d) for v in (ln1_gain, ln1_bias, ln2_gain, ln2_bias))
     second_t = sort_second.T
-    mine = call(
-        slice_kernel, (ids,), (w_query, w_key, w_value, w_out), [shaped((4 * d, 2 * HD), LOW)], [],
-        1 << 20,
-    )[0]
+    hbm = pl.BlockSpec(memory_space=pltpu.HBM)
+    mine = pl.pallas_call(
+        slice_kernel,
+        in_specs=[pl.BlockSpec(memory_space=pltpu.SMEM)] + [hbm] * 4,
+        out_specs=hbm,
+        out_shape=shaped((4 * d, 2 * HD), LOW),
+        scratch_shapes=[pltpu.VMEM((4 * d, 2 * HD), LOW), pltpu.SemaphoreType.DMA((8,))],
+    )(ids, w_query, w_key, w_value, w_out)
     near_w = swap(mine, ["head"], dp_size)
 
     low_rows, wide_rows = shaped((rows_all, d), LOW), shaped((rows_all, d), F32)

time: 187 us -> 187 us (level)
    pallas_call x9 -> x8, Pallas kernels: 101 us -> 98.1 us  [call(): pl.pallas_call(kernel, in_specs=[smem] * n_scalars + [pl.BlockSpec(memory...]
    pallas_call x0 -> x1, Pallas kernels: none -> 2.56 us  [on_device(): pl.pallas_call(slice_kernel, in_specs=[pl.BlockSpec(memory_space=pltpu.SM...]
where the time goes in v3:
time: 187 us; the launch traced here: 186 us
  Pallas kernels  101 us (54%)
  waiting for transfers between devices  46 us (25%)
  starting transfers between devices  27.6 us (15%)
  other arithmetic  9.42 us (5%)
    pallas_call x8, Pallas kernels, call(): pl.pallas_call(kernel, in_specs=[smem] * n_scalars + [pl.BlockSpec(memory...  98.1 us
    ppermute x24, waiting for transfers between devices, swap(): return lax.ppermute(values, AXES, pairs)  46 us
    ppermute x24, starting transfers between devices, swap(): return lax.ppermute(values, AXES, pairs)  27.6 us
    convert_element_type x8, other arithmetic, low_sum(): return total.astype(LOW)  8.86 us
  transfers between devices with their start and end apart: 24, of which 15 were waited for; matrix products, arithmetic and copies ran while one was open for 2% of the time, Pallas kernels for 33%

profile of v3, /device:TPU:0, one launch (start us, length us, event | category | flops | bytes accessed | tf_op | source)
XLA Modules:
  0.0 186.3 jit_solution(17443452217569179287)
XLA Ops:
  1.4 2.6 %shard_map.254 = bf16[2048,128]{1,0:T(8,128)(2,1)} custom-call(s32[5]{0:T(128)} %stack.71.ids.refs_1_.refs_0_, bf16[512,256]{1,0:T(8,128)(2,1)} %refs_2_.3, bf16[512,256]{1,0:T(8,128)(2,1)} %refs_3_.1, bf16[512,256]{1,0:T(8,128)(2,1)} %refs_4_.1, bf16[256,512]{1,0:T(8,128)(2,1)} %refs_5_.3), custom_call_target="tpu_custom_call" | custom-call | tf_op jit(solution)/shard_map/pallas_call | solution.py:897
  3.9 3.0 %collective-permute-start = (bf16[2048,128]{1,0:T(8,128)(2,1)}, bf16[2048,128]{1,0:T(8,128)(2,1)S(1)}, u32[]{:S(2)}, u32[]{:S(2)}) collective-permute-start(bf16[2048,128]{1,0:T(8,128)(2,1)} %shard_map.254), channel_id=1, source_target_pairs={{0,1},{1,0},{2,3},{3,2},{4,5},{5,4},{6,7},{7,6},{8,9},{9,8},{10,11... | collective-permute-start | bytes 1572872 | tf_op jit(solution)/shard_map/ppermute | solution.py:681
  7.0 11.6 %shard_map.255 = (bf16[1024,512]{1,0:T(8,128)(2,1)}, bf16[512,1024]{1,0:T(8,128)(2,1)}, f32[32,512]{1,0:T(8,128)}, f32[32,512]{1,0:T(8,128)}, f32[16,4,8,8]{3,2,...) custom-call(s32[8]{0:T(128)} %refs_0_.10, s32[5]{0:T(128)} %stack.71.ids.refs_1_.refs_0_, ...), custom_call_target="tpu_custom_call" | custom-call | flops 17179869184 | bytes 16777216 | tf_op jit(solution)/shard_map/pallas_call | solution.py:859
  19.1 1.9 %collective-permute-done.1.refs_7_ = bf16[2048,128]{1,0:T(8,128)(2,1)S(1)} collective-permute-done((bf16[2048,128]{1,0:T(8,128)(2,1)S(1)}, bf16[2048,128]{1,0:T(8,128)(2,1)S(1)}, u32[]{:S(2)}, u32[]{:S(2)}) %collective-permute-start.1) | collective-permute-done | bytes 524320 | tf_op jit(solution)/shard_map/ppermute | solution.py:681
  21.8 34.3 %shard_map.256 = (bf16[1024,512]{1,0:T(8,128)(2,1)}, bf16[1024,512]{1,0:T(8,128)(2,1)}, bf16[1024,512]{1,0:T(8,128)(2,1)}, bf16[1024,512]{1,0:T(8,128)(2,1)}, bf...) custom-call(s32[8]{0:T(128)} %refs_0_.10, ...), custom_call_target="tpu_custom_call" | custom-call | flops 17179869184 | bytes 16777216 | tf_op jit(solution)/shard_map/pallas_call | solution.py:859
  56.3 6.2 %shard_map.257 = (bf16[256,512]{1,0:T(8,128)(2,1)}, bf16[256,512]{1,0:T(8,128)(2,1)}, bf16[256,512]{1,0:T(8,128)(2,1)}, f32[1,8,8]{2,1,0:T(8,128)}) custom-call(s32[8]{0:T(128)} %refs_0_.10, s32[5]{0:T(128)} %stack.71.ids.refs_1_.refs_0_, bf16[1024,512]{1,0:T(8,128)(2,1)} %get-tuple-element.109.refs_2_, bf16[4,512,512]{2,1,0:T(8,128)(2,1)} %get-tuple-element.100.refs_3_, ...), custom_call_target="tpu_custom_call" | custom-call | flops 17179869184 | bytes 16777216 | tf_op jit(solution)/shard_map/pallas_call | solution.py:859
  62.6 1.9 %fusion.2 = (bf16[2,2,2,288,128]{4,3,2,1,0:T(8,128)(2,1)S(1)}, bf16[2,2,2,288,128]{4,3,2,1,0:T(8,128)(2,1)S(1)}, bf16[2,2,2,288,128]{4,3,2,1,0:T(8,128)(2,1)S(1)}) fusion(bf16[4,2,2,2,288,128]{5,4,3,2,1,0:T(8,128)(2,1)} %bitcast.11, s32[]{:T(128)S(6)} %select_n.125, bf16[4,2,2,2,288,128]{5,4,3,2,1,0:T(8,128)(2,1)S(1)} %bitcast.92, s32[]{:T(128)S(6)} %select_n.124, ...), kind=kLoop, calls=%fused_computation.7 | loop fusion | flops 3538944 | bytes 5308428 | tf_op jit(solution)/shard_map/convert_element_type | solution.py:702
  64.5 1.8 collective-permute-start.3
  66.4 1.5 collective-permute-start.4
  68.1 21.9 %shard_map.258 = (bf16[4,4,2,136,128]{4,3,2,1,0:T(8,128)(2,1)}, bf16[4,4,2,136,128]{4,3,2,1,0:T(8,128)(2,1)}, bf16[768,512]{1,0:T(8,128)(2,1)}, bf16[768,512]{1,...) custom-call(s32[8]{0:T(128)} %refs_0_.10, s32[5]{0:T(128)} %stack.71.ids.refs_1_.refs_0_, ...), custom_call_target="tpu_custom_call" | custom-call | flops 17179869184 | bytes 16777216 | tf_op jit(solution)/shard_map/pallas_call | solution.py:859
  90.1 4.0 %collective-permute-done.5 = bf16[2,2,2,288,128]{4,3,2,1,0:T(8,128)(2,1)S(1)} collective-permute-done((bf16[2,2,2,288,128]{4,3,2,1,0:T(8,128)(2,1)S(1)}, bf16[2,2,2,288,128]{4,3,2,1,0:T(8,128)(2,1)S(1)}, u32[]{:S(2)}, u32[]{:S(2)}) %collective-permute-start.5) | collective-permute-done | bytes 589856 | tf_op jit(solution)/shard_map/ppermute | solution.py:681
  94.1 2.1 %fusion.3 = bf16[2,2,288,128]{3,2,1,0:T(8,128)(2,1)} fusion(bf16[2,2,2,288,128]{4,3,2,1,0:T(8,128)(2,1)S(1)} %collective-permute-done.5, s32[]{:T(128)S(6)} %select_n.126, bf16[2,2,2,288,128]{4,3,2,1,0:T(8,128)(2,1)S(1)} %collective-permute-done.4, bf16[2,2,2,288,128]{4,3,2,1,0:T(8,128)(2,1)S(1)} %collective-permute-done.3, ...), kind=kLoop, calls=%fused_computation.10 | loop fusion | flops 1474560 | bytes 1769484 | tf_op jit(solution)/shard_map/convert_element_type | solution.py:702
  96.2 1.8 collective-permute-start.6
  99.3 1.3 fusion.12
  100.6 1.7 collective-permute-start.10
  102.3 1.5 collective-permute-start.11
  104.2 1.7 collective-permute-done.6
  107.0 2.8 %collective-permute-start.8 = (bf16[2,288,128]{2,1,0:T(8,128)(2,1)S(1)}, bf16[2,288,128]{2,1,0:T(8,128)(2,1)S(1)}, u32[]{:S(2)}, u32[]{:S(2)}) collective-permute-start(bf16[2,288,128]{2,1,0:T(8,128)(2,1)S(1)} %fusion.9), channel_id=1, source_target_pairs={{0,16},{1,17},{2,18},{3,19},{4,20},{5,21},{6,22},{7,23},{8,24},{9,... | collective-permute-start | bytes 442376 | tf_op jit(solution)/shard_map/ppermute | solution.py:681
  109.8 6.8 %shard_map.259 = bf16[1024,512]{1,0:T(8,128)(2,1)} custom-call(bf16[2048,512]{1,0:T(8,128)(2,1)} %refs_0_.9, bf16[1024,2048]{1,0:T(8,128)(2,1)} %get-tuple-element.131.refs_1_.refs_2_.refs_3_.refs_4_, bf16[1024,2048]{1,0:T(8,128)(2,1)} %get-tuple-element.131.refs_1_.refs_2_.refs_3_.refs_4_, ...), custom_call_target="tpu_custom_call" | custom-call | flops 17179869184 | bytes 16777216 | tf_op jit(solution)/shard_map/pallas_call | solution.py:859
  120.2 2.7 %collective-permute-start.13 = (bf16[2,288,128]{2,1,0:T(8,128)(2,1)S(1)}, bf16[2,288,128]{2,1,0:T(8,128)(2,1)S(1)}, u32[]{:S(2)}, u32[]{:S(2)}) collective-permute-start(bf16[2,288,128]{2,1,0:T(8,128)(2,1)S(1)} %fusion.8), channel_id=1, source_target_pairs={{0,16},{1,17},{2,18},{3,19},{4,20},{5,21},{6,22},{7,23},{8,24},{9,... | collective-permute-start | bytes 442376 | tf_op jit(solution)/shard_map/ppermute | solution.py:681
  122.9 8.1 %shard_map.260 = bf16[1024,512]{1,0:T(8,128)(2,1)} custom-call(s32[8]{0:T(128)} %refs_0_.10, s32[5]{0:T(128)} %stack.71.ids.refs_1_.refs_0_, f32[32,512]{1,0:T(8,128)} %get-tuple-element.137.refs_2_, bf16[4,512,512]{2,1,0:T(8,128)(2,1)} %get-tuple-element.100.refs_3_, f32[1,512]{1,0:T(1,128)} %bitcast.116, ...), custom_call_target="tpu_custom_call" | custom-call | flops 17179869184 | bytes 16777216 | tf_op jit(solution)/shard_map/pallas_call | solution.py:859
  131.0 1.6 collective-permute-start.14
  133.1 7.5 %collective-permute-done.14 = bf16[2,2,288,128]{3,2,1,0:T(8,128)(2,1)S(1)} collective-permute-done((bf16[2,2,288,128]{3,2,1,0:T(8,128)(2,1)S(1)}, bf16[2,2,288,128]{3,2,1,0:T(8,128)(2,1)S(1)}, u32[]{:S(2)}, u32[]{:S(2)}) %collective-permute-start.14) | collective-permute-done | bytes 294944 | tf_op jit(solution)/shard_map/ppermute | solution.py:681
  141.7 1.5 collective-permute-start.20
  145.0 10.9 %collective-permute-done.15 = bf16[2,2,2,136,128]{4,3,2,1,0:T(8,128)(2,1)S(1)} collective-permute-done((bf16[2,2,2,136,128]{4,3,2,1,0:T(8,128)(2,1)S(1)}, bf16[2,2,2,136,128]{4,3,2,1,0:T(8,128)(2,1)S(1)}, u32[]{:S(2)}, u32[]{:S(2)}) %collective-permute-start.15) | collective-permute-done | bytes 278560 | tf_op jit(solution)/shard_map/ppermute | solution.py:681
  157.2 6.3 %collective-permute-done.21 = bf16[2,2,2,288,128]{4,3,2,1,0:T(8,128)(2,1)S(1)} collective-permute-done((bf16[2,2,2,288,128]{4,3,2,1,0:T(8,128)(2,1)S(1)}, bf16[2,2,2,288,128]{4,3,2,1,0:T(8,128)(2,1)S(1)}, u32[]{:S(2)}, u32[]{:S(2)}) %collective-permute-start.21) | collective-permute-done | bytes 589856 | tf_op jit(solution)/shard_map/ppermute | solution.py:681
  163.9 1.6 collective-permute-start.16
  165.5 1.5 collective-permute-start.17
  168.4 6.1 %shard_map.261 = (f32[512,2048]{1,0:T(8,128)}, f32[2048,512]{1,0:T(8,128)}, f32[256,512]{1,0:T(8,128)}) custom-call(s32[5]{0:T(128)S(1)} %copy-done, bf16[4,2,2,2,288,128]{5,4,3,2,1,0:T(8,128)(2,1)S(1)} %pad_maximum_fusion.refs_1_, bf16[4,2,2,2,288,128]{5,4,3,2,1,0:T(8,128)(2,1)S(1)} %collective-permute-done.22.refs_2_), custom_call_target="tpu_custom_call" | custom-call | flops 17179869184 | bytes 16777216 | tf_op jit(solution)/shard_map/pallas_call | solution.py:859
  175.0 5.2 %collective-permute-done.18 = bf16[2,2,2,136,128]{4,3,2,1,0:T(8,128)(2,1)S(1)} collective-permute-done((bf16[2,2,2,136,128]{4,3,2,1,0:T(8,128)(2,1)S(1)}, bf16[2,2,2,136,128]{4,3,2,1,0:T(8,128)(2,1)S(1)}, u32[]{:S(2)}, u32[]{:S(2)}) %collective-permute-start.18) | collective-permute-done | bytes 278560 | tf_op jit(solution)/shard_map/ppermute | solution.py:681
  180.4 2.7 %collective-permute-done.23.refs_2_ = bf16[4,2,2,2,136,128]{5,4,3,2,1,0:T(8,128)(2,1)S(1)} collective-permute-done((bf16[4,2,2,2,136,128]{5,4,3,2,1,0:T(8,128)(2,1)S(1)}, bf16[4,2,2,2,136,128]{5,4,3,2,1,0:T(8,128)(2,1)S(1)}, u32[]{:S(2)}, u32[]{:S(2)}) %collective-permute-start.23) | collective-permute-done | bytes 1114144 | tf_op jit(solution)/shard_map/ppermute | solution.py:681
  183.1 3.0 %shard_map.262 = (f32[512,256]{1,0:T(8,128)}, f32[512,256]{1,0:T(8,128)}, f32[512,256]{1,0:T(8,128)}, f32[512,512]{1,0:T(8,128)}, f32[8,512]{1,0:T(8,128)}, /*in...) custom-call(s32[5]{0:T(128)S(1)} %copy-done, ...), custom_call_target="tpu_custom_call" | custom-call | flops 17179869184 | bytes 16777216 | tf_op jit(solution)/shard_map/pallas_call | solution.py:859
  (60 shorter events, 16.0 us)
Async XLA Ops:
  3.9 15.2 %collective-permute-start = (bf16[2048,128]{1,0:T(8,128)(2,1)}, bf16[2048,128]{1,0:T(8,128)(2,1)S(1)}, u32[]{:S(2)}, u32[]{:S(2)}) collective-permute-start(bf16[2048,128]{1,0:T(8,128)(2,1)} %shard_map.254), channel_id=1, source_target_pairs={{0,1},{1,0},{2,3},{3,2},{4,5},{5,4},{6,7},{7,6},{8,9},{9,8},{10,11... | collective-permute-start | bytes 1572872 | tf_op jit(solution)/shard_map/ppermute | solution.py:681
  19.1 1.9 %collective-permute-start.1 = (bf16[2048,128]{1,0:T(8,128)(2,1)S(1)}, bf16[2048,128]{1,0:T(8,128)(2,1)S(1)}, u32[]{:S(2)}, u32[]{:S(2)}) collective-permute-start(bf16[2048,128]{1,0:T(8,128)(2,1)S(1)} %collective-permute-done.refs_6_), channel_id=1, source_target_pairs={{0,2},{1,3},{2,0},{3,1},{4,6},{5,7},{6,4},{7,5},{8,10},{9,11},{10,... | collective-permute-start | bytes 1572872 | tf_op jit(solution)/shard_map/ppermute | solution.py:681
  56.1 6.4 %collective-permute-start.2 = (bf16[4,4,2,288,128]{4,3,2,1,0:T(8,128)(2,1)}, bf16[4,4,2,288,128]{4,3,2,1,0:T(8,128)(2,1)}, u32[]{:S(2)}, u32[]{:S(2)}) collective-permute-start(bf16[4,4,2,288,128]{4,3,2,1,0:T(8,128)(2,1)} %get-tuple-element.98), channel_id=1, source_target_pairs={{0,2},{1,3},{2,0},{3,1},{4,6},{5,7},{6,4},{7,5},{8,10},{9,11},{10,... | collective-permute-start | bytes 7077896 | tf_op jit(solution)/shard_map/ppermute | solution.py:681
  56.3 6.3 %copy-start.1 = (bf16[4,4,2,288,128]{4,3,2,1,0:T(8,128)(2,1)S(1)}, bf16[4,4,2,288,128]{4,3,2,1,0:T(8,128)(2,1)}, u32[]{:S(2)}) copy-start(bf16[4,4,2,288,128]{4,3,2,1,0:T(8,128)(2,1)} %get-tuple-element.96) | copy-start | bytes 7077892
  64.5 25.5 %collective-permute-start.3 = (bf16[2,2,2,288,128]{4,3,2,1,0:T(8,128)(2,1)S(1)}, bf16[2,2,2,288,128]{4,3,2,1,0:T(8,128)(2,1)S(1)}, u32[]{:S(2)}, u32[]{:S(2)}) collective-permute-start(bf16[2,2,2,288,128]{4,3,2,1,0:T(8,128)(2,1)S(1)} %get-tuple-element.168), channel_id=1, source_target_pairs={{0,1},{1,0},{2,3},{3,2},{4,5},{5,4},{6,7},{7,6},{8,9},{9,8},{10,11... | collective-permute-start | bytes 1769480 | tf_op jit(solution)/shard_map/ppermute | solution.py:681
  66.4 23.7 %collective-permute-start.4 = (bf16[2,2,2,288,128]{4,3,2,1,0:T(8,128)(2,1)S(1)}, bf16[2,2,2,288,128]{4,3,2,1,0:T(8,128)(2,1)S(1)}, u32[]{:S(2)}, u32[]{:S(2)}) collective-permute-start(bf16[2,2,2,288,128]{4,3,2,1,0:T(8,128)(2,1)S(1)} %get-tuple-element.167), channel_id=1, source_target_pairs={{0,4},{1,5},{2,6},{3,7},{4,0},{5,1},{6,2},{7,3},{8,12},{9,13},{10,... | collective-permute-start | bytes 1769480 | tf_op jit(solution)/shard_map/ppermute | solution.py:681
  67.9 26.3 %collective-permute-start.5 = (bf16[2,2,2,288,128]{4,3,2,1,0:T(8,128)(2,1)S(1)}, bf16[2,2,2,288,128]{4,3,2,1,0:T(8,128)(2,1)S(1)}, u32[]{:S(2)}, u32[]{:S(2)}) collective-permute-start(bf16[2,2,2,288,128]{4,3,2,1,0:T(8,128)(2,1)S(1)} %get-tuple-element.166), channel_id=1, source_target_pairs={{0,5},{1,4},{2,7},{3,6},{4,1},{5,0},{6,3},{7,2},{8,13},{9,12},{10,... | collective-permute-start | bytes 1769480 | tf_op jit(solution)/shard_map/ppermute | solution.py:681
  90.1 9.2 %copy-start.2 = (bf16[4,4,2,136,128]{4,3,2,1,0:T(8,128)(2,1)S(1)}, bf16[4,4,2,136,128]{4,3,2,1,0:T(8,128)(2,1)}, u32[]{:S(2)}) copy-start(bf16[4,4,2,136,128]{4,3,2,1,0:T(8,128)(2,1)} %get-tuple-element.126) | copy-start | bytes 3342340
  90.1 4.0 %copy-start.3 = (bf16[2,2,2,288,128]{4,3,2,1,0:T(8,128)(2,1)}, bf16[2,2,2,288,128]{4,3,2,1,0:T(8,128)(2,1)S(1)}, u32[]{:S(2)}) copy-start(bf16[2,2,2,288,128]{4,3,2,1,0:T(8,128)(2,1)S(1)} %collective-permute-done.3) | copy-start | bytes 1769476
  90.1 6.1 %copy-start.5 = (bf16[2,2,2,288,128]{4,3,2,1,0:T(8,128)(2,1)}, bf16[2,2,2,288,128]{4,3,2,1,0:T(8,128)(2,1)S(1)}, u32[]{:S(2)}) copy-start(bf16[2,2,2,288,128]{4,3,2,1,0:T(8,128)(2,1)S(1)} %collective-permute-done.4) | copy-start | bytes 1769476
  96.2 3.1 %collective-permute-start.7 = (bf16[4,4,2,136,128]{4,3,2,1,0:T(8,128)(2,1)}, bf16[4,4,2,136,128]{4,3,2,1,0:T(8,128)(2,1)}, u32[]{:S(2)}, u32[]{:S(2)}) collective-permute-start(bf16[4,4,2,136,128]{4,3,2,1,0:T(8,128)(2,1)} %get-tuple-element.127), channel_id=1, source_target_pairs={{0,2},{1,3},{2,0},{3,1},{4,6},{5,7},{6,4},{7,5},{8,10},{9,11},{10,... | collective-permute-start | bytes 3342344 | tf_op jit(solution)/shard_map/ppermute | solution.py:681
  96.2 9.7 %collective-permute-start.6 = (bf16[2,2,288,128]{3,2,1,0:T(8,128)(2,1)}, bf16[2,2,288,128]{3,2,1,0:T(8,128)(2,1)}, u32[]{:S(2)}, u32[]{:S(2)}) collective-permute-start(bf16[2,2,288,128]{3,2,1,0:T(8,128)(2,1)} %fusion.3), channel_id=1, source_target_pairs={{0,8},{1,9},{2,10},{3,11},{4,12},{5,13},{6,14},{7,15},{8,0},{9,1},... | collective-permute-start | bytes 884744 | tf_op jit(solution)/shard_map/ppermute | solution.py:681
  98.0 7.9 %copy-start.4 = (bf16[2,2,2,288,128]{4,3,2,1,0:T(8,128)(2,1)S(1)}, bf16[2,2,2,288,128]{4,3,2,1,0:T(8,128)(2,1)}, u32[]{:S(2)}) copy-start(bf16[2,2,2,288,128]{4,3,2,1,0:T(8,128)(2,1)} %copy-done.3) | copy-start | bytes 1769476
  98.0 7.9 %copy-start.6 = (bf16[2,2,2,288,128]{4,3,2,1,0:T(8,128)(2,1)S(1)}, bf16[2,2,2,288,128]{4,3,2,1,0:T(8,128)(2,1)}, u32[]{:S(2)}) copy-start(bf16[2,2,2,288,128]{4,3,2,1,0:T(8,128)(2,1)} %copy-done.5) | copy-start | bytes 1769476
  98.0 7.9 %copy-start.8 = (bf16[2,2,2,288,128]{4,3,2,1,0:T(8,128)(2,1)S(1)}, bf16[2,2,2,288,128]{4,3,2,1,0:T(8,128)(2,1)}, u32[]{:S(2)}) copy-start(bf16[2,2,2,288,128]{4,3,2,1,0:T(8,128)(2,1)} %copy-done.7) | copy-start | bytes 1769476
  100.6 16.0 %collective-permute-start.10 = (bf16[2,2,2,136,128]{4,3,2,1,0:T(8,128)(2,1)S(1)}, bf16[2,2,2,136,128]{4,3,2,1,0:T(8,128)(2,1)S(1)}, u32[]{:S(2)}, u32[]{:S(2)}) collective-permute-start(bf16[2,2,2,136,128]{4,3,2,1,0:T(8,128)(2,1)S(1)} %get-tuple-element.170), channel_id=1, source_target_pairs={{0,4},{1,5},{2,6},{3,7},{4,0},{5,1},{6,2},{7,3},{8,12},{9,13},{10,... | collective-permute-start | bytes 835592 | tf_op jit(solution)/shard_map/ppermute | solution.py:681
  102.3 14.4 %collective-permute-start.11 = (bf16[2,2,2,136,128]{4,3,2,1,0:T(8,128)(2,1)S(1)}, bf16[2,2,2,136,128]{4,3,2,1,0:T(8,128)(2,1)S(1)}, u32[]{:S(2)}, u32[]{:S(2)}) collective-permute-start(bf16[2,2,2,136,128]{4,3,2,1,0:T(8,128)(2,1)S(1)} %get-tuple-element.169), channel_id=1, source_target_pairs={{0,5},{1,4},{2,7},{3,6},{4,1},{5,0},{6,3},{7,2},{8,13},{9,12},{10,... | collective-permute-start | bytes 835592 | tf_op jit(solution)/shard_map/ppermute | solution.py:681
  103.8 14.1 %collective-permute-start.9 = (bf16[2,2,2,136,128]{4,3,2,1,0:T(8,128)(2,1)S(1)}, bf16[2,2,2,136,128]{4,3,2,1,0:T(8,128)(2,1)S(1)}, u32[]{:S(2)}, u32[]{:S(2)}) collective-permute-start(bf16[2,2,2,136,128]{4,3,2,1,0:T(8,128)(2,1)S(1)} %get-tuple-element.171), channel_id=1, source_target_pairs={{0,1},{1,0},{2,3},{3,2},{4,5},{5,4},{6,7},{7,6},{8,9},{9,8},{10,11... | collective-permute-start | bytes 835592 | tf_op jit(solution)/shard_map/ppermute | solution.py:681
  107.0 12.0 %collective-permute-start.8 = (bf16[2,288,128]{2,1,0:T(8,128)(2,1)S(1)}, bf16[2,288,128]{2,1,0:T(8,128)(2,1)S(1)}, u32[]{:S(2)}, u32[]{:S(2)}) collective-permute-start(bf16[2,288,128]{2,1,0:T(8,128)(2,1)S(1)} %fusion.9), channel_id=1, source_target_pairs={{0,16},{1,17},{2,18},{3,19},{4,20},{5,21},{6,22},{7,23},{8,24},{9,... | collective-permute-start | bytes 442376 | tf_op jit(solution)/shard_map/ppermute | solution.py:681
  120.2 10.8 %collective-permute-start.13 = (bf16[2,288,128]{2,1,0:T(8,128)(2,1)S(1)}, bf16[2,288,128]{2,1,0:T(8,128)(2,1)S(1)}, u32[]{:S(2)}, u32[]{:S(2)}) collective-permute-start(bf16[2,288,128]{2,1,0:T(8,128)(2,1)S(1)} %fusion.8), channel_id=1, source_target_pairs={{0,16},{1,17},{2,18},{3,19},{4,20},{5,21},{6,22},{7,23},{8,24},{9,... | collective-permute-start | bytes 442376 | tf_op jit(solution)/shard_map/ppermute | solution.py:681
  131.0 9.6 %collective-permute-start.14 = (bf16[2,2,288,128]{3,2,1,0:T(8,128)(2,1)S(1)}, bf16[2,2,288,128]{3,2,1,0:T(8,128)(2,1)S(1)}, u32[]{:S(2)}, u32[]{:S(2)}) collective-permute-start(bf16[2,2,288,128]{3,2,1,0:T(8,128)(2,1)S(1)} %get-tuple-element.175), channel_id=1, source_target_pairs={{0,8},{1,9},{2,10},{3,11},{4,12},{5,13},{6,14},{7,15},{8,0},{9,1},... | collective-permute-start | bytes 884744 | tf_op jit(solution)/shard_map/ppermute | solution.py:681
  132.7 11.6 %collective-permute-start.12 = (bf16[2,2,2,136,128]{4,3,2,1,0:T(8,128)(2,1)S(1)}, bf16[2,2,2,136,128]{4,3,2,1,0:T(8,128)(2,1)S(1)}, u32[]{:S(2)}, u32[]{:S(2)}) collective-permute-start(bf16[2,2,2,136,128]{4,3,2,1,0:T(8,128)(2,1)S(1)} %fusion.6), channel_id=1, source_target_pairs={{0,8},{1,9},{2,10},{3,11},{4,12},{5,13},{6,14},{7,15},{8,0},{9,1},... | collective-permute-start | bytes 835592 | tf_op jit(solution)/shard_map/ppermute | solution.py:681
  140.7 16.3 %collective-permute-start.19 = (bf16[2,2,2,288,128]{4,3,2,1,0:T(8,128)(2,1)S(1)}, bf16[2,2,2,288,128]{4,3,2,1,0:T(8,128)(2,1)S(1)}, u32[]{:S(2)}, u32[]{:S(2)}) collective-permute-start(bf16[2,2,2,288,128]{4,3,2,1,0:T(8,128)(2,1)S(1)} %get-tuple-element.173), channel_id=1, source_target_pairs={{0,1},{1,0},{2,3},{3,2},{4,5},{5,4},{6,7},{7,6},{8,9},{9,8},{10,11... | collective-permute-start | bytes 1769480 | tf_op jit(solution)/shard_map/ppermute | solution.py:681
  141.7 15.5 %collective-permute-start.20 = (bf16[2,2,2,288,128]{4,3,2,1,0:T(8,128)(2,1)S(1)}, bf16[2,2,2,288,128]{4,3,2,1,0:T(8,128)(2,1)S(1)}, u32[]{:S(2)}, u32[]{:S(2)}) collective-permute-start(bf16[2,2,2,288,128]{4,3,2,1,0:T(8,128)(2,1)S(1)} %get-tuple-element.173), channel_id=1, source_target_pairs={{0,4},{1,5},{2,6},{3,7},{4,0},{5,1},{6,2},{7,3},{8,12},{9,13},{10,... | collective-permute-start | bytes 1769480 | tf_op jit(solution)/shard_map/ppermute | solution.py:681
  143.2 20.3 %collective-permute-start.21 = (bf16[2,2,2,288,128]{4,3,2,1,0:T(8,128)(2,1)S(1)}, bf16[2,2,2,288,128]{4,3,2,1,0:T(8,128)(2,1)S(1)}, u32[]{:S(2)}, u32[]{:S(2)}) collective-permute-start(bf16[2,2,2,288,128]{4,3,2,1,0:T(8,128)(2,1)S(1)} %get-tuple-element.173), channel_id=1, source_target_pairs={{0,5},{1,4},{2,7},{3,6},{4,1},{5,0},{6,3},{7,2},{8,13},{9,12},{10,... | collective-permute-start | bytes 1769480 | tf_op jit(solution)/shard_map/ppermute | solution.py:681
  144.3 11.5 %collective-permute-start.15 = (bf16[2,2,2,136,128]{4,3,2,1,0:T(8,128)(2,1)S(1)}, bf16[2,2,2,136,128]{4,3,2,1,0:T(8,128)(2,1)S(1)}, u32[]{:S(2)}, u32[]{:S(2)}) collective-permute-start(bf16[2,2,2,136,128]{4,3,2,1,0:T(8,128)(2,1)S(1)} %add_convert_fusion.4), channel_id=1, source_target_pairs={{0,16},{1,17},{2,18},{3,19},{4,20},{5,21},{6,22},{7,23},{8,24},{9,... | collective-permute-start | bytes 835592 | tf_op jit(solution)/shard_map/ppermute | solution.py:681
  163.5 4.9 %copy-start = (s32[5]{0:T(128)S(1)}, s32[5]{0:T(128)}, u32[]{:S(2)}) copy-start(s32[5]{0:T(128)} %stack.71.ids.refs_1_.refs_0_) | copy-start | bytes 64
  163.8 4.6 %collective-permute-start.22 = (bf16[4,2,2,2,288,128]{5,4,3,2,1,0:T(8,128)(2,1)S(1)}, bf16[4,2,2,2,288,128]{5,4,3,2,1,0:T(8,128)(2,1)S(1)}, u32[]{:S(2)}, u32[]{:S(2)}) collective-permute-start(bf16[4,2,2,2,288,128]{5,4,3,2,1,0:T(8,128)(2,1)S(1)} %pad_maximum_fusion.refs_1_), channel_id=1, source_target_pairs={{0,2},{1,3},{2,0},{3,1},{4,6},{5,7},{6,4},{7,5},{8,10},{9,11},{10,... | collective-permute-start | bytes 7077896 | tf_op jit(solution)/shard_map/ppermute | solution.py:681
  163.9 10.6 %collective-permute-start.16 = (bf16[2,2,2,136,128]{4,3,2,1,0:T(8,128)(2,1)S(1)}, bf16[2,2,2,136,128]{4,3,2,1,0:T(8,128)(2,1)S(1)}, u32[]{:S(2)}, u32[]{:S(2)}) collective-permute-start(bf16[2,2,2,136,128]{4,3,2,1,0:T(8,128)(2,1)S(1)} %add_convert_fusion.3), channel_id=1, source_target_pairs={{0,1},{1,0},{2,3},{3,2},{4,5},{5,4},{6,7},{7,6},{8,9},{9,8},{10,11... | collective-permute-start | bytes 835592 | tf_op jit(solution)/shard_map/ppermute | solution.py:681
  165.5 9.5 %collective-permute-start.17 = (bf16[2,2,2,136,128]{4,3,2,1,0:T(8,128)(2,1)S(1)}, bf16[2,2,2,136,128]{4,3,2,1,0:T(8,128)(2,1)S(1)}, u32[]{:S(2)}, u32[]{:S(2)}) collective-permute-start(bf16[2,2,2,136,128]{4,3,2,1,0:T(8,128)(2,1)S(1)} %add_convert_fusion.3), channel_id=1, source_target_pairs={{0,4},{1,5},{2,6},{3,7},{4,0},{5,1},{6,2},{7,3},{8,12},{9,13},{10,... | collective-permute-start | bytes 835592 | tf_op jit(solution)/shard_map/ppermute | solution.py:681
  166.9 13.2 %collective-permute-start.18 = (bf16[2,2,2,136,128]{4,3,2,1,0:T(8,128)(2,1)S(1)}, bf16[2,2,2,136,128]{4,3,2,1,0:T(8,128)(2,1)S(1)}, u32[]{:S(2)}, u32[]{:S(2)}) collective-permute-start(bf16[2,2,2,136,128]{4,3,2,1,0:T(8,128)(2,1)S(1)} %add_convert_fusion.3), channel_id=1, source_target_pairs={{0,5},{1,4},{2,7},{3,6},{4,1},{5,0},{6,3},{7,2},{8,13},{9,12},{10,... | collective-permute-start | bytes 835592 | tf_op jit(solution)/shard_map/ppermute | solution.py:681
  180.3 2.8 %collective-permute-start.23 = (bf16[4,2,2,2,136,128]{5,4,3,2,1,0:T(8,128)(2,1)S(1)}, bf16[4,2,2,2,136,128]{5,4,3,2,1,0:T(8,128)(2,1)S(1)}, u32[]{:S(2)}, u32[]{:S(2)}) collective-permute-start(bf16[4,2,2,2,136,128]{5,4,3,2,1,0:T(8,128)(2,1)S(1)} %pad_maximum_fusion.1.refs_1_), channel_id=1, source_target_pairs={{0,2},{1,3},{2,0},{3,1},{4,6},{5,7},{6,4},{7,5},{8,10},{9,11},{10,... | collective-permute-start | bytes 3342344 | tf_op jit(solution)/shard_map/ppermute | solution.py:681
  (3 other events, 4.8 us)
